TPU v7x, 32 devices: a whole 2x2x4 slice. The times are simulated.
32 devices in a mesh: tm: 8 (over y, x, core), space: 4 (over z).
Axes of the slice: x: 2, y: 2, z: 4, core: 2. Of those that a mesh axis runs over, the one named last changes fastest.
Arguments:
- adjoint_iterate: float32 [64, 16, 32, 128], P('tm', None, 'space'), may hold values from -6 to 6
- innovations: float32 [64, 16, 512], P('tm', None, 'space'), may hold values from -6 to 6
- station_cells: int32 [64, 512], P('tm', 'space'), may hold values from 0 to 1023
- diffusivity: float32 [16, 32, 128], P(None, 'space'), may hold values from 0.01 to 0.08
- wind_x: float32 [16, 32, 128], P(None, 'space'), may hold values from -0.2 to 0.2
- wind_y: float32 [16, 32, 128], P(None, 'space'), may hold values from -0.2 to 0.2
- vertical_mixing: float32 [16, 32, 128], P(None, 'space'), may hold values from 0.01 to 0.1
Outputs:
- updated_iterate: float32 [64, 16, 32, 128], P('tm', None, 'space')
Inputs may be any that keep to these rules, and one draw needn't show every extreme that they name: `station_cells`: A station's column within its tile of 8 x 128 columns is numbered x * 128 + y; several stations may share a column.
All inputs are finite; a program needn't handle non-finite values.
Results may differ from a plain program's by a relative error of at most 0.0003.
Values sent between devices are 32-bit elements; how exact they have to be, the bound alone decides.
No kernel may reach another device: no remote copies, remote signals or barrier semaphores. Data moves between devices by JAX's collectives and lax.ppermute only.
A program may use at most 64 MiB of HBM per device.

v0:
```python
import math

import jax
import jax.numpy as jnp
from jax import lax
from jax.sharding import PartitionSpec as P

LEV = 16
TX = 8
NY = 128
STEPS_DEV = 8
INNER = 4


circ_alpha = 0.1


def from_behind(value, axis, steps):
    count = lax.axis_size(axis)
    leading, last = (max(0, -steps), min(count, count - steps))
    return lax.ppermute(value, axis, [(source, source + steps) for source in range(leading, last)])


def with_halo(cells, sides, width):
    for axis, dim in sides:
        count = lax.axis_size(axis)
        ends = count - 1
        head = lax.slice_in_dim(cells, 0, width, axis=dim)
        tail = lax.slice_in_dim(cells, cells.shape[dim] - width, cells.shape[dim], axis=dim)
        cells = jnp.concatenate(
            [
                lax.ppermute(tail, axis, [(i, (i + 1) % count) for i in range(ends)]),
                cells,
                lax.ppermute(head, axis, [((i + 1) % count, i) for i in range(ends)]),
            ],
            axis=dim,
        )
    return cells


def transfer_rates(diffusivity, wind_x, wind_y, vertical_mixing):
    east_rate = diffusivity + jnp.maximum(-wind_x, 0.0)
    west_rate = diffusivity + jnp.maximum(wind_x, 0.0)
    north_rate = diffusivity + jnp.maximum(-wind_y, 0.0)
    south_rate = diffusivity + jnp.maximum(wind_y, 0.0)
    return jnp.stack(
        [east_rate, west_rate, north_rate, south_rate, vertical_mixing, vertical_mixing]
    )


def apply_transpose(padded, rates_pad, retained):
    center = padded[..., 1:-1, 1:-1, 1:-1]
    summed = retained * center
    summed = summed + rates_pad[0, 1:-1, :-2, 1:-1] * padded[..., 1:-1, :-2, 1:-1]
    summed = summed + rates_pad[1, 1:-1, 2:, 1:-1] * padded[..., 1:-1, 2:, 1:-1]
    summed = summed + rates_pad[2, 1:-1, 1:-1, :-2] * padded[..., 1:-1, 1:-1, :-2]
    summed = summed + rates_pad[3, 1:-1, 1:-1, 2:] * padded[..., 1:-1, 1:-1, 2:]
    summed = summed + rates_pad[4, :-2, 1:-1, 1:-1] * padded[..., :-2, 1:-1, 1:-1]
    summed = summed + rates_pad[5, 2:, 1:-1, 1:-1] * padded[..., 2:, 1:-1, 1:-1]
    return summed


def fourier_tables(horizon):
    freq_rows = jnp.arange(horizon, dtype=jnp.int32)
    phase_int = freq_rows[:, None] * freq_rows[None, :] % horizon
    angles = phase_int.astype(jnp.float32) * (2.0 * math.pi / horizon)
    return (jnp.cos(angles), jnp.sin(angles))


def rotation(horizon, freq_count):
    freq_rows = jnp.arange(freq_count, dtype=jnp.int32)
    angles = freq_rows.astype(jnp.float32) * (2.0 * math.pi / horizon)
    return (jnp.cos(angles)[:, None, None, None], jnp.sin(angles)[:, None, None, None])


def rotate_step(source, applied, cos_freq, sin_freq, beta_step):
    real_part = source[0] + beta_step * (cos_freq * applied[0] - sin_freq * applied[1])
    imag_part = source[1] + beta_step * (sin_freq * applied[0] + cos_freq * applied[1])
    return jnp.stack([real_part, imag_part])


def matmul_exact(table, rows):
    return jnp.dot(table, rows, precision=lax.Precision.HIGHEST)


def body(adjoint_iterate, innovations, station_cells, diffusivity, wind_x, wind_y, vertical_mixing):
    time_parts = lax.axis_size("tm")
    horizon = STEPS_DEV * time_parts
    levels_local = LEV // time_parts
    time_rank = lax.axis_index("tm")
    rate_fields = transfer_rates(diffusivity, wind_x, wind_y, vertical_mixing)
    retained = 1.0 - jnp.sum(rate_fields, axis=0)

    def scatter_step(cell_ids, values):
        return jnp.zeros((LEV, TX * NY), jnp.float32).at[:, cell_ids].add(values)

    forcing = jax.vmap(scatter_step)(station_cells, innovations).reshape(STEPS_DEV, LEV, TX, NY)
    leading = from_behind(adjoint_iterate[:1], "tm", -1)
    following = jnp.concatenate([adjoint_iterate[1:], leading], axis=0)
    extended = with_halo(jnp.concatenate([rate_fields, following], axis=0), (("space", 2),), 1)
    extended = jnp.pad(extended, ((0, 0), (1, 1), (0, 0), (1, 1)))
    rates_pad = extended[:6]
    residual = forcing - adjoint_iterate + apply_transpose(extended[6:], rates_pad, retained)
    log_beta = math.log(circ_alpha) / horizon
    beta_step = math.exp(log_beta)
    step_global = (time_rank * STEPS_DEV + jnp.arange(STEPS_DEV, dtype=jnp.int32)).astype(
        jnp.float32
    )
    scaled = residual * jnp.exp(-step_global * log_beta)[:, None, None, None]
    gathered = lax.all_to_all(scaled, "tm", split_axis=1, concat_axis=0, tiled=True)
    flat_rows = gathered.reshape(horizon, -1)
    cos_table, sin_table = fourier_tables(horizon)
    real_src = matmul_exact(cos_table, flat_rows)
    imag_src = -matmul_exact(sin_table, flat_rows)
    source = jnp.stack([real_src, imag_src]).reshape(2, horizon, levels_local, TX, NY)
    cos_freq, sin_freq = rotation(horizon, horizon)
    level_start = time_rank * levels_local
    local_rates = lax.dynamic_slice_in_dim(rates_pad, level_start, levels_local + 2, 1)
    local_retained = lax.dynamic_slice_in_dim(retained, level_start, levels_local, 0)
    iterate = source
    for sweep_index in range(INNER):
        padded = with_halo(iterate, (("tm", 2), ("space", 3)), 1)
        padded = jnp.pad(padded, ((0, 0), (0, 0), (0, 0), (0, 0), (1, 1)))
        applied = apply_transpose(padded, local_rates, local_retained)
        iterate = rotate_step(source, applied, cos_freq, sin_freq, beta_step)
    real_rows = iterate[0].reshape(horizon, -1)
    imag_rows = iterate[1].reshape(horizon, -1)
    restored = (matmul_exact(cos_table, real_rows) - matmul_exact(sin_table, imag_rows)) / horizon
    restored = restored.reshape(horizon, levels_local, TX, NY)
    returned = lax.all_to_all(restored, "tm", split_axis=0, concat_axis=1, tiled=True)
    correction = returned * jnp.exp(step_global * log_beta)[:, None, None, None]
    return adjoint_iterate + correction


def solution(mesh):
    in_specs = (
        P("tm", None, "space", None),
        P("tm", None, "space"),
        P("tm", "space"),
        P(None, "space", None),
        P(None, "space", None),
        P(None, "space", None),
        P(None, "space", None),
    )
    out_specs = P("tm", None, "space", None)
    return jax.shard_map(body, mesh=mesh, in_specs=in_specs, out_specs=out_specs, check_vma=False)
```

profile of v0, /device:TPU:0, one launch (start us, length us, event | category | flops | bytes accessed | tf_op | source)
XLA Modules:
  0.0 212.5 jit_solution(13806551617667307890)
XLA Ops:
  11.1 5.0 %collective-permute-start.1 = (f32[14,16,1,128]{3,1,2,0:T(8,128)S(1)}, f32[14,16,1,128]{3,1,2,0:T(8,128)S(1)}, u32[]{:S(2)}, u32[]{:S(2)}) collective-permute-start(f32[14,16,1,128]{3,1,2,0:T(8,128)S(1)} %get-tuple-element.41), channel_id=1, source_target_pairs={{0,1},{1,2},{2,3},{4,5},{5,6},{6,7},{8,9},{9,10},{10,11},{12,13},{... | collective-permute-start | bytes 344072 | tf_op jit(solution)/shard_map/ppermute | solution.py:32
  18.5 8.2 %scatter_custom_fusion = f32[8192,16]{1,0:T(8,128)} fusion(s32[1024]{0:T(1024)S(1)} %select_bitcast_fusion, f32[1024,16]{1,0:T(8,128)S(1)} %bitcast.87, f32[]{:T(128)} %constant.20.clone.1), kind=kCustom, calls=%fused_computation.35 | custom fusion | flops 16384 | bytes 524292
  26.7 2.9 %copy.48 = f32[8,1024,16]{1,0,2:T(8,128)S(1)} copy(f32[8,1024,16]{2,1,0:T(8,128)} %bitcast.71) | data formatting | bytes 1048576
  33.8 14.0 %all_to_all.33 = f32[8,16,8,128]{3,2,0,1:T(8,128)S(1)} all-to-all(f32[8,16,8,128]{3,2,0,1:T(8,128)S(1)} %copy.37), channel_id=1, replica_groups=mesh['tm'=8,'space'=4] {'tm'}, dimensions={1} | all-to-all | bytes 1048576 | tf_op jit(solution)/shard_map/all_to_all | solution.py:110
  52.0 2.1 collective-permute-start.3
  55.4 2.8 %collective-permute-done.4 = f32[2,64,1,8,128]{4,3,2,1,0:T(8,128)} collective-permute-done((f32[2,64,1,8,128]{4,3,2,1,0:T(8,128)}, f32[2,64,1,8,128]{4,3,2,1,0:T(8,128)}, u32[]{:S(2)}, u32[]{:S(2)}) %collective-permute-start.4) | collective-permute-done | bytes 524320 | tf_op jit(solution)/shard_map/ppermute | solution.py:34
  58.3 2.6 %pad_maximum_fusion.63 = (f32[2,64,4,1,128]{4,3,2,1,0:T(1,128)}, f32[2,64,4,1,128]{4,3,2,1,0:T(1,128)}) fusion(f32[2,64,1,8,128]{4,3,2,1,0:T(8,128)} %collective-permute-done.4, f32[2,64,2,8,128]{4,3,2,1,0:T(8,128)S(1)} %constant_dynamic-update-slice_fusion.2, f32[2,64,1,8,128]{4,3,2,1,0:T(8,128)} %collective-permute-done.3), kind=kLoop, calls=%fused_computation.205 | loop fusion | flops 262144 | bytes 2621440 | tf_op jit(solution)/shard_map/slice | solution.py:29
  60.9 4.5 %collective-permute-start.5 = (f32[2,64,4,1,128]{4,3,2,1,0:T(1,128)}, f32[2,64,4,1,128]{4,3,2,1,0:T(1,128)S(1)}, u32[]{:S(2)}, u32[]{:S(2)}) collective-permute-start(f32[2,64,4,1,128]{4,3,2,1,0:T(1,128)} %get-tuple-element.15), channel_id=1, source_target_pairs={{0,1},{1,2},{2,3},{4,5},{5,6},{6,7},{8,9},{9,10},{10,11},{12,13},{... | collective-permute-start | bytes 786440 | tf_op jit(solution)/shard_map/ppermute | solution.py:32
  67.1 2.6 %collective-permute-done.5 = f32[2,64,4,1,128]{4,3,2,1,0:T(1,128)S(1)} collective-permute-done((f32[2,64,4,1,128]{4,3,2,1,0:T(1,128)}, f32[2,64,4,1,128]{4,3,2,1,0:T(1,128)S(1)}, u32[]{:S(2)}, u32[]{:S(2)}) %collective-permute-start.5) | collective-permute-done | bytes 262176 | tf_op jit(solution)/shard_map/ppermute | solution.py:32
  69.6 4.4 %collective-permute-done.6 = f32[2,64,4,1,128]{4,3,2,1,0:T(1,128)} collective-permute-done((f32[2,64,4,1,128]{4,3,2,1,0:T(1,128)}, f32[2,64,4,1,128]{4,3,2,1,0:T(1,128)}, u32[]{:S(2)}, u32[]{:S(2)}) %collective-permute-start.6) | collective-permute-done | bytes 262176 | tf_op jit(solution)/shard_map/ppermute | solution.py:34
  74.0 7.3 %select_maximum_fusion.15 = f32[2,64,4,10,130]{4,3,2,1,0:T(8,128)S(1)} fusion(f32[2,64,4,1,128]{4,3,2,1,0:T(1,128)} %collective-permute-done.6, f32[2,64,4,1,128]{4,3,2,1,0:T(1,128)S(1)} %collective-permute-done.5, f32[2,64,1,8,128]{4,3,2,1,0:T(8,128)} %collective-permute-done.4, f32[2,64,2,8,128]{4,3,2,1,0:T(8,128)S(1)} %constant_dynamic-update-slice_fusion.2, ...), kind=kLoop, calls=%fused_computation.18 | loop fusion | flops 7987200 | bytes 5283840 | tf_op jit(solution)/shard_map/concatenate | solution.py:30
  81.4 2.3 %fusion.42 = f32[2,64,2,8,128]{4,3,2,1,0:T(8,128)S(1)} fusion(f32[2,64,1,8,128]{4,3,2,1,0:T(8,128)} %collective-permute-done.4, f32[2,64,2,8,128]{4,3,2,1,0:T(8,128)S(1)} %constant_dynamic-update-slice_fusion.2, f32[2,64,1,8,128]{4,3,2,1,0:T(8,128)} %collective-permute-done.3, f32[2,64,4,10,130]{4,3,2,1,0:T(8,128)S(1)} %select_maximum_fusion.15, ...), kind=kLoop, calls=%fused_computation.130 | loop fusion | flops 5505024 | bytes 5824512 | tf_op jit(solution)/shard_map/add | solution.py:59
  84.0 10.7 %collective-permute-start.7 = (f32[2,64,1,8,128]{4,3,2,1,0:T(8,128)S(1)}, f32[2,64,1,8,128]{4,3,2,1,0:T(8,128)S(1)}, u32[]{:S(2)}, u32[]{:S(2)}) collective-permute-start(f32[2,64,1,8,128]{4,3,2,1,0:T(8,128)S(1)} %get-tuple-element.35), channel_id=1, source_target_pairs={{0,4},{4,8},{8,12},{12,16},{16,20},{20,24},{24,28},{1,5},{5,9},{9,... | collective-permute-start | bytes 1572872 | tf_op jit(solution)/shard_map/ppermute | solution.py:32
  96.2 5.3 %collective-permute-done.8 = f32[2,64,1,8,128]{4,3,2,1,0:T(8,128)S(1)} collective-permute-done((f32[2,64,1,8,128]{4,3,2,1,0:T(8,128)S(1)}, f32[2,64,1,8,128]{4,3,2,1,0:T(8,128)S(1)}, u32[]{:S(2)}, u32[]{:S(2)}) %collective-permute-start.8) | collective-permute-done | bytes 524320 | tf_op jit(solution)/shard_map/ppermute | solution.py:34
  101.8 3.5 %collective-permute-start.9 = (f32[2,64,4,1,128]{4,3,2,1,0:T(1,128)S(1)}, f32[2,64,4,1,128]{4,3,2,1,0:T(1,128)S(1)}, u32[]{:S(2)}, u32[]{:S(2)}) collective-permute-start(f32[2,64,4,1,128]{4,3,2,1,0:T(1,128)S(1)} %get-tuple-element.13), channel_id=1, source_target_pairs={{0,1},{1,2},{2,3},{4,5},{5,6},{6,7},{8,9},{9,10},{10,11},{12,13},{... | collective-permute-start | bytes 786440 | tf_op jit(solution)/shard_map/ppermute | solution.py:32
  106.6 2.6 %collective-permute-done.9 = f32[2,64,4,1,128]{4,3,2,1,0:T(1,128)S(1)} collective-permute-done((f32[2,64,4,1,128]{4,3,2,1,0:T(1,128)S(1)}, f32[2,64,4,1,128]{4,3,2,1,0:T(1,128)S(1)}, u32[]{:S(2)}, u32[]{:S(2)}) %collective-permute-start.9) | collective-permute-done | bytes 262176 | tf_op jit(solution)/shard_map/ppermute | solution.py:32
  109.1 4.4 %collective-permute-done.10 = f32[2,64,4,1,128]{4,3,2,1,0:T(1,128)S(1)} collective-permute-done((f32[2,64,4,1,128]{4,3,2,1,0:T(1,128)S(1)}, f32[2,64,4,1,128]{4,3,2,1,0:T(1,128)S(1)}, u32[]{:S(2)}, u32[]{:S(2)}) %collective-permute-start.10) | collective-permute-done | bytes 262176 | tf_op jit(solution)/shard_map/ppermute | solution.py:34
  113.5 6.7 %select_maximum_fusion.10 = f32[2,64,4,10,130]{4,3,2,1,0:T(8,128)S(1)} fusion(f32[2,64,4,1,128]{4,3,2,1,0:T(1,128)S(1)} %collective-permute-done.10, f32[2,64,4,1,128]{4,3,2,1,0:T(1,128)S(1)} %collective-permute-done.9, f32[2,64,1,8,128]{4,3,2,1,0:T(8,128)S(1)} %collective-permute-done.8, f32[2,64,1,8,128]{4,3,2,1,0:T(8,128)S(1)} %collective-permute-done.7, ...), kind=kLoop, calls=%fused_computation.13 | loop fusion | flops 9318400 | bytes 5283840 | tf_op jit(solution)/shard_map/concatenate | solution.py:30
  121.9 9.0 %collective-permute-start.11 = (f32[2,64,1,8,128]{4,3,2,1,0:T(8,128)S(1)}, f32[2,64,1,8,128]{4,3,2,1,0:T(8,128)S(1)}, u32[]{:S(2)}, u32[]{:S(2)}) collective-permute-start(f32[2,64,1,8,128]{4,3,2,1,0:T(8,128)S(1)} %get-tuple-element.33), channel_id=1, source_target_pairs={{0,4},{4,8},{8,12},{12,16},{16,20},{20,24},{24,28},{1,5},{5,9},{9,... | collective-permute-start | bytes 1572872 | tf_op jit(solution)/shard_map/ppermute | solution.py:32
  132.3 4.1 %collective-permute-done.12 = f32[2,64,1,8,128]{4,3,2,1,0:T(8,128)S(1)} collective-permute-done((f32[2,64,1,8,128]{4,3,2,1,0:T(8,128)S(1)}, f32[2,64,1,8,128]{4,3,2,1,0:T(8,128)S(1)}, u32[]{:S(2)}, u32[]{:S(2)}) %collective-permute-start.12) | collective-permute-done | bytes 524320 | tf_op jit(solution)/shard_map/ppermute | solution.py:34
  136.8 3.5 %collective-permute-start.13 = (f32[2,64,4,1,128]{4,3,2,1,0:T(1,128)S(1)}, f32[2,64,4,1,128]{4,3,2,1,0:T(1,128)S(1)}, u32[]{:S(2)}, u32[]{:S(2)}) collective-permute-start(f32[2,64,4,1,128]{4,3,2,1,0:T(1,128)S(1)} %get-tuple-element.11), channel_id=1, source_target_pairs={{0,1},{1,2},{2,3},{4,5},{5,6},{6,7},{8,9},{9,10},{10,11},{12,13},{... | collective-permute-start | bytes 786440 | tf_op jit(solution)/shard_map/ppermute | solution.py:32
  141.6 2.6 %collective-permute-done.13 = f32[2,64,4,1,128]{4,3,2,1,0:T(1,128)S(1)} collective-permute-done((f32[2,64,4,1,128]{4,3,2,1,0:T(1,128)S(1)}, f32[2,64,4,1,128]{4,3,2,1,0:T(1,128)S(1)}, u32[]{:S(2)}, u32[]{:S(2)}) %collective-permute-start.13) | collective-permute-done | bytes 262176 | tf_op jit(solution)/shard_map/ppermute | solution.py:32
  144.1 4.4 %collective-permute-done.14 = f32[2,64,4,1,128]{4,3,2,1,0:T(1,128)S(1)} collective-permute-done((f32[2,64,4,1,128]{4,3,2,1,0:T(1,128)S(1)}, f32[2,64,4,1,128]{4,3,2,1,0:T(1,128)S(1)}, u32[]{:S(2)}, u32[]{:S(2)}) %collective-permute-start.14) | collective-permute-done | bytes 262176 | tf_op jit(solution)/shard_map/ppermute | solution.py:34
  148.5 6.7 %select_maximum_fusion.5 = f32[2,64,4,10,130]{4,3,2,1,0:T(8,128)S(1)} fusion(f32[2,64,4,1,128]{4,3,2,1,0:T(1,128)S(1)} %collective-permute-done.14, f32[2,64,4,1,128]{4,3,2,1,0:T(1,128)S(1)} %collective-permute-done.13, f32[2,64,1,8,128]{4,3,2,1,0:T(8,128)S(1)} %collective-permute-done.12, f32[2,64,1,8,128]{4,3,2,1,0:T(8,128)S(1)} %collective-permute-done.11, ...), kind=kLoop, calls=%fused_computation.8 | loop fusion | flops 9318400 | bytes 5283840 | tf_op jit(solution)/shard_map/concatenate | solution.py:30
  156.9 8.0 %collective-permute-start.15 = (f32[2,64,1,8,128]{4,3,2,1,0:T(8,128)S(1)}, f32[2,64,1,8,128]{4,3,2,1,0:T(8,128)S(1)}, u32[]{:S(2)}, u32[]{:S(2)}) collective-permute-start(f32[2,64,1,8,128]{4,3,2,1,0:T(8,128)S(1)} %get-tuple-element.31), channel_id=1, source_target_pairs={{0,4},{4,8},{8,12},{12,16},{16,20},{20,24},{24,28},{1,5},{5,9},{9,... | collective-permute-start | bytes 1572872 | tf_op jit(solution)/shard_map/ppermute | solution.py:32
  166.4 4.1 %collective-permute-done.16 = f32[2,64,1,8,128]{4,3,2,1,0:T(8,128)S(1)} collective-permute-done((f32[2,64,1,8,128]{4,3,2,1,0:T(8,128)S(1)}, f32[2,64,1,8,128]{4,3,2,1,0:T(8,128)S(1)}, u32[]{:S(2)}, u32[]{:S(2)}) %collective-permute-start.16) | collective-permute-done | bytes 524320 | tf_op jit(solution)/shard_map/ppermute | solution.py:34
  170.7 2.5 %collective-permute-start.17 = (f32[2,64,4,1,128]{4,3,2,1,0:T(1,128)S(1)}, f32[2,64,4,1,128]{4,3,2,1,0:T(1,128)S(1)}, u32[]{:S(2)}, u32[]{:S(2)}) collective-permute-start(f32[2,64,4,1,128]{4,3,2,1,0:T(1,128)S(1)} %get-tuple-element.9), channel_id=1, source_target_pairs={{0,1},{1,2},{2,3},{4,5},{5,6},{6,7},{8,9},{9,10},{10,11},{12,13},{... | collective-permute-start | bytes 786440 | tf_op jit(solution)/shard_map/ppermute | solution.py:32
  174.7 2.4 %collective-permute-done.17 = f32[2,64,4,1,128]{4,3,2,1,0:T(1,128)S(1)} collective-permute-done((f32[2,64,4,1,128]{4,3,2,1,0:T(1,128)S(1)}, f32[2,64,4,1,128]{4,3,2,1,0:T(1,128)S(1)}, u32[]{:S(2)}, u32[]{:S(2)}) %collective-permute-start.17) | collective-permute-done | bytes 262176 | tf_op jit(solution)/shard_map/ppermute | solution.py:32
  177.1 4.6 %collective-permute-done.18 = f32[2,64,4,1,128]{4,3,2,1,0:T(1,128)S(1)} collective-permute-done((f32[2,64,4,1,128]{4,3,2,1,0:T(1,128)S(1)}, f32[2,64,4,1,128]{4,3,2,1,0:T(1,128)S(1)}, u32[]{:S(2)}, u32[]{:S(2)}) %collective-permute-start.18) | collective-permute-done | bytes 262176 | tf_op jit(solution)/shard_map/ppermute | solution.py:34
  181.6 6.7 %select_maximum_fusion = f32[2,64,4,10,130]{4,3,2,1,0:T(8,128)S(1)} fusion(f32[2,64,4,1,128]{4,3,2,1,0:T(1,128)S(1)} %collective-permute-done.18, f32[2,64,4,1,128]{4,3,2,1,0:T(1,128)S(1)} %collective-permute-done.17, f32[2,64,1,8,128]{4,3,2,1,0:T(8,128)S(1)} %collective-permute-done.16, f32[2,64,1,8,128]{4,3,2,1,0:T(8,128)S(1)} %collective-permute-done.15, ...), kind=kLoop, calls=%fused_computation.3 | loop fusion | flops 9318400 | bytes 5283840 | tf_op jit(solution)/shard_map/concatenate | solution.py:30
  192.3 9.5 %all-to-all-start.1 = ((f32[64,2,8,128]{3,2,1,0:T(8,128)}), f32[64,2,8,128]{3,2,1,0:T(8,128)S(1)}, u32[]{:S(2)}, u32[]{:S(2)}) async-start(f32[64,2,8,128]{3,2,1,0:T(8,128)} %bitcast.42), calls=%async_computation.1 | async-start | bytes 1048576 | tf_op jit(solution)/shard_map/all_to_all | solution.py:130
  201.8 9.7 %all-to-all-done.1 = f32[64,2,8,128]{3,2,1,0:T(8,128)S(1)} async-done(((f32[64,2,8,128]{3,2,1,0:T(8,128)}), f32[64,2,8,128]{3,2,1,0:T(8,128)S(1)}, u32[]{:S(2)}, u32[]{:S(2)}) %all-to-all-start.1) | async-done | bytes 524320 | tf_op jit(solution)/shard_map/all_to_all | solution.py:130
  (100 shorter events, 42.4 us)
Async XLA Ops:
  1.2 10.0 %collective-permute-start = (f32[1,16,8,128]{3,1,2,0:T(8,128)S(1)}, f32[1,16,8,128]{3,1,2,0:T(8,128)S(1)}, u32[]{:S(2)}, u32[]{:S(2)}) collective-permute-start(f32[1,16,8,128]{3,1,2,0:T(8,128)S(1)} %slice.399), channel_id=1, source_target_pairs={{4,0},{8,4},{12,8},{16,12},{20,16},{24,20},{28,24},{5,1},{9,5},{13... | collective-permute-start | bytes 196616 | tf_op jit(solution)/shard_map/ppermute | solution.py:21
  9.6 23.3 %copy-start.3 = (f32[8,16,8,128]{3,2,1,0:T(8,128)S(1)}, f32[8,16,8,128]{3,2,1,0:T(8,128)}, u32[]{:S(2)}) copy-start(f32[8,16,8,128]{3,2,1,0:T(8,128)} %param.7) | copy-start | bytes 1572868
  11.1 18.5 %collective-permute-start.1 = (f32[14,16,1,128]{3,1,2,0:T(8,128)S(1)}, f32[14,16,1,128]{3,1,2,0:T(8,128)S(1)}, u32[]{:S(2)}, u32[]{:S(2)}) collective-permute-start(f32[14,16,1,128]{3,1,2,0:T(8,128)S(1)} %get-tuple-element.41), channel_id=1, source_target_pairs={{0,1},{1,2},{2,3},{4,5},{5,6},{6,7},{8,9},{9,10},{10,11},{12,13},{... | collective-permute-start | bytes 344072 | tf_op jit(solution)/shard_map/ppermute | solution.py:32
  16.1 13.5 %collective-permute-start.2 = (f32[14,16,1,128]{3,1,2,0:T(8,128)S(1)}, f32[14,16,1,128]{3,1,2,0:T(8,128)S(1)}, u32[]{:S(2)}, u32[]{:S(2)}) collective-permute-start(f32[14,16,1,128]{3,1,2,0:T(8,128)S(1)} %get-tuple-element.42), channel_id=1, source_target_pairs={{1,0},{2,1},{3,2},{5,4},{6,5},{7,6},{9,8},{10,9},{11,10},{13,12},{... | collective-permute-start | bytes 344072 | tf_op jit(solution)/shard_map/ppermute | solution.py:34
  31.1 1.7 copy-start
  33.7 33.1 %slice-start = ((f32[14,18,10,130]{3,1,2,0:T(8,128)}), f32[6,18,10,130]{3,1,2,0:T(8,128)S(1)}, s32[]{:S(2)}) async-start(f32[14,18,10,130]{3,1,2,0:T(8,128)} %copy-done), calls=%async_computation.2 | async-start | bytes 2949120 | tf_op jit(solution)/shard_map/slice | solution.py:102
  48.6 0.9 copy-start.5
  49.4 0.8 copy-start.7
  50.1 0.8 copy-start.1
  52.0 3.4 %collective-permute-start.3 = (f32[2,64,1,8,128]{4,3,2,1,0:T(8,128)}, f32[2,64,1,8,128]{4,3,2,1,0:T(8,128)}, u32[]{:S(2)}, u32[]{:S(2)}) collective-permute-start(f32[2,64,1,8,128]{4,3,2,1,0:T(8,128)} %get-tuple-element.37), channel_id=1, source_target_pairs={{0,4},{4,8},{8,12},{12,16},{16,20},{20,24},{24,28},{1,5},{5,9},{9,... | collective-permute-start | bytes 1572872 | tf_op jit(solution)/shard_map/ppermute | solution.py:32
  54.1 4.1 %collective-permute-start.4 = (f32[2,64,1,8,128]{4,3,2,1,0:T(8,128)}, f32[2,64,1,8,128]{4,3,2,1,0:T(8,128)}, u32[]{:S(2)}, u32[]{:S(2)}) collective-permute-start(f32[2,64,1,8,128]{4,3,2,1,0:T(8,128)} %get-tuple-element.38), channel_id=1, source_target_pairs={{4,0},{8,4},{12,8},{16,12},{20,16},{24,20},{28,24},{5,1},{9,5},{13... | collective-permute-start | bytes 1572872 | tf_op jit(solution)/shard_map/ppermute | solution.py:34
  60.9 8.7 %collective-permute-start.5 = (f32[2,64,4,1,128]{4,3,2,1,0:T(1,128)}, f32[2,64,4,1,128]{4,3,2,1,0:T(1,128)S(1)}, u32[]{:S(2)}, u32[]{:S(2)}) collective-permute-start(f32[2,64,4,1,128]{4,3,2,1,0:T(1,128)} %get-tuple-element.15), channel_id=1, source_target_pairs={{0,1},{1,2},{2,3},{4,5},{5,6},{6,7},{8,9},{9,10},{10,11},{12,13},{... | collective-permute-start | bytes 786440 | tf_op jit(solution)/shard_map/ppermute | solution.py:32
  65.5 8.6 %collective-permute-start.6 = (f32[2,64,4,1,128]{4,3,2,1,0:T(1,128)}, f32[2,64,4,1,128]{4,3,2,1,0:T(1,128)}, u32[]{:S(2)}, u32[]{:S(2)}) collective-permute-start(f32[2,64,4,1,128]{4,3,2,1,0:T(1,128)} %get-tuple-element.16), channel_id=1, source_target_pairs={{1,0},{2,1},{3,2},{5,4},{6,5},{7,6},{9,8},{10,9},{11,10},{13,12},{... | collective-permute-start | bytes 786440 | tf_op jit(solution)/shard_map/ppermute | solution.py:34
  67.1 16.6 %copy-start.2 = (f32[8,8,16,128]{3,2,1,0:T(8,128)S(1)}, f32[8,8,16,128]{3,2,1,0:T(8,128)}, u32[]{:S(2)}) copy-start(f32[8,8,16,128]{3,2,1,0:T(8,128)} %copy-done.1) | copy-start | bytes 1572868
  84.0 12.2 %collective-permute-start.7 = (f32[2,64,1,8,128]{4,3,2,1,0:T(8,128)S(1)}, f32[2,64,1,8,128]{4,3,2,1,0:T(8,128)S(1)}, u32[]{:S(2)}, u32[]{:S(2)}) collective-permute-start(f32[2,64,1,8,128]{4,3,2,1,0:T(8,128)S(1)} %get-tuple-element.35), channel_id=1, source_target_pairs={{0,4},{4,8},{8,12},{12,16},{16,20},{20,24},{24,28},{1,5},{5,9},{9,... | collective-permute-start | bytes 1572872 | tf_op jit(solution)/shard_map/ppermute | solution.py:32
  94.7 6.8 %collective-permute-start.8 = (f32[2,64,1,8,128]{4,3,2,1,0:T(8,128)S(1)}, f32[2,64,1,8,128]{4,3,2,1,0:T(8,128)S(1)}, u32[]{:S(2)}, u32[]{:S(2)}) collective-permute-start(f32[2,64,1,8,128]{4,3,2,1,0:T(8,128)S(1)} %get-tuple-element.36), channel_id=1, source_target_pairs={{4,0},{8,4},{12,8},{16,12},{20,16},{24,20},{28,24},{5,1},{9,5},{13... | collective-permute-start | bytes 1572872 | tf_op jit(solution)/shard_map/ppermute | solution.py:34
  101.8 7.3 %collective-permute-start.9 = (f32[2,64,4,1,128]{4,3,2,1,0:T(1,128)S(1)}, f32[2,64,4,1,128]{4,3,2,1,0:T(1,128)S(1)}, u32[]{:S(2)}, u32[]{:S(2)}) collective-permute-start(f32[2,64,4,1,128]{4,3,2,1,0:T(1,128)S(1)} %get-tuple-element.13), channel_id=1, source_target_pairs={{0,1},{1,2},{2,3},{4,5},{5,6},{6,7},{8,9},{9,10},{10,11},{12,13},{... | collective-permute-start | bytes 786440 | tf_op jit(solution)/shard_map/ppermute | solution.py:32
  105.3 8.3 %collective-permute-start.10 = (f32[2,64,4,1,128]{4,3,2,1,0:T(1,128)S(1)}, f32[2,64,4,1,128]{4,3,2,1,0:T(1,128)S(1)}, u32[]{:S(2)}, u32[]{:S(2)}) collective-permute-start(f32[2,64,4,1,128]{4,3,2,1,0:T(1,128)S(1)} %get-tuple-element.14), channel_id=1, source_target_pairs={{1,0},{2,1},{3,2},{5,4},{6,5},{7,6},{9,8},{10,9},{11,10},{13,12},{... | collective-permute-start | bytes 786440 | tf_op jit(solution)/shard_map/ppermute | solution.py:34
  121.9 10.5 %collective-permute-start.11 = (f32[2,64,1,8,128]{4,3,2,1,0:T(8,128)S(1)}, f32[2,64,1,8,128]{4,3,2,1,0:T(8,128)S(1)}, u32[]{:S(2)}, u32[]{:S(2)}) collective-permute-start(f32[2,64,1,8,128]{4,3,2,1,0:T(8,128)S(1)} %get-tuple-element.33), channel_id=1, source_target_pairs={{0,4},{4,8},{8,12},{12,16},{16,20},{20,24},{24,28},{1,5},{5,9},{9,... | collective-permute-start | bytes 1572872 | tf_op jit(solution)/shard_map/ppermute | solution.py:32
  130.9 5.6 %collective-permute-start.12 = (f32[2,64,1,8,128]{4,3,2,1,0:T(8,128)S(1)}, f32[2,64,1,8,128]{4,3,2,1,0:T(8,128)S(1)}, u32[]{:S(2)}, u32[]{:S(2)}) collective-permute-start(f32[2,64,1,8,128]{4,3,2,1,0:T(8,128)S(1)} %get-tuple-element.34), channel_id=1, source_target_pairs={{4,0},{8,4},{12,8},{16,12},{20,16},{24,20},{28,24},{5,1},{9,5},{13... | collective-permute-start | bytes 1572872 | tf_op jit(solution)/shard_map/ppermute | solution.py:34
  136.8 7.3 %collective-permute-start.13 = (f32[2,64,4,1,128]{4,3,2,1,0:T(1,128)S(1)}, f32[2,64,4,1,128]{4,3,2,1,0:T(1,128)S(1)}, u32[]{:S(2)}, u32[]{:S(2)}) collective-permute-start(f32[2,64,4,1,128]{4,3,2,1,0:T(1,128)S(1)} %get-tuple-element.11), channel_id=1, source_target_pairs={{0,1},{1,2},{2,3},{4,5},{5,6},{6,7},{8,9},{9,10},{10,11},{12,13},{... | collective-permute-start | bytes 786440 | tf_op jit(solution)/shard_map/ppermute | solution.py:32
  140.3 8.3 %collective-permute-start.14 = (f32[2,64,4,1,128]{4,3,2,1,0:T(1,128)S(1)}, f32[2,64,4,1,128]{4,3,2,1,0:T(1,128)S(1)}, u32[]{:S(2)}, u32[]{:S(2)}) collective-permute-start(f32[2,64,4,1,128]{4,3,2,1,0:T(1,128)S(1)} %get-tuple-element.12), channel_id=1, source_target_pairs={{1,0},{2,1},{3,2},{5,4},{6,5},{7,6},{9,8},{10,9},{11,10},{13,12},{... | collective-permute-start | bytes 786440 | tf_op jit(solution)/shard_map/ppermute | solution.py:34
  156.9 9.5 %collective-permute-start.15 = (f32[2,64,1,8,128]{4,3,2,1,0:T(8,128)S(1)}, f32[2,64,1,8,128]{4,3,2,1,0:T(8,128)S(1)}, u32[]{:S(2)}, u32[]{:S(2)}) collective-permute-start(f32[2,64,1,8,128]{4,3,2,1,0:T(8,128)S(1)} %get-tuple-element.31), channel_id=1, source_target_pairs={{0,4},{4,8},{8,12},{12,16},{16,20},{20,24},{24,28},{1,5},{5,9},{9,... | collective-permute-start | bytes 1572872 | tf_op jit(solution)/shard_map/ppermute | solution.py:32
  164.9 5.5 %collective-permute-start.16 = (f32[2,64,1,8,128]{4,3,2,1,0:T(8,128)S(1)}, f32[2,64,1,8,128]{4,3,2,1,0:T(8,128)S(1)}, u32[]{:S(2)}, u32[]{:S(2)}) collective-permute-start(f32[2,64,1,8,128]{4,3,2,1,0:T(8,128)S(1)} %get-tuple-element.32), channel_id=1, source_target_pairs={{4,0},{8,4},{12,8},{16,12},{20,16},{24,20},{28,24},{5,1},{9,5},{13... | collective-permute-start | bytes 1572872 | tf_op jit(solution)/shard_map/ppermute | solution.py:34
  170.7 6.3 %collective-permute-start.17 = (f32[2,64,4,1,128]{4,3,2,1,0:T(1,128)S(1)}, f32[2,64,4,1,128]{4,3,2,1,0:T(1,128)S(1)}, u32[]{:S(2)}, u32[]{:S(2)}) collective-permute-start(f32[2,64,4,1,128]{4,3,2,1,0:T(1,128)S(1)} %get-tuple-element.9), channel_id=1, source_target_pairs={{0,1},{1,2},{2,3},{4,5},{5,6},{6,7},{8,9},{9,10},{10,11},{12,13},{... | collective-permute-start | bytes 786440 | tf_op jit(solution)/shard_map/ppermute | solution.py:32
  173.2 16.6 %copy-start.8 = (f32[64,2048]{1,0:T(8,128)S(1)}, f32[64,2048]{1,0:T(8,128)}, u32[]{:S(2)}) copy-start(f32[64,2048]{1,0:T(8,128)} %copy-done.7) | copy-start | bytes 1572868
  173.2 8.4 %collective-permute-start.18 = (f32[2,64,4,1,128]{4,3,2,1,0:T(1,128)S(1)}, f32[2,64,4,1,128]{4,3,2,1,0:T(1,128)S(1)}, u32[]{:S(2)}, u32[]{:S(2)}) collective-permute-start(f32[2,64,4,1,128]{4,3,2,1,0:T(1,128)S(1)} %get-tuple-element.10), channel_id=1, source_target_pairs={{1,0},{2,1},{3,2},{5,4},{6,5},{7,6},{9,8},{10,9},{11,10},{13,12},{... | collective-permute-start | bytes 786440 | tf_op jit(solution)/shard_map/ppermute | solution.py:34
  188.3 2.3 %copy-start.6 = (f32[64,2048]{1,0:T(8,128)S(1)}, f32[64,2048]{1,0:T(8,128)}, u32[]{:S(2)}) copy-start(f32[64,2048]{1,0:T(8,128)} %copy-done.5) | copy-start | bytes 1572868
  188.3 23.2 %copy-start.4 = (f32[8,16,8,128]{3,2,1,0:T(8,128)S(1)}, f32[8,16,8,128]{3,2,1,0:T(8,128)}, u32[]{:S(2)}) copy-start(f32[8,16,8,128]{3,2,1,0:T(8,128)} %param.7) | copy-start | bytes 1572868
  192.3 19.2 %all-to-all-start.1 = ((f32[64,2,8,128]{3,2,1,0:T(8,128)}), f32[64,2,8,128]{3,2,1,0:T(8,128)S(1)}, u32[]{:S(2)}, u32[]{:S(2)}) async-start(f32[64,2,8,128]{3,2,1,0:T(8,128)} %bitcast.42), calls=%async_computation.1 | async-start | bytes 1048576 | tf_op jit(solution)/shard_map/all_to_all | solution.py:130
where the time goes:
time: 214 us; the launch traced here: 212 us
  starting transfers between devices  71.4 us (33%)
  other arithmetic  56.4 us (26%)
  waiting for transfers between devices  54.2 us (25%)
  blocking collectives  14 us (7%)
  local copies, waits for them, and re-layouts  12.8 us (6%)
  matrix products  2.97 us (1%)
    ppermute x9, starting transfers between devices, with_halo(): lax.ppermute(tail, axis, [(i, (i + 1) % count) for i in range(ends)])  48.7 us
    ppermute x9, waiting for transfers between devices, with_halo(): lax.ppermute(head, axis, [((i + 1) % count, i) for i in range(ends)])  34.1 us
    concatenate x5, other arithmetic, with_halo(): jnp.concatenate([lax.ppermute(tail, axis, [(i, (i + 1) % count) for i in...  28.8 us
    all_to_all x1, blocking collectives, body(): lax.all_to_all(scaled, 'tm', split_axis=1, concat_axis=0, tiled=True)  14 us
    unnamed x8, other arithmetic  13.4 us
    ppermute x9, starting transfers between devices, with_halo(): lax.ppermute(head, axis, [((i + 1) % count, i) for i in range(ends)])  11.9 us
    unnamed x28, local copies, waits for them, and re-layouts  10.8 us
    ppermute x9, waiting for transfers between devices, with_halo(): lax.ppermute(tail, axis, [(i, (i + 1) % count) for i in range(ends)])  10.5 us
  transfers between devices with their start and end apart: 20, of which 15 were waited for; matrix products, arithmetic and copies ran while one was open for 10% of the time, Pallas kernels for 0%

commit v1 on v0

v1 whole, which is shorter than its diff:
```python
import jax
import jax.numpy as jnp
from jax import lax
from jax.experimental import pallas as pl
from jax.experimental.pallas import tpu as pltpu
from jax.sharding import PartitionSpec as P

LEV = 16
TX = 8
NY = 128
STEPS_DEV = 8
SWEEPS = 5
HALO = SWEEPS - 1
NEXT = SWEEPS
FNEXT = SWEEPS - 1
OWN = STEPS_DEV - NEXT
XW = TX + 2 * HALO
FT = 16

circ_alpha = 0.1

T_LAM = NEXT * LEV * TX
T_INN = T_LAM + FNEXT * LEV
T_ROWS = T_INN + 8

Z1_LAM = OWN * SWEEPS * LEV
Z1_RATE = Z1_LAM + 4 * HALO * LEV
Z1_INN = Z1_RATE + 7 * LEV
Z1_ROWS = Z1_INN + 8

Z2_LAM = NEXT * SWEEPS * LEV
Z2_INN = Z2_LAM + FNEXT * LEV
Z2_ROWS = Z2_INN + 8


def east(diff, wind):
    return diff + jnp.maximum(-wind, 0.0)


def west(diff, wind):
    return diff + jnp.maximum(wind, 0.0)


def column(ref, base, col, half):
    return ref[pl.ds(base + half * 8 * TX + col, 8, stride=TX), :]


def edge_columns(lam_ref, steps, diff_ref, wx_ref, up_ref, down_ref):
    for step in range(steps[0], steps[1]):
        slot = step - steps[0]
        for half in range(2):
            for place in range(SWEEPS):
                row = (slot * SWEEPS + place) * LEV + 8 * half
                col = TX - SWEEPS + place
                up = column(lam_ref, step * LEV * TX, col, half)
                if place == 0:
                    up = up * east(column(diff_ref, 0, col, half), column(wx_ref, 0, col, half))
                up_ref[row : row + 8, :] = up
                down = column(lam_ref, step * LEV * TX, place, half)
                if place == SWEEPS - 1:
                    down = down * west(column(diff_ref, 0, place, half), column(wx_ref, 0, place, half))
                down_ref[row : row + 8, :] = down


def pack_first(lam_ref, inn_ref, cell_ref, diff_ref, wx_ref, wy_ref, vm_ref, t_ref, up_ref, down_ref):
    t_ref[0:T_LAM, :] = lam_ref[0:T_LAM, :]
    t_ref[T_LAM:T_INN, :] = inn_ref[0 : FNEXT * LEV, :]
    cells = cell_ref[...].astype(jnp.float32)
    t_ref[T_INN:T_ROWS, :] = cells
    edge_columns(lam_ref, (NEXT, STEPS_DEV), diff_ref, wx_ref, up_ref, down_ref)
    for index, ref in enumerate((diff_ref, wx_ref, wy_ref, vm_ref)):
        for place in range(HALO):
            for half in range(2):
                row = Z1_LAM + (index * HALO + place) * LEV + 8 * half
                up_ref[row : row + 8, :] = column(ref, 0, TX - HALO + place, half)
                down_ref[row : row + 8, :] = column(ref, 0, place, half)
    for ref in (up_ref, down_ref):
        ref[Z1_RATE:Z1_INN, :] = inn_ref[LEV : 8 * LEV, :]
        ref[Z1_INN:Z1_ROWS, :] = cells


def pack_second(t_ref, diff_ref, wx_ref, up_ref, down_ref):
    edge_columns(t_ref, (0, NEXT), diff_ref, wx_ref, up_ref, down_ref)
    for ref in (up_ref, down_ref):
        ref[Z2_LAM:Z2_ROWS, :] = t_ref[T_LAM:T_ROWS, :]


def sweep_kernel(
    scale_ref, lam_ref, inn_ref, cell_ref, diff_ref, wx_ref, wy_ref, vm_ref, t_ref, l1_ref, r1_ref, l2_ref, r2_ref,
    out_ref, za_ref, zb_ref, f_ref, ret_ref, e_ref, w_ref, n_ref, s_ref, v_ref, val_ref, cel_ref,
):
    wrap = scale_ref[0]
    first = scale_ref[1]
    extra = scale_ref[2]
    lane = lax.broadcasted_iota(jnp.int32, (8, NY), 1)

    zero = jnp.zeros((8, NY), jnp.float32)
    for edge in range(2):
        base = edge * (LEV + 1) * XW
        for part in range(XW // 8):
            v_ref[base + 8 * part : base + 8 * part + 8, :] = zero
    for at in range(XW):
        for half in range(2):
            fields = []
            for index, ref in enumerate((diff_ref, wx_ref, wy_ref, vm_ref)):
                if at < HALO:
                    row = Z1_LAM + (index * HALO + at) * LEV + 8 * half
                    fields.append(l1_ref[row : row + 8, :])
                elif at < HALO + TX:
                    fields.append(column(ref, 0, at - HALO, half))
                else:
                    row = Z1_LAM + (index * HALO + at - HALO - TX) * LEV + 8 * half
                    fields.append(r1_ref[row : row + 8, :])
            diff, wind_x, wind_y, mixing = fields
            e_rate, w_rate = east(diff, wind_x), west(diff, wind_x)
            n_rate, s_rate = east(diff, wind_y), west(diff, wind_y)
            rows = pl.ds(8 * half * XW + at, 8, stride=XW)
            ret_ref[rows, :] = 1.0 - (e_rate + w_rate + n_rate + s_rate + mixing + mixing)
            e_ref[rows, :] = e_rate
            w_ref[rows, :] = w_rate
            n_ref[rows, :] = jnp.where(lane == 0, 0.0, pltpu.roll(n_rate, 1, 1))
            s_ref[rows, :] = jnp.where(lane == NY - 1, 0.0, pltpu.roll(s_rate, NY - 1, 1))
            v_ref[pl.ds((8 * half + 1) * XW + at, 8, stride=XW), :] = mixing

    for ref in (za_ref, zb_ref):
        for edge in range(2):
            base = edge * (LEV + 1) * XW * 8
            for part in range(XW):
                ref[base + 8 * part : base + 8 * part + 8, :] = zero

    def factor(slot):
        return None if slot < OWN else (first if slot == OWN else wrap)

    def scaled(value, amount):
        return value if amount is None else value * amount

    def place_level(lev, carry):
        for slot in range(STEPS_DEV):
            if slot < OWN:
                row = pl.multiple_of(((slot + NEXT) * LEV + lev) * TX, 8)
                value = lam_ref[pl.ds(row, 8), :]
            else:
                row = pl.multiple_of(((slot - OWN) * LEV + lev) * TX, 8)
                value = t_ref[pl.ds(row, 8), :]
            za_ref[pl.ds(((lev + 1) * XW + HALO) * 8 + slot, 8, stride=8), :] = scaled(value, factor(slot))
        return carry

    lax.fori_loop(0, LEV, place_level, 0)

    def halo_rows(slot, place, half):
        if slot < OWN:
            return 0, (slot * SWEEPS + place) * LEV + 8 * half
        return 1, ((slot - OWN) * SWEEPS + place) * LEV + 8 * half

    for slot in range(STEPS_DEV):
        for half in range(2):
            for place in range(HALO):
                which, row = halo_rows(slot, place + 1, half)
                value = (l1_ref, l2_ref)[which][row : row + 8, :]
                za_ref[pl.ds(((8 * half + 1) * XW + place) * 8 + slot, 8, stride=XW * 8), :] = scaled(value, factor(slot))
                which, row = halo_rows(slot, place, half)
                value = (r1_ref, r2_ref)[which][row : row + 8, :]
                at = HALO + TX + place
                za_ref[pl.ds(((8 * half + 1) * XW + at) * 8 + slot, 8, stride=XW * 8), :] = scaled(value, factor(slot))

    val_ref[0, 0 : 8 * LEV, :] = inn_ref[...]
    cel_ref[0, 0:8, :] = cell_ref[...]
    val_ref[0, 8 * LEV : 12 * LEV, :] = t_ref[T_LAM:T_INN, :] * wrap
    cel_ref[0, 8:16, :] = t_ref[T_INN:T_ROWS, :].astype(jnp.int32)
    for tile, (one, two) in enumerate(((l1_ref, l2_ref), (r1_ref, r2_ref))):
        val_ref[tile + 1, 0:LEV, :] = jnp.zeros((LEV, NY), jnp.float32)
        val_ref[tile + 1, LEV : 8 * LEV, :] = one[Z1_RATE:Z1_INN, :]
        cel_ref[tile + 1, 0:8, :] = one[Z1_INN:Z1_ROWS, :].astype(jnp.int32)
        val_ref[tile + 1, 8 * LEV : 12 * LEV, :] = two[Z2_LAM:Z2_INN, :] * wrap
        cel_ref[tile + 1, 8:16, :] = two[Z2_INN:Z2_ROWS, :].astype(jnp.int32)

    row_y = lax.broadcasted_iota(jnp.int32, (NY, NY), 0)

    def scatter_step(step, carry):
        for tile in range(3):
            value = val_ref[tile, pl.ds(pl.multiple_of(step * LEV, LEV), LEV), :]
            cell = cel_ref[tile, pl.ds(step, 1), :]
            cell_x = lax.shift_right_logical(cell, 7)
            cell_y = cell & (NY - 1)
            high = value.astype(jnp.bfloat16)
            rest = value - high.astype(jnp.float32)
            mid = rest.astype(jnp.bfloat16)
            low = (rest - mid.astype(jnp.float32)).astype(jnp.bfloat16)
            hot_y = jnp.where(row_y == cell_y, 1.0, 0.0).astype(jnp.bfloat16)
            columns = ((0, TX), (TX - HALO, TX), (0, HALO))[tile]
            blocks = []
            for x in range(*columns):
                hot_x = jnp.broadcast_to(jnp.where(cell_x == x, 1.0, 0.0), (LEV, NY)).astype(jnp.bfloat16)
                blocks.append(jnp.concatenate([high * hot_x, mid * hot_x, low * hot_x], axis=1))
            left = jnp.concatenate(blocks, axis=0)
            right = jnp.concatenate([hot_y, hot_y, hot_y], axis=1)
            placed = lax.dot_general(
                left, right, (((1,), (1,)), ((), ())), preferred_element_type=jnp.float32
            )
            start = (HALO, 0, HALO + TX)[tile]
            for index in range(columns[1] - columns[0]):
                for half in range(2):
                    row = index * LEV + 8 * half
                    f_ref[pl.ds((8 * half * XW + start + index) * FT + step, 8, stride=XW * FT), :] = placed[row : row + 8, :]
        return carry

    lax.fori_loop(0, STEPS_DEV + FNEXT, scatter_step, 0)

    for slot in range(STEPS_DEV):
        for half in range(2):
            for at, place, pair in ((0, 0, (l1_ref, l2_ref)), (XW - 1, SWEEPS - 1, (r1_ref, r2_ref))):
                which, row = halo_rows(slot, place, half)
                value = scaled(pair[which][row : row + 8, :], factor(slot))
                rows = pl.ds((8 * half * XW + at) * FT + HALO + slot, 8, stride=XW * FT)
                f_ref[rows, :] = f_ref[rows, :] + value

    @pl.when(extra != 0.0)
    def _():
        for lev in range(LEV):
            rows = pl.ds((lev * XW + HALO) * FT + STEPS_DEV, 8, stride=FT)
            f_ref[rows, :] = f_ref[rows, :] - t_ref[lev * TX : lev * TX + 8, :] * extra
        for half in range(2):
            for place in range(HALO):
                for at, row, ref in (
                    (place, halo_rows(OWN, place + 1, half)[1], l2_ref),
                    (HALO + TX + place, halo_rows(OWN, place, half)[1], r2_ref),
                ):
                    rows = pl.ds((8 * half * XW + at) * FT + STEPS_DEV, 8, stride=XW * FT)
                    f_ref[rows, :] = f_ref[rows, :] - ref[row : row + 8, :] * extra

    def spread(ref, row):
        return jnp.broadcast_to(ref[pl.ds(row, 1), :], (8, NY))

    buffers = (za_ref, zb_ref)
    for sweep in range(SWEEPS):
        source, target = buffers[sweep % 2], buffers[(sweep + 1) % 2]
        offset = HALO - sweep

        def level(lev, carry, source=source, target=target, offset=offset, sweep=sweep):
            def state(up, at):
                return source[pl.ds(pl.multiple_of(((lev + 1 + up) * XW + at) * 8, 8), 8), :]

            for at in range(sweep, XW - sweep):
                row = lev * XW + at
                centre = state(0, at)
                total = f_ref[pl.ds(row * FT + offset, 8), :] + spread(ret_ref, row) * centre
                if at > 0:
                    total = total + spread(e_ref, row - 1) * state(0, at - 1)
                if at < XW - 1:
                    total = total + spread(w_ref, row + 1) * state(0, at + 1)
                total = total + spread(n_ref, row) * pltpu.roll(centre, 1, 1)
                total = total + spread(s_ref, row) * pltpu.roll(centre, NY - 1, 1)
                total = total + spread(v_ref, row) * state(-1, at)
                total = total + spread(v_ref, row + 2 * XW) * state(1, at)
                if sweep < SWEEPS - 1:
                    target[pl.ds(pl.multiple_of(((lev + 1) * XW + at) * 8, 8), 8), :] = total
                else:
                    out_ref[pl.ds(lev * TX + at - HALO, 8, stride=LEV * TX), :] = total
            return carry

        lax.fori_loop(0, LEV, level, 0)


def vmem(count):
    return [pl.BlockSpec(memory_space=pltpu.VMEM)] * count


def rows_of(count):
    return jax.ShapeDtypeStruct((count, NY), jnp.float32)


def body(adjoint_iterate, innovations, station_cells, diffusivity, wind_x, wind_y, vertical_mixing):
    time_parts = lax.axis_size("tm")
    tiles = lax.axis_size("space")
    lam = adjoint_iterate.reshape(STEPS_DEV * LEV * TX, NY)
    inn = innovations.reshape(STEPS_DEV * LEV, NY)
    fields = [field.reshape(LEV * TX, NY) for field in (diffusivity, wind_x, wind_y, vertical_mixing)]

    ahead = [((i + 1) % time_parts, i) for i in range(time_parts)]
    upward = [(i, i + 1) for i in range(tiles - 1)]
    downward = [(i + 1, i) for i in range(tiles - 1)]

    pay_t, pay_up, pay_down = pl.pallas_call(
        pack_first,
        out_shape=(rows_of(T_ROWS), rows_of(Z1_ROWS), rows_of(Z1_ROWS)),
        in_specs=vmem(7),
        out_specs=tuple(vmem(3)),
        name="pack_first",
    )(lam, inn, station_cells, *fields)
    got_t = lax.ppermute(pay_t, "tm", ahead)
    left_one = lax.ppermute(pay_up, "space", upward)
    right_one = lax.ppermute(pay_down, "space", downward)
    pay_up2, pay_down2 = pl.pallas_call(
        pack_second,
        out_shape=(rows_of(Z2_ROWS), rows_of(Z2_ROWS)),
        in_specs=vmem(3),
        out_specs=tuple(vmem(2)),
        name="pack_second",
    )(got_t, fields[0], fields[1])
    left_two = lax.ppermute(pay_up2, "space", upward)
    right_two = lax.ppermute(pay_down2, "space", downward)

    last = lax.axis_index("tm") == time_parts - 1
    scales = jnp.stack(
        [
            jnp.where(last, circ_alpha, 1.0),
            jnp.where(last, 0.0, 1.0),
            jnp.where(last, circ_alpha, 0.0),
        ]
    ).astype(jnp.float32)

    state_rows = (LEV + 2) * XW * 8
    out = pl.pallas_call(
        sweep_kernel,
        out_shape=rows_of(STEPS_DEV * LEV * TX),
        in_specs=[pl.BlockSpec(memory_space=pltpu.SMEM)] + vmem(12),
        out_specs=vmem(1)[0],
        scratch_shapes=[
            pltpu.VMEM((state_rows, NY), jnp.float32),
            pltpu.VMEM((state_rows, NY), jnp.float32),
            pltpu.VMEM((LEV * XW * FT, NY), jnp.float32),
        ]
        + [pltpu.VMEM((LEV * XW, NY), jnp.float32)] * 5
        + [
            pltpu.VMEM(((LEV + 2) * XW, NY), jnp.float32),
            pltpu.VMEM((3, 12 * LEV, NY), jnp.float32),
            pltpu.VMEM((3, 16, NY), jnp.int32),
        ],
        name="sweeps",
    )(scales, lam, inn, station_cells, *fields, got_t, left_one, right_one, left_two, right_two)
    return out.reshape(STEPS_DEV, LEV, TX, NY)


def solution(mesh):
    in_specs = (
        P("tm", None, "space", None),
        P("tm", None, "space"),
        P("tm", "space"),
        P(None, "space", None),
        P(None, "space", None),
        P(None, "space", None),
        P(None, "space", None),
    )
    out_specs = P("tm", None, "space", None)
    return jax.shard_map(body, mesh=mesh, in_specs=in_specs, out_specs=out_specs, check_vma=False)
```

time: 214 us -> 42.3 us (0.20)
  starting transfers between devices: 71.4 us -> 13.5 us
  other arithmetic: 56.4 us -> 0.65 us
  waiting for transfers between devices: 54.2 us -> 7.33 us
  Pallas kernels: 0 us -> 19.1 us
  blocking collectives: 14 us -> 0 us
  local copies, waits for them, and re-layouts: 12.8 us -> 1.43 us
  matrix products: 2.97 us -> 0 us
    ppermute x19 -> x5, starting transfers between devices: 61.9 us -> 13.5 us  [the longest x1 4.05 us: body(): left_two = lax.ppermute(pay_up2, 'space', upward)]
    ppermute x19 -> x5, waiting for transfers between devices: 44.5 us -> 7.33 us  [the longest x1 4.02 us: body(): right_two = lax.ppermute(pay_down2, 'space', downward)]
    concatenate x5 -> x0, other arithmetic: 28.8 us -> none  [with_halo(): jnp.concatenate([lax.ppermute(tail, axis, [(i, (i + 1) % count) for i in...]
    pallas_call x0 -> x3, Pallas kernels: none -> 19.1 us  [the longest x1 15 us: body(): pl.pallas_call(sweep_kernel, out_shape=rows_of(STEPS_DEV * LEV * TX), in_...]
    all_to_all x1 -> x0, blocking collectives: 14 us -> none  [body(): lax.all_to_all(scaled, 'tm', split_axis=1, concat_axis=0, tiled=True)]
    unnamed x8 -> x0, other arithmetic: 13.4 us -> none
    all_to_all x1 -> x0, waiting for transfers between devices: 9.7 us -> none  [body(): lax.all_to_all(restored, 'tm', split_axis=0, concat_axis=1, tiled=True)]
    all_to_all x1 -> x0, starting transfers between devices: 9.48 us -> none  [body(): lax.all_to_all(restored, 'tm', split_axis=0, concat_axis=1, tiled=True)]
  transfers between devices with their start and end apart: 20 -> 5, of which waited for: 15 -> 3; matrix products, arithmetic and copies ran while one was open for 10% -> 2% of each run, Pallas kernels for 0% -> 4%
where the time goes in v1:
time: 42.3 us; the launch traced here: 42 us
  Pallas kernels  19.1 us (45%)
  starting transfers between devices  13.5 us (32%)
  waiting for transfers between devices  7.33 us (17%)
  local copies, waits for them, and re-layouts  1.43 us (3%)
  other arithmetic  0.65 us (2%)
    pallas_call x1, Pallas kernels, body(): pl.pallas_call(sweep_kernel, out_shape=rows_of(STEPS_DEV * LEV * TX), in_...  15 us
    ppermute x1, starting transfers between devices, body(): left_two = lax.ppermute(pay_up2, 'space', upward)  4.05 us
    ppermute x1, waiting for transfers between devices, body(): right_two = lax.ppermute(pay_down2, 'space', downward)  4.02 us
    ppermute x1, starting transfers between devices, body(): left_one = lax.ppermute(pay_up, 'space', upward)  3.49 us
    ppermute x1, starting transfers between devices, body(): got_t = lax.ppermute(pay_t, 'tm', ahead)  3.36 us
    ppermute x1, waiting for transfers between devices, body(): left_two = lax.ppermute(pay_up2, 'space', upward)  2.8 us
    pallas_call x1, Pallas kernels, body(): pl.pallas_call(pack_first, out_shape=(rows_of(T_ROWS), rows_of(Z1_ROWS),...  2.18 us
    pallas_call x1, Pallas kernels, body(): pl.pallas_call(pack_second, out_shape=(rows_of(Z2_ROWS), rows_of(Z2_ROWS)...  1.87 us
  transfers between devices with their start and end apart: 5, of which 3 were waited for; matrix products, arithmetic and copies ran while one was open for 2% of the time, Pallas kernels for 4%

profile of v1, /device:TPU:0, one launch (start us, length us, event | category | flops | bytes accessed | tf_op | source)
XLA Modules:
  0.0 42.0 jit_solution(14998483484346434178)
XLA Ops:
  0.0 2.2 %pack_first.1 = (f32[712,128]{1,0:T(8,128)}, f32[616,128]{1,0:T(8,128)}, f32[616,128]{1,0:T(8,128)}) custom-call(f32[1024,128]{1,0:T(8,128)} %bitcast.10, f32[128,128]{1,0:T(8,128)} %bitcast.18, s32[8,128]{1,0:T(8,128)} %cell_ref.3, f32[128,128]{1,0:T(8,128)} %bitcast.12, f32[128,128]{1,0:T(8,128)} %bitcast.15, f32[128,128]{1,0:T(8,128)} %bitcast.20, ...), custom_call_target="tpu_custom_call" | custom-call | tf_op jit(solution)/shard_map/pack_first/pallas_call | solution.py:283
  2.2 3.4 %collective-permute-start = (f32[712,128]{1,0:T(8,128)}, f32[712,128]{1,0:T(8,128)S(1)}, u32[]{:S(2)}, u32[]{:S(2)}) collective-permute-start(f32[712,128]{1,0:T(8,128)} %get-tuple-element.10), channel_id=1, source_target_pairs={{4,0},{8,4},{12,8},{16,12},{20,16},{24,20},{28,24},{0,28},{5,1},{9... | collective-permute-start | bytes 1093640 | tf_op jit(solution)/shard_map/ppermute | solution.py:290
  5.5 3.5 %collective-permute-start.1 = (f32[616,128]{1,0:T(8,128)}, f32[616,128]{1,0:T(8,128)S(1)}, u32[]{:S(2)}, u32[]{:S(2)}) collective-permute-start(f32[616,128]{1,0:T(8,128)} %get-tuple-element.11), channel_id=1, source_target_pairs={{0,1},{1,2},{2,3},{4,5},{5,6},{6,7},{8,9},{9,10},{10,11},{12,13},{... | collective-permute-start | bytes 946184 | tf_op jit(solution)/shard_map/ppermute | solution.py:291
  9.0 1.3 %collective-permute-start.2 = (f32[616,128]{1,0:T(8,128)}, f32[616,128]{1,0:T(8,128)S(1)}, u32[]{:S(2)}, u32[]{:S(2)}) collective-permute-start(f32[616,128]{1,0:T(8,128)} %get-tuple-element.12), channel_id=1, source_target_pairs={{1,0},{2,1},{3,2},{5,4},{6,5},{7,6},{9,8},{10,9},{11,10},{13,12},{... | collective-permute-start | bytes 946184 | tf_op jit(solution)/shard_map/ppermute | solution.py:292
  10.3 0.5 %collective-permute-done.t_ref = f32[712,128]{1,0:T(8,128)S(1)} collective-permute-done((f32[712,128]{1,0:T(8,128)}, f32[712,128]{1,0:T(8,128)S(1)}, u32[]{:S(2)}, u32[]{:S(2)}) %collective-permute-start) | collective-permute-done | bytes 364576 | tf_op jit(solution)/shard_map/ppermute | solution.py:290
  10.8 0.0 copy-start
  10.8 0.7 %copy-done = f32[712,128]{1,0:T(8,128)} copy-done((f32[712,128]{1,0:T(8,128)}, f32[712,128]{1,0:T(8,128)S(1)}, u32[]{:S(2)}) %copy-start) | copy-done | bytes 364568
  11.6 1.9 %pack_second.1 = (f32[472,128]{1,0:T(8,128)}, f32[472,128]{1,0:T(8,128)}) custom-call(f32[712,128]{1,0:T(8,128)} %copy-done, f32[128,128]{1,0:T(8,128)} %bitcast.13, f32[128,128]{1,0:T(8,128)} %bitcast.16), custom_call_target="tpu_custom_call" | custom-call | tf_op jit(solution)/shard_map/pack_second/pallas_call | solution.py:293
  13.4 4.1 %collective-permute-start.3 = (f32[472,128]{1,0:T(8,128)}, f32[472,128]{1,0:T(8,128)S(1)}, u32[]{:S(2)}, u32[]{:S(2)}) collective-permute-start(f32[472,128]{1,0:T(8,128)} %get-tuple-element.13), channel_id=1, source_target_pairs={{0,1},{1,2},{2,3},{4,5},{5,6},{6,7},{8,9},{9,10},{10,11},{12,13},{... | collective-permute-start | bytes 725000 | tf_op jit(solution)/shard_map/ppermute | solution.py:300
  17.5 1.3 %collective-permute-start.4 = (f32[472,128]{1,0:T(8,128)}, f32[472,128]{1,0:T(8,128)S(1)}, u32[]{:S(2)}, u32[]{:S(2)}) collective-permute-start(f32[472,128]{1,0:T(8,128)} %get-tuple-element.14), channel_id=1, source_target_pairs={{1,0},{2,1},{3,2},{5,4},{6,5},{7,6},{9,8},{10,9},{11,10},{13,12},{... | collective-permute-start | bytes 725000 | tf_op jit(solution)/shard_map/ppermute | solution.py:301
  18.8 0.7 %pad_maximum_fusion.scale_ref = f32[3]{0:T(128)} fusion(f32[1]{0:T(128)} %bitcast.2, f32[1]{0:T(128)} %bitcast.1, f32[1]{0:T(128)} %bitcast), kind=kLoop, calls=%fused_computation | loop fusion | flops 6 | bytes 24 | tf_op jit(solution)/shard_map/stack | solution.py:304
  19.5 0.0 collective-permute-done.1.l1_ref
  19.5 0.0 copy-start.1
  19.5 0.0 collective-permute-done.2.r1_ref
  19.5 0.0 copy-start.2
  19.5 2.8 %collective-permute-done.3.l2_ref = f32[472,128]{1,0:T(8,128)S(1)} collective-permute-done((f32[472,128]{1,0:T(8,128)}, f32[472,128]{1,0:T(8,128)S(1)}, u32[]{:S(2)}, u32[]{:S(2)}) %collective-permute-start.3) | collective-permute-done | bytes 241696 | tf_op jit(solution)/shard_map/ppermute | solution.py:300
  22.3 0.0 copy-start.3
  22.3 4.0 %collective-permute-done.4.r2_ref = f32[472,128]{1,0:T(8,128)S(1)} collective-permute-done((f32[472,128]{1,0:T(8,128)}, f32[472,128]{1,0:T(8,128)S(1)}, u32[]{:S(2)}, u32[]{:S(2)}) %collective-permute-start.4) | collective-permute-done | bytes 241696 | tf_op jit(solution)/shard_map/ppermute | solution.py:301
  26.3 0.0 copy-done.1
  26.3 0.0 copy-done.2
  26.3 0.0 copy-done.3
  26.3 0.0 copy-start.4
  26.3 0.7 %copy-done.4 = f32[472,128]{1,0:T(8,128)} copy-done((f32[472,128]{1,0:T(8,128)}, f32[472,128]{1,0:T(8,128)S(1)}, u32[]{:S(2)}) %copy-start.4) | copy-done | bytes 241688
  27.0 15.0 %sweeps.1 = f32[1024,128]{1,0:T(8,128)} custom-call(f32[3]{0:T(128)} %pad_maximum_fusion.scale_ref, f32[1024,128]{1,0:T(8,128)} %bitcast.11, f32[128,128]{1,0:T(8,128)} %bitcast.19, s32[8,128]{1,0:T(8,128)} %cell_ref.3, f32[128,128]{1,0:T(8,128)} %bitcast.14, f32[128,128]{1,0:T(8,128)} %bitcast.17, f32[128,128]{1,0:T(8,128)} %bitcast.21, ...), custom_call_target="tpu_custom_call" | custom-call | tf_op jit(solution)/shard_map/sweeps/pallas_call | solution.py:313
Async XLA Ops:
  2.2 8.7 %collective-permute-start = (f32[712,128]{1,0:T(8,128)}, f32[712,128]{1,0:T(8,128)S(1)}, u32[]{:S(2)}, u32[]{:S(2)}) collective-permute-start(f32[712,128]{1,0:T(8,128)} %get-tuple-element.10), channel_id=1, source_target_pairs={{4,0},{8,4},{12,8},{16,12},{20,16},{24,20},{28,24},{0,28},{5,1},{9... | collective-permute-start | bytes 1093640 | tf_op jit(solution)/shard_map/ppermute | solution.py:290
  5.5 13.9 %collective-permute-start.1 = (f32[616,128]{1,0:T(8,128)}, f32[616,128]{1,0:T(8,128)S(1)}, u32[]{:S(2)}, u32[]{:S(2)}) collective-permute-start(f32[616,128]{1,0:T(8,128)} %get-tuple-element.11), channel_id=1, source_target_pairs={{0,1},{1,2},{2,3},{4,5},{5,6},{6,7},{8,9},{9,10},{10,11},{12,13},{... | collective-permute-start | bytes 946184 | tf_op jit(solution)/shard_map/ppermute | solution.py:291
  9.0 10.4 %collective-permute-start.2 = (f32[616,128]{1,0:T(8,128)}, f32[616,128]{1,0:T(8,128)S(1)}, u32[]{:S(2)}, u32[]{:S(2)}) collective-permute-start(f32[616,128]{1,0:T(8,128)} %get-tuple-element.12), channel_id=1, source_target_pairs={{1,0},{2,1},{3,2},{5,4},{6,5},{7,6},{9,8},{10,9},{11,10},{13,12},{... | collective-permute-start | bytes 946184 | tf_op jit(solution)/shard_map/ppermute | solution.py:292
  10.8 0.7 %copy-start = (f32[712,128]{1,0:T(8,128)}, f32[712,128]{1,0:T(8,128)S(1)}, u32[]{:S(2)}) copy-start(f32[712,128]{1,0:T(8,128)S(1)} %collective-permute-done.t_ref) | copy-start | bytes 1093636
  13.4 8.8 %collective-permute-start.3 = (f32[472,128]{1,0:T(8,128)}, f32[472,128]{1,0:T(8,128)S(1)}, u32[]{:S(2)}, u32[]{:S(2)}) collective-permute-start(f32[472,128]{1,0:T(8,128)} %get-tuple-element.13), channel_id=1, source_target_pairs={{0,1},{1,2},{2,3},{4,5},{5,6},{6,7},{8,9},{9,10},{10,11},{12,13},{... | collective-permute-start | bytes 725000 | tf_op jit(solution)/shard_map/ppermute | solution.py:300
  17.5 8.8 %collective-permute-start.4 = (f32[472,128]{1,0:T(8,128)}, f32[472,128]{1,0:T(8,128)S(1)}, u32[]{:S(2)}, u32[]{:S(2)}) collective-permute-start(f32[472,128]{1,0:T(8,128)} %get-tuple-element.14), channel_id=1, source_target_pairs={{1,0},{2,1},{3,2},{5,4},{6,5},{7,6},{9,8},{10,9},{11,10},{13,12},{... | collective-permute-start | bytes 725000 | tf_op jit(solution)/shard_map/ppermute | solution.py:301
  19.5 6.8 %copy-start.1 = (f32[616,128]{1,0:T(8,128)}, f32[616,128]{1,0:T(8,128)S(1)}, u32[]{:S(2)}) copy-start(f32[616,128]{1,0:T(8,128)S(1)} %collective-permute-done.1.l1_ref) | copy-start | bytes 946180
  19.5 6.8 %copy-start.2 = (f32[616,128]{1,0:T(8,128)}, f32[616,128]{1,0:T(8,128)S(1)}, u32[]{:S(2)}) copy-start(f32[616,128]{1,0:T(8,128)S(1)} %collective-permute-done.2.r1_ref) | copy-start | bytes 946180
  22.3 4.0 %copy-start.3 = (f32[472,128]{1,0:T(8,128)}, f32[472,128]{1,0:T(8,128)S(1)}, u32[]{:S(2)}) copy-start(f32[472,128]{1,0:T(8,128)S(1)} %collective-permute-done.3.l2_ref) | copy-start | bytes 724996
  26.3 0.7 %copy-start.4 = (f32[472,128]{1,0:T(8,128)}, f32[472,128]{1,0:T(8,128)S(1)}, u32[]{:S(2)}) copy-start(f32[472,128]{1,0:T(8,128)S(1)} %collective-permute-done.4.r2_ref) | copy-start | bytes 724996

commit v2 on v0

v2 whole, which is shorter than its diff:
```python
import jax
import jax.numpy as jnp
from jax import lax
from jax.experimental import pallas as pl
from jax.experimental.pallas import tpu as pltpu
from jax.sharding import PartitionSpec as P

LEV = 16
TX = 8
NY = 128
STEPS_DEV = 8
SWEEPS = 5
HALO = SWEEPS - 1
NEXT = SWEEPS
FNEXT = SWEEPS - 1
OWN = STEPS_DEV - NEXT
XW = TX + 2 * HALO
ZW = XW + 2
STEP = LEV * TX
PLANE = XW * LEV

circ_alpha = 0.1

TAIL = FNEXT * LEV + 8
T_COL = NEXT * LEV
T_ROWS = 2 * TAIL + TX * T_COL
N_LAM = SWEEPS * OWN * LEV
N_RATE = N_LAM + 4 * HALO * LEV
N_EDGE = N_RATE + LEV
N_INN = N_EDGE + 7 * LEV
N_ROWS = N_INN + 8
M_LAM = SWEEPS * T_COL
M_ROWS = M_LAM + TAIL


def toward(diff, wind):
    return diff + jnp.maximum(-wind, 0.0)


def against(diff, wind):
    return diff + jnp.maximum(wind, 0.0)


def column(ref, base, col, half):
    return ref[pl.ds(base + half * 8 * TX + col, 8, stride=TX), :]


def pack_kernel(lam_ref, inn_ref, cell_ref, diff_ref, wx_ref, wy_ref, vm_ref, up_ref, down_ref, t_ref):
    cells = cell_ref[...].astype(jnp.float32)
    rates = (diff_ref, wx_ref, wy_ref, vm_ref)
    for half in range(2):
        for place in range(SWEEPS):
            for slot in range(OWN):
                row = (place * OWN + slot) * LEV + 8 * half
                base = (NEXT + slot) * STEP
                up_ref[row : row + 8, :] = column(lam_ref, base, TX - SWEEPS + place, half)
                down_ref[row : row + 8, :] = column(lam_ref, base, place, half)
        for index, ref in enumerate(rates):
            for place in range(HALO):
                row = N_LAM + (index * HALO + place) * LEV + 8 * half
                up_ref[row : row + 8, :] = column(ref, 0, TX - HALO + place, half)
                down_ref[row : row + 8, :] = column(ref, 0, place, half)
        row = N_RATE + 8 * half
        col = TX - SWEEPS
        up_ref[row : row + 8, :] = toward(column(diff_ref, 0, col, half), column(wx_ref, 0, col, half))
        col = SWEEPS - 1
        down_ref[row : row + 8, :] = against(column(diff_ref, 0, col, half), column(wx_ref, 0, col, half))
    for ref in (up_ref, down_ref):
        ref[N_EDGE:N_INN, :] = inn_ref[LEV : 8 * LEV, :]
        ref[N_INN:N_ROWS, :] = cells
    for half in range(2):
        for col in range(TX):
            for slot in range(NEXT):
                row = TAIL + col * T_COL + slot * LEV + 8 * half
                t_ref[row : row + 8, :] = column(lam_ref, slot * STEP, col, half)
    for base in (0, TAIL + TX * T_COL):
        t_ref[base : base + FNEXT * LEV, :] = inn_ref[0 : FNEXT * LEV, :]
        t_ref[base + FNEXT * LEV : base + TAIL, :] = cells


def place_forcing(value, cell, columns, row_y):
    cell_x = lax.shift_right_logical(cell, 7).astype(jnp.float32)
    cell_y = (cell & (NY - 1)).astype(jnp.float32)
    high = value.astype(jnp.bfloat16)
    rest = value - high.astype(jnp.float32)
    mid = rest.astype(jnp.bfloat16)
    low = (rest - mid.astype(jnp.float32)).astype(jnp.bfloat16)
    spread_x = jnp.broadcast_to(cell_x, (LEV, NY)).astype(jnp.bfloat16)
    spread_y = jnp.broadcast_to(cell_y, (LEV, NY)).astype(jnp.bfloat16)
    zero = jnp.zeros((LEV, NY), jnp.bfloat16)
    one = jnp.ones((LEV, NY), jnp.bfloat16)
    hot_y = jnp.concatenate(
        [jnp.where(row_y[LEV * part : LEV * part + LEV] == spread_y, one, zero) for part in range(NY // LEV)], axis=0
    )
    blocks = []
    for x in range(*columns):
        hot = spread_x == jnp.full((LEV, NY), x, jnp.bfloat16)
        blocks.append(jnp.concatenate([jnp.where(hot, part, zero) for part in (high, mid, low)], axis=1))
    return lax.dot_general(
        jnp.concatenate(blocks, axis=0),
        jnp.concatenate([hot_y, hot_y, hot_y], axis=1),
        (((1,), (1,)), ((), ())),
        preferred_element_type=jnp.float32,
    )


def level_rows():
    return lax.broadcasted_iota(jnp.int32, (NY, NY), 0).astype(jnp.float32).astype(jnp.bfloat16)


LEFT = (TX - HALO, TX)
RIGHT = (0, HALO)


def sweeps(chains, first_chain, za_ref, zb_ref, coef_ref, forcing_rows, store):
    width = chains * LEV
    buffers = (za_ref, zb_ref)
    for sweep in range(SWEEPS):
        source, target = buffers[sweep % 2], buffers[(sweep + 1) % 2]

        def at_column(at, carry, source=source, target=target, sweep=sweep):
            base = pl.multiple_of(at * width, LEV)
            plane = pl.multiple_of((at - 1) * LEV, LEV)
            for half in range(2):
                coef = [coef_ref[pl.ds(kind * PLANE + plane + 8 * half, 8), :] for kind in range(7)]
                for chain in range(chains):
                    row = base + chain * LEV + 8 * half
                    centre = source[pl.ds(row, 8), :]
                    step = first_chain + chain + HALO - sweep
                    ref, start = forcing_rows(step)
                    total = ref[pl.ds(start + plane + 8 * half, 8), :] + coef[0] * centre
                    total = total + coef[1] * source[pl.ds(row - width, 8), :]
                    total = total + coef[2] * source[pl.ds(row + width, 8), :]
                    total = total + coef[3] * pltpu.roll(centre, 1, 1)
                    total = total + coef[4] * pltpu.roll(centre, NY - 1, 1)
                    total = total + coef[5] * source[pl.ds(row - 1, 8), :]
                    total = total + coef[6] * source[pl.ds(row + 1, 8), :]
                    if sweep < SWEEPS - 1:
                        target[pl.ds(row, 8), :] = total
                    else:
                        store(chain, at, half, total)
            return carry

        lax.fori_loop(sweep + 1, ZW - 1 - sweep, at_column, 0)


def early_kernel(
    wrap_ref, lam_ref, inn_ref, cell_ref, diff_ref, wx_ref, wy_ref, vm_ref, t_ref, left_ref, right_ref,
    out_ref, coef_ref, f_ref, fown_ref,
    za_ref, zb_ref,
):
    wrap = wrap_ref[0]
    lane = lax.broadcasted_iota(jnp.int32, (8, NY), 1)
    sub = lax.broadcasted_iota(jnp.int32, (8, NY), 0)
    e_rows, w_rows = {}, {}
    for at in range(XW):
        mixings = []
        for half in range(2):
            fields = []
            for index, ref in enumerate((diff_ref, wx_ref, wy_ref, vm_ref)):
                if HALO <= at < HALO + TX:
                    fields.append(column(ref, 0, at - HALO, half))
                else:
                    side, place = (left_ref, at) if at < HALO else (right_ref, at - HALO - TX)
                    row = N_LAM + (index * HALO + place) * LEV + 8 * half
                    fields.append(side[row : row + 8, :])
            diff, wind_x, wind_y, mixing = fields
            e_rate, w_rate = toward(diff, wind_x), against(diff, wind_x)
            n_rate, s_rate = toward(diff, wind_y), against(diff, wind_y)
            mixings.append(mixing)
            row = at * LEV + 8 * half

            def put(kind, at_row, value):
                coef_ref[kind * PLANE + at_row : kind * PLANE + at_row + 8, :] = value

            put(0, row, 1.0 - (e_rate + w_rate + n_rate + s_rate + mixing + mixing))
            if at < XW - 1:
                put(1, row + LEV, e_rate)
            if at > 0:
                put(2, row - LEV, w_rate)
            put(3, row, jnp.where(lane == 0, 0.0, pltpu.roll(n_rate, 1, 1)))
            put(4, row, jnp.where(lane == NY - 1, 0.0, pltpu.roll(s_rate, NY - 1, 1)))
        row = at * LEV
        down_low, down_high = pltpu.roll(mixings[0], 1, 0), pltpu.roll(mixings[1], 1, 0)
        put(5, row, jnp.where(sub == 0, 0.0, down_low))
        put(5, row + 8, jnp.where(sub == 0, down_low, down_high))
        up_low, up_high = pltpu.roll(mixings[0], 7, 0), pltpu.roll(mixings[1], 7, 0)
        put(6, row, jnp.where(sub == 7, up_high, up_low))
        put(6, row + 8, jnp.where(sub == 7, 0.0, up_high))
    coef_ref[PLANE : PLANE + LEV, :] = left_ref[N_RATE:N_EDGE, :]
    coef_ref[3 * PLANE - LEV : 3 * PLANE, :] = right_ref[N_RATE:N_EDGE, :]

    row_y = level_rows()

    def own_step(step, carry):
        value = inn_ref[pl.ds(pl.multiple_of(step * LEV, LEV), LEV), :]
        placed = place_forcing(value, cell_ref[pl.ds(step, 1), :], (0, TX), row_y)
        f_ref[pl.ds(pl.multiple_of(step * PLANE + HALO * LEV, LEV), TX * LEV), :] = placed
        return carry

    lax.fori_loop(0, STEPS_DEV, own_step, 0)

    def next_step(step, carry):
        value = t_ref[pl.ds(pl.multiple_of(step * LEV, LEV), LEV), :] * wrap
        cell = t_ref[pl.ds(FNEXT * LEV + step, 1), :].astype(jnp.int32)
        fown_ref[pl.ds(pl.multiple_of(step * STEP, STEP), STEP), :] = place_forcing(value, cell, (0, TX), row_y)
        return carry

    lax.fori_loop(0, FNEXT, next_step, 0)

    def side_step(step, carry):
        for ref, columns, start in ((left_ref, LEFT, 0), (right_ref, RIGHT, HALO + TX)):
            value = ref[pl.ds(pl.multiple_of(N_EDGE + (step - 1) * LEV, LEV), LEV), :]
            cell = ref[pl.ds(N_INN + step, 1), :].astype(jnp.int32)
            placed = place_forcing(value, cell, columns, row_y)
            f_ref[pl.ds(pl.multiple_of(step * PLANE + start * LEV, LEV), HALO * LEV), :] = placed
        return carry

    lax.fori_loop(1, STEPS_DEV, side_step, 0)

    block = SWEEPS * OWN * LEV
    za_ref[0:block, :] = left_ref[0:block, :]
    za_ref[block + TX * OWN * LEV : 2 * block + TX * OWN * LEV, :] = right_ref[0:block, :]
    for col in range(TX):
        for slot in range(OWN):
            for half in range(2):
                row = block + (col * OWN + slot) * LEV + 8 * half
                za_ref[row : row + 8, :] = column(lam_ref, (NEXT + slot) * STEP, col, half)

    def store(chain, at, half, total):
        out_ref[pl.ds(chain * STEP + half * 8 * TX + at - SWEEPS, 8, stride=TX), :] = total

    sweeps(OWN, 0, za_ref, zb_ref, coef_ref, lambda step: (f_ref, step * PLANE), store)


def late_kernel(
    scale_ref, early_ref, coef_ref, f_ref, fown_ref, t_ref, left_ref, right_ref,
    out_ref, za_ref, zb_ref, fnext_ref,
):
    wrap, first, extra = scale_ref[0], scale_ref[1], scale_ref[2]
    out_ref[0 : OWN * STEP, :] = early_ref[...]
    for at in range(ZW):
        if at < SWEEPS:
            ref, base = left_ref, at * T_COL
        elif at < SWEEPS + TX:
            ref, base = t_ref, TAIL + (at - SWEEPS) * T_COL
        else:
            ref, base = right_ref, TAIL + (at - SWEEPS - TX) * T_COL
        row = at * T_COL
        za_ref[row : row + LEV, :] = ref[base : base + LEV, :] * first
        za_ref[row + LEV : row + T_COL, :] = ref[base + LEV : base + T_COL, :] * wrap

    row_y = level_rows()

    def side_step(step, carry):
        for ref, base, columns, start in ((left_ref, M_LAM, LEFT, 0), (right_ref, 0, RIGHT, HALO + TX)):
            value = ref[pl.ds(pl.multiple_of(base + step * LEV, LEV), LEV), :] * wrap
            cell = ref[pl.ds(base + FNEXT * LEV + step, 1), :].astype(jnp.int32)
            placed = place_forcing(value, cell, columns, row_y)
            fnext_ref[pl.ds(pl.multiple_of(step * PLANE + start * LEV, LEV), HALO * LEV), :] = placed
        rows = pl.ds(pl.multiple_of(step * PLANE + HALO * LEV, LEV), STEP)
        fnext_ref[rows, :] = fown_ref[pl.ds(pl.multiple_of(step * STEP, STEP), STEP), :]
        return carry

    lax.fori_loop(0, FNEXT, side_step, 0)

    @pl.when(extra != 0.0)
    def _():
        for at in range(XW):
            if at < HALO:
                ref, base = left_ref, (at + 1) * T_COL
            elif at < HALO + TX:
                ref, base = t_ref, TAIL + (at - HALO) * T_COL
            else:
                ref, base = right_ref, TAIL + (at - HALO - TX) * T_COL
            rows = slice(at * LEV, at * LEV + LEV)
            fnext_ref[rows, :] = fnext_ref[rows, :] - ref[base : base + LEV, :] * extra

    def forcing_rows(step):
        return (f_ref, (step - OWN) * PLANE) if step < STEPS_DEV else (fnext_ref, (step - STEPS_DEV) * PLANE)

    def store(chain, at, half, total):
        out_ref[pl.ds((OWN + chain) * STEP + half * 8 * TX + at - SWEEPS, 8, stride=TX), :] = total

    sweeps(NEXT, OWN, za_ref, zb_ref, coef_ref, forcing_rows, store)


def vmem(count):
    return [pl.BlockSpec(memory_space=pltpu.VMEM)] * count


def rows_of(count):
    return jax.ShapeDtypeStruct((count, NY), jnp.float32)


def scratch(count):
    return pltpu.VMEM((count, NY), jnp.float32)


SMEM_SPEC = pl.BlockSpec(memory_space=pltpu.SMEM)


def body(adjoint_iterate, innovations, station_cells, diffusivity, wind_x, wind_y, vertical_mixing):
    time_parts = lax.axis_size("tm")
    tiles = lax.axis_size("space")
    lam = adjoint_iterate.reshape(STEPS_DEV * STEP, NY)
    inn = innovations.reshape(STEPS_DEV * LEV, NY)
    fields = [field.reshape(STEP, NY) for field in (diffusivity, wind_x, wind_y, vertical_mixing)]
    last = lax.axis_index("tm") == time_parts - 1
    scales = jnp.where(
        last, jnp.array([circ_alpha, 0.0, circ_alpha], jnp.float32), jnp.array([1.0, 1.0, 0.0], jnp.float32)
    )

    ahead = [((i + 1) % time_parts, i) for i in range(time_parts)]
    upward = [(i, i + 1) for i in range(tiles - 1)]
    downward = [(i + 1, i) for i in range(tiles - 1)]

    pay_up, pay_down, pay_t = pl.pallas_call(
        pack_kernel,
        out_shape=(rows_of(N_ROWS), rows_of(N_ROWS), rows_of(T_ROWS)),
        in_specs=vmem(7),
        out_specs=tuple(vmem(3)),
        compiler_params=pltpu.CompilerParams(vmem_limit_bytes=8 << 20),
        name="pack",
    )(lam, inn, station_cells, *fields)
    got_t = lax.ppermute(pay_t, "tm", ahead)
    left_one = lax.ppermute(pay_up, "space", upward)
    right_one = lax.ppermute(pay_down, "space", downward)
    left_two = lax.ppermute(got_t[T_ROWS - M_ROWS :], "space", upward)
    right_two = lax.ppermute(got_t[:M_ROWS], "space", downward)

    out_early, coef, forcing, forcing_next = pl.pallas_call(
        early_kernel,
        out_shape=(rows_of(OWN * STEP), rows_of(7 * PLANE), rows_of(STEPS_DEV * PLANE), rows_of(FNEXT * STEP)),
        in_specs=[SMEM_SPEC] + vmem(10),
        out_specs=tuple(vmem(4)),
        scratch_shapes=[scratch(ZW * OWN * LEV), scratch(ZW * OWN * LEV)],
        compiler_params=pltpu.CompilerParams(vmem_limit_bytes=20 << 20),
        cost_estimate=pl.CostEstimate(flops=20_000_000, bytes_accessed=8_000_000, transcendentals=0),
        name="early",
    )(scales, lam, inn, station_cells, *fields, got_t, left_one, right_one)

    out = pl.pallas_call(
        late_kernel,
        out_shape=rows_of(STEPS_DEV * STEP),
        in_specs=[SMEM_SPEC] + vmem(7),
        out_specs=vmem(1)[0],
        scratch_shapes=[scratch(ZW * T_COL), scratch(ZW * T_COL), scratch(FNEXT * PLANE)],
        compiler_params=pltpu.CompilerParams(vmem_limit_bytes=20 << 20),
        cost_estimate=pl.CostEstimate(flops=20_000_000, bytes_accessed=8_000_000, transcendentals=0),
        name="late",
    )(scales, out_early, coef, forcing[OWN * PLANE :], forcing_next, got_t, left_two, right_two)
    return out.reshape(STEPS_DEV, LEV, TX, NY)


def solution(mesh):
    in_specs = (
        P("tm", None, "space", None),
        P("tm", None, "space"),
        P("tm", "space"),
        P(None, "space", None),
        P(None, "space", None),
        P(None, "space", None),
        P(None, "space", None),
    )
    out_specs = P("tm", None, "space", None)
    return jax.shard_map(body, mesh=mesh, in_specs=in_specs, out_specs=out_specs, check_vma=False)
```

time: 214 us -> 41.5 us (0.19)
  starting transfers between devices: 71.4 us -> 13.8 us
  other arithmetic: 56.4 us -> 0.01 us
  waiting for transfers between devices: 54.2 us -> 2.4 us
  Pallas kernels: 0 us -> 17.8 us
  blocking collectives: 14 us -> 0 us
  local copies, waits for them, and re-layouts: 12.8 us -> 6.69 us
  matrix products: 2.97 us -> 0 us
    ppermute x19 -> x5, starting transfers between devices: 61.9 us -> 13.8 us  [the longest x1 4.18 us: body(): left_two = lax.ppermute(got_t[T_ROWS - M_ROWS:], 'space', upward)]
    ppermute x19 -> x5, waiting for transfers between devices: 44.5 us -> 2.4 us  [the longest x1 2 us: body(): right_one = lax.ppermute(pay_down, 'space', downward)]
    concatenate x5 -> x0, other arithmetic: 28.8 us -> none  [with_halo(): jnp.concatenate([lax.ppermute(tail, axis, [(i, (i + 1) % count) for i in...]
    pallas_call x0 -> x3, Pallas kernels: none -> 17.8 us  [the longest x1 9.72 us: body(): pl.pallas_call(early_kernel, out_shape=(rows_of(OWN * STEP), rows_of(7 *...]
    all_to_all x1 -> x0, blocking collectives: 14 us -> none  [body(): lax.all_to_all(scaled, 'tm', split_axis=1, concat_axis=0, tiled=True)]
    unnamed x8 -> x0, other arithmetic: 13.4 us -> none
    all_to_all x1 -> x0, waiting for transfers between devices: 9.7 us -> none  [body(): lax.all_to_all(restored, 'tm', split_axis=0, concat_axis=1, tiled=True)]
    all_to_all x1 -> x0, starting transfers between devices: 9.48 us -> none  [body(): lax.all_to_all(restored, 'tm', split_axis=0, concat_axis=1, tiled=True)]
  transfers between devices with their start and end apart: 20 -> 5, of which waited for: 15 -> 2; matrix products, arithmetic and copies ran while one was open for 10% -> 0% of each run, Pallas kernels for 0% -> 24%
where the time goes in v2:
time: 41.5 us; the launch traced here: 40.9 us
  Pallas kernels  17.8 us (43%)
  starting transfers between devices  13.8 us (33%)
  local copies, waits for them, and re-layouts  6.69 us (16%)
  waiting for transfers between devices  2.4 us (6%)
    pallas_call x1, Pallas kernels, body(): pl.pallas_call(early_kernel, out_shape=(rows_of(OWN * STEP), rows_of(7 *...  9.72 us
    pallas_call x1, Pallas kernels, body(): pl.pallas_call(late_kernel, out_shape=rows_of(STEPS_DEV * STEP), in_specs...  7.97 us
    unnamed x30, local copies, waits for them, and re-layouts  6.62 us
    ppermute x1, starting transfers between devices, body(): left_two = lax.ppermute(got_t[T_ROWS - M_ROWS:], 'space', upward)  4.18 us
    ppermute x1, starting transfers between devices, body(): left_one = lax.ppermute(pay_up, 'space', upward)  3.49 us
    ppermute x1, starting transfers between devices, body(): got_t = lax.ppermute(pay_t, 'tm', ahead)  3.41 us
    ppermute x1, waiting for transfers between devices, body(): right_one = lax.ppermute(pay_down, 'space', downward)  2 us
    ppermute x1, starting transfers between devices, body(): right_one = lax.ppermute(pay_down, 'space', downward)  1.42 us
  transfers between devices with their start and end apart: 5, of which 2 were waited for; matrix products, arithmetic and copies ran while one was open for 0% of the time, Pallas kernels for 24%

profile of v2, /device:TPU:0, one launch (start us, length us, event | category | flops | bytes accessed | tf_op | source)
XLA Modules:
  0.0 40.9 jit_solution(4617303567560025989)
XLA Ops:
  0.0 0.7 %copy-done.12 = s32[8,128]{1,0:T(8,128)S(1)} copy-done((s32[8,128]{1,0:T(8,128)S(1)}, s32[8,128]{1,0:T(8,128)}, u32[]{:S(2)}) %copy-start.12) | copy-done | bytes 4120
  0.7 1.0 %copy-done = f32[8,16,8,128]{3,2,1,0:T(8,128)S(1)} copy-done((f32[8,16,8,128]{3,2,1,0:T(8,128)S(1)}, f32[8,16,8,128]{3,2,1,0:T(8,128)}, u32[]{:S(2)}) %copy-start) | copy-done | bytes 524312
  1.7 0.8 %copy-done.2 = f32[8,16,128]{2,1,0:T(8,128)S(1)} copy-done((f32[8,16,128]{2,1,0:T(8,128)S(1)}, f32[8,16,128]{2,1,0:T(8,128)}, u32[]{:S(2)}) %copy-start.2) | copy-done | bytes 65560
  2.6 0.8 %copy-done.4 = f32[16,8,128]{2,1,0:T(8,128)S(1)} copy-done((f32[16,8,128]{2,1,0:T(8,128)S(1)}, f32[16,8,128]{2,1,0:T(8,128)}, u32[]{:S(2)}) %copy-start.4) | copy-done | bytes 65560
  3.4 0.8 %copy-done.6 = f32[16,8,128]{2,1,0:T(8,128)S(1)} copy-done((f32[16,8,128]{2,1,0:T(8,128)S(1)}, f32[16,8,128]{2,1,0:T(8,128)}, u32[]{:S(2)}) %copy-start.6) | copy-done | bytes 65560
  4.3 0.8 %copy-done.8 = f32[16,8,128]{2,1,0:T(8,128)S(1)} copy-done((f32[16,8,128]{2,1,0:T(8,128)S(1)}, f32[16,8,128]{2,1,0:T(8,128)}, u32[]{:S(2)}) %copy-start.8) | copy-done | bytes 65560
  5.1 0.8 %copy-done.10 = f32[16,8,128]{2,1,0:T(8,128)S(1)} copy-done((f32[16,8,128]{2,1,0:T(8,128)S(1)}, f32[16,8,128]{2,1,0:T(8,128)}, u32[]{:S(2)}) %copy-start.10) | copy-done | bytes 65560
  5.9 0.2 pack.1
  6.1 0.0 copy-start.1
  6.1 3.4 %collective-permute-start = (f32[784,128]{1,0:T(8,128)S(1)}, f32[784,128]{1,0:T(8,128)S(1)}, u32[]{:S(2)}, u32[]{:S(2)}) collective-permute-start(f32[784,128]{1,0:T(8,128)S(1)} %get-tuple-element.12), channel_id=1, source_target_pairs={{4,0},{8,4},{12,8},{16,12},{20,16},{24,20},{28,24},{0,28},{5,1},{9... | collective-permute-start | bytes 1204232 | tf_op jit(solution)/shard_map/ppermute | solution.py:326
  9.5 3.5 %collective-permute-start.1 = (f32[632,128]{1,0:T(8,128)S(1)}, f32[632,128]{1,0:T(8,128)S(1)}, u32[]{:S(2)}, u32[]{:S(2)}) collective-permute-start(f32[632,128]{1,0:T(8,128)S(1)} %get-tuple-element.13), channel_id=1, source_target_pairs={{0,1},{1,2},{2,3},{4,5},{5,6},{6,7},{8,9},{9,10},{10,11},{12,13},{... | collective-permute-start | bytes 970760 | tf_op jit(solution)/shard_map/ppermute | solution.py:327
  13.0 0.0 copy-start.3
  13.0 0.0 copy-start.5
  13.0 0.0 copy-start.7
  13.0 0.0 copy-start.9
  13.1 0.0 copy-start.11
  13.1 1.4 %collective-permute-start.2 = (f32[632,128]{1,0:T(8,128)S(1)}, f32[632,128]{1,0:T(8,128)S(1)}, u32[]{:S(2)}, u32[]{:S(2)}) collective-permute-start(f32[632,128]{1,0:T(8,128)S(1)} %get-tuple-element.14), channel_id=1, source_target_pairs={{1,0},{2,1},{3,2},{5,4},{6,5},{7,6},{9,8},{10,9},{11,10},{13,12},{... | collective-permute-start | bytes 970760 | tf_op jit(solution)/shard_map/ppermute | solution.py:328
  14.5 0.4 collective-permute-done.t_ref
  14.9 4.2 %collective-permute-start.3 = (f32[472,128]{1,0:T(8,128)S(1)}, f32[472,128]{1,0:T(8,128)S(1)}, u32[]{:S(2)}, u32[]{:S(2)}) collective-permute-start(f32[472,128]{1,0:T(8,128)S(1)} %get-tuple-element.20), channel_id=1, source_target_pairs={{0,1},{1,2},{2,3},{4,5},{5,6},{6,7},{8,9},{9,10},{10,11},{12,13},{... | collective-permute-start | bytes 725000 | tf_op jit(solution)/shard_map/ppermute | solution.py:329
  19.1 1.3 %collective-permute-start.4 = (f32[472,128]{1,0:T(8,128)S(1)}, f32[472,128]{1,0:T(8,128)S(1)}, u32[]{:S(2)}, u32[]{:S(2)}) collective-permute-start(f32[472,128]{1,0:T(8,128)S(1)} %get-tuple-element.19), channel_id=1, source_target_pairs={{1,0},{2,1},{3,2},{5,4},{6,5},{7,6},{9,8},{10,9},{11,10},{13,12},{... | collective-permute-start | bytes 725000 | tf_op jit(solution)/shard_map/ppermute | solution.py:330
  20.4 0.0 copy-start.13
  20.4 0.0 copy-start.14
  20.5 0.6 %copy-done.13 = f32[3]{0:T(128)S(1)} copy-done((f32[3]{0:T(128)S(1)}, f32[3]{0:T(128)}, u32[]{:S(2)}) %copy-start.13) | copy-done | bytes 36
  21.1 0.0 copy-done.14
  21.1 0.0 collective-permute-done.1.left_ref
  21.1 2.0 %collective-permute-done.2.right_ref = f32[632,128]{1,0:T(8,128)S(1)} collective-permute-done((f32[632,128]{1,0:T(8,128)S(1)}, f32[632,128]{1,0:T(8,128)S(1)}, u32[]{:S(2)}, u32[]{:S(2)}) %collective-permute-start.2) | collective-permute-done | bytes 323616 | tf_op jit(solution)/shard_map/ppermute | solution.py:328
  23.1 0.0 copy-done.1
  23.1 0.0 copy-done.3
  23.2 9.7 %early.1 = (f32[384,128]{1,0:T(8,128)S(1)}, f32[1792,128]{1,0:T(8,128)S(1)}, f32[2048,128]{1,0:T(8,128)S(1)}, f32[512,128]{1,0:T(8,128)S(1)}) custom-call(f32[3]{0:T(128)S(1)} %broadcast_select_fusion.wrap_ref.scale_ref, f32[1024,128]{1,0:T(8,128)S(1)} %bitcast.8, f32[128,128]{1,0:T(8,128)S(1)} %bitcast.10, s32[8,128]{1,0:T(8,128)S(1)} %copy-done.12, ...), custom_call_target="tpu_custom_call" | custom-call | flops 20000000 | bytes 8000000 | tf_op jit(solution)/shard_map/early/pallas_call | solution.py:332
  32.9 0.0 collective-permute-done.3.left_ref
  32.9 0.0 collective-permute-done.4.right_ref
  33.0 8.0 %late.1 = f32[1024,128]{1,0:T(8,128)} custom-call(f32[3]{0:T(128)S(1)} %broadcast_select_fusion.wrap_ref.scale_ref, f32[384,128]{1,0:T(8,128)S(1)} %get-tuple-element.15.early_ref, f32[1792,128]{1,0:T(8,128)S(1)} %get-tuple-element.16.coef_ref, f32[1280,128]{1,0:T(8,128)S(1)} %slice.9.f_ref, f32[512,128]{1,0:T(8,128)S(1)} %get-tuple-element.18.fown_ref, ...), custom_call_target="tpu_custom_call" | custom-call | flops 20000000 | bytes 8000000 | tf_op jit(solution)/shard_map/late/pallas_call | solution.py:343
  (14 shorter events, 0.1 us)
Async XLA Ops:
  0.0 0.7 %copy-start.12 = (s32[8,128]{1,0:T(8,128)S(1)}, s32[8,128]{1,0:T(8,128)}, u32[]{:S(2)}) copy-start(s32[8,128]{1,0:T(8,128)} %cell_ref.3) | copy-start | bytes 12292
  0.7 1.0 %copy-start = (f32[8,16,8,128]{3,2,1,0:T(8,128)S(1)}, f32[8,16,8,128]{3,2,1,0:T(8,128)}, u32[]{:S(2)}) copy-start(f32[8,16,8,128]{3,2,1,0:T(8,128)} %param.9) | copy-start | bytes 1572868
  1.7 0.8 %copy-start.2 = (f32[8,16,128]{2,1,0:T(8,128)S(1)}, f32[8,16,128]{2,1,0:T(8,128)}, u32[]{:S(2)}) copy-start(f32[8,16,128]{2,1,0:T(8,128)} %param.10) | copy-start | bytes 196612
  2.6 0.8 %copy-start.4 = (f32[16,8,128]{2,1,0:T(8,128)S(1)}, f32[16,8,128]{2,1,0:T(8,128)}, u32[]{:S(2)}) copy-start(f32[16,8,128]{2,1,0:T(8,128)} %param.12) | copy-start | bytes 196612
  3.4 0.8 %copy-start.6 = (f32[16,8,128]{2,1,0:T(8,128)S(1)}, f32[16,8,128]{2,1,0:T(8,128)}, u32[]{:S(2)}) copy-start(f32[16,8,128]{2,1,0:T(8,128)} %param.13) | copy-start | bytes 196612
  4.2 0.8 %copy-start.8 = (f32[16,8,128]{2,1,0:T(8,128)S(1)}, f32[16,8,128]{2,1,0:T(8,128)}, u32[]{:S(2)}) copy-start(f32[16,8,128]{2,1,0:T(8,128)} %param.14) | copy-start | bytes 196612
  5.1 0.8 %copy-start.10 = (f32[16,8,128]{2,1,0:T(8,128)S(1)}, f32[16,8,128]{2,1,0:T(8,128)}, u32[]{:S(2)}) copy-start(f32[16,8,128]{2,1,0:T(8,128)} %param.15) | copy-start | bytes 196612
  6.1 17.0 %copy-start.1 = (f32[8,16,8,128]{3,2,1,0:T(8,128)S(1)}, f32[8,16,8,128]{3,2,1,0:T(8,128)}, u32[]{:S(2)}) copy-start(f32[8,16,8,128]{3,2,1,0:T(8,128)} %param.9) | copy-start | bytes 1572868
  6.1 8.8 %collective-permute-start = (f32[784,128]{1,0:T(8,128)S(1)}, f32[784,128]{1,0:T(8,128)S(1)}, u32[]{:S(2)}, u32[]{:S(2)}) collective-permute-start(f32[784,128]{1,0:T(8,128)S(1)} %get-tuple-element.12), channel_id=1, source_target_pairs={{4,0},{8,4},{12,8},{16,12},{20,16},{24,20},{28,24},{0,28},{5,1},{9... | collective-permute-start | bytes 1204232 | tf_op jit(solution)/shard_map/ppermute | solution.py:326
  9.5 11.6 %collective-permute-start.1 = (f32[632,128]{1,0:T(8,128)S(1)}, f32[632,128]{1,0:T(8,128)S(1)}, u32[]{:S(2)}, u32[]{:S(2)}) collective-permute-start(f32[632,128]{1,0:T(8,128)S(1)} %get-tuple-element.13), channel_id=1, source_target_pairs={{0,1},{1,2},{2,3},{4,5},{5,6},{6,7},{8,9},{9,10},{10,11},{12,13},{... | collective-permute-start | bytes 970760 | tf_op jit(solution)/shard_map/ppermute | solution.py:327
  13.0 10.1 %copy-start.3 = (f32[8,16,128]{2,1,0:T(8,128)S(1)}, f32[8,16,128]{2,1,0:T(8,128)}, u32[]{:S(2)}) copy-start(f32[8,16,128]{2,1,0:T(8,128)} %param.10) | copy-start | bytes 196612
  13.0 10.1 %copy-start.5 = (f32[16,8,128]{2,1,0:T(8,128)S(1)}, f32[16,8,128]{2,1,0:T(8,128)}, u32[]{:S(2)}) copy-start(f32[16,8,128]{2,1,0:T(8,128)} %param.12) | copy-start | bytes 196612
  13.0 10.1 %copy-start.7 = (f32[16,8,128]{2,1,0:T(8,128)S(1)}, f32[16,8,128]{2,1,0:T(8,128)}, u32[]{:S(2)}) copy-start(f32[16,8,128]{2,1,0:T(8,128)} %param.13) | copy-start | bytes 196612
  13.0 10.1 %copy-start.9 = (f32[16,8,128]{2,1,0:T(8,128)S(1)}, f32[16,8,128]{2,1,0:T(8,128)}, u32[]{:S(2)}) copy-start(f32[16,8,128]{2,1,0:T(8,128)} %param.14) | copy-start | bytes 196612
  13.1 10.1 %copy-start.11 = (f32[16,8,128]{2,1,0:T(8,128)S(1)}, f32[16,8,128]{2,1,0:T(8,128)}, u32[]{:S(2)}) copy-start(f32[16,8,128]{2,1,0:T(8,128)} %param.15) | copy-start | bytes 196612
  13.1 10.0 %collective-permute-start.2 = (f32[632,128]{1,0:T(8,128)S(1)}, f32[632,128]{1,0:T(8,128)S(1)}, u32[]{:S(2)}, u32[]{:S(2)}) collective-permute-start(f32[632,128]{1,0:T(8,128)S(1)} %get-tuple-element.14), channel_id=1, source_target_pairs={{1,0},{2,1},{3,2},{5,4},{6,5},{7,6},{9,8},{10,9},{11,10},{13,12},{... | collective-permute-start | bytes 970760 | tf_op jit(solution)/shard_map/ppermute | solution.py:328
  14.9 18.0 %collective-permute-start.3 = (f32[472,128]{1,0:T(8,128)S(1)}, f32[472,128]{1,0:T(8,128)S(1)}, u32[]{:S(2)}, u32[]{:S(2)}) collective-permute-start(f32[472,128]{1,0:T(8,128)S(1)} %get-tuple-element.20), channel_id=1, source_target_pairs={{0,1},{1,2},{2,3},{4,5},{5,6},{6,7},{8,9},{9,10},{10,11},{12,13},{... | collective-permute-start | bytes 725000 | tf_op jit(solution)/shard_map/ppermute | solution.py:329
  19.1 13.8 %collective-permute-start.4 = (f32[472,128]{1,0:T(8,128)S(1)}, f32[472,128]{1,0:T(8,128)S(1)}, u32[]{:S(2)}, u32[]{:S(2)}) collective-permute-start(f32[472,128]{1,0:T(8,128)S(1)} %get-tuple-element.19), channel_id=1, source_target_pairs={{1,0},{2,1},{3,2},{5,4},{6,5},{7,6},{9,8},{10,9},{11,10},{13,12},{... | collective-permute-start | bytes 725000 | tf_op jit(solution)/shard_map/ppermute | solution.py:330
  20.4 0.7 %copy-start.13 = (f32[3]{0:T(128)S(1)}, f32[3]{0:T(128)}, u32[]{:S(2)}) copy-start(f32[3]{0:T(128)} %constant.12.clone) | copy-start | bytes 40
  20.4 0.7 %copy-start.14 = (f32[3]{0:T(128)S(1)}, f32[3]{0:T(128)}, u32[]{:S(2)}) copy-start(f32[3]{0:T(128)} %constant.13.clone) | copy-start | bytes 40

commit v3 on v2

v3 whole, which is shorter than its diff:
```python
import jax
import jax.numpy as jnp
from jax import lax
from jax.experimental import pallas as pl
from jax.experimental.pallas import tpu as pltpu
from jax.sharding import PartitionSpec as P

LEV = 16
TX = 8
NY = 128
STEPS_DEV = 8
SWEEPS = 5
HALO = SWEEPS - 1
NEXT = SWEEPS
FNEXT = SWEEPS - 1
OWN = STEPS_DEV - NEXT
XW = TX + 2 * HALO
ZW = XW + 2
STEP = LEV * TX
PLANE = XW * LEV
BLOCK = 4

circ_alpha = 0.1

TAIL = FNEXT * LEV + 8
T_COL = NEXT * LEV
T_ROWS = 2 * TAIL + TX * T_COL
N_LAM = SWEEPS * OWN * LEV
N_RATE = N_LAM + 4 * HALO * LEV
N_EDGE = N_RATE + LEV
N_INN = N_EDGE + 7 * LEV
N_ROWS = N_INN + 8
M_LAM = SWEEPS * T_COL
M_ROWS = M_LAM + TAIL


def toward(diff, wind):
    return diff + jnp.maximum(-wind, 0.0)


def against(diff, wind):
    return diff + jnp.maximum(wind, 0.0)


def column(ref, base, col, half):
    return ref[pl.ds(base + half * 8 * TX + col, 8, stride=TX), :]


def pack_kernel(
    lam_hbm, inn_hbm, cell_hbm, diff_hbm, wx_hbm, wy_hbm, vm_hbm,
    up_ref, down_ref, t_ref, own_ref,
    lam_ref, inn_ref, cell_ref, diff_ref, wx_ref, wy_ref, vm_ref, sems,
):
    late, soon = pl.ds(NEXT * STEP, OWN * STEP), pl.ds(0, NEXT * STEP)
    pairs = [(lam_hbm.at[late], lam_ref.at[late])]
    pairs += [(diff_hbm, diff_ref), (wx_hbm, wx_ref), (wy_hbm, wy_ref), (vm_hbm, vm_ref)]
    pairs += [(inn_hbm, inn_ref), (cell_hbm, cell_ref), (lam_hbm.at[soon], lam_ref.at[soon])]
    copies = [pltpu.make_async_copy(source, target, sems.at[index]) for index, (source, target) in enumerate(pairs)]
    for copy in copies:
        copy.start()
    for copy in copies[:-1]:
        copy.wait()
    cells = cell_ref[...].astype(jnp.float32)
    rates = (diff_ref, wx_ref, wy_ref, vm_ref)
    for half in range(2):
        for col in range(TX):
            for slot in range(OWN):
                value = column(lam_ref, (NEXT + slot) * STEP, col, half)
                row = slot * LEV + 8 * half
                own_ref[col * OWN * LEV + row : col * OWN * LEV + row + 8, :] = value
                if col >= TX - SWEEPS:
                    start = (col - TX + SWEEPS) * OWN * LEV + row
                    up_ref[start : start + 8, :] = value
                if col < SWEEPS:
                    start = col * OWN * LEV + row
                    down_ref[start : start + 8, :] = value
        for index, ref in enumerate(rates):
            for place in range(HALO):
                row = N_LAM + (index * HALO + place) * LEV + 8 * half
                up_ref[row : row + 8, :] = column(ref, 0, TX - HALO + place, half)
                down_ref[row : row + 8, :] = column(ref, 0, place, half)
        row = N_RATE + 8 * half
        col = TX - SWEEPS
        up_ref[row : row + 8, :] = toward(column(diff_ref, 0, col, half), column(wx_ref, 0, col, half))
        col = SWEEPS - 1
        down_ref[row : row + 8, :] = against(column(diff_ref, 0, col, half), column(wx_ref, 0, col, half))
    for ref in (up_ref, down_ref):
        ref[N_EDGE:N_INN, :] = inn_ref[LEV : 8 * LEV, :]
        ref[N_INN:N_ROWS, :] = cells
    for base in (0, TAIL + TX * T_COL):
        t_ref[base : base + FNEXT * LEV, :] = inn_ref[0 : FNEXT * LEV, :]
        t_ref[base + FNEXT * LEV : base + TAIL, :] = cells
    copies[-1].wait()
    for half in range(2):
        for col in range(TX):
            for slot in range(NEXT):
                row = TAIL + col * T_COL + slot * LEV + 8 * half
                t_ref[row : row + 8, :] = column(lam_ref, slot * STEP, col, half)


def place_forcing(value, cell, columns, row_y):
    cell_x = lax.shift_right_logical(cell, 7).astype(jnp.float32)
    cell_y = (cell & (NY - 1)).astype(jnp.float32)
    high = value.astype(jnp.bfloat16)
    rest = value - high.astype(jnp.float32)
    mid = rest.astype(jnp.bfloat16)
    low = (rest - mid.astype(jnp.float32)).astype(jnp.bfloat16)
    spread_x = jnp.broadcast_to(cell_x, (LEV, NY)).astype(jnp.bfloat16)
    spread_y = jnp.broadcast_to(cell_y, (LEV, NY)).astype(jnp.bfloat16)
    zero = jnp.zeros((LEV, NY), jnp.bfloat16)
    one = jnp.ones((LEV, NY), jnp.bfloat16)
    hot_y = jnp.concatenate(
        [jnp.where(row_y[LEV * part : LEV * part + LEV] == spread_y, one, zero) for part in range(NY // LEV)], axis=0
    )
    blocks = []
    for x in range(*columns):
        hot = spread_x == jnp.full((LEV, NY), x, jnp.bfloat16)
        blocks.append(jnp.concatenate([jnp.where(hot, part, zero) for part in (high, mid, low)], axis=1))
    return lax.dot_general(
        jnp.concatenate(blocks, axis=0),
        jnp.concatenate([hot_y, hot_y, hot_y], axis=1),
        (((1,), (1,)), ((), ())),
        preferred_element_type=jnp.float32,
    )


def level_rows():
    return lax.broadcasted_iota(jnp.int32, (NY, NY), 0).astype(jnp.float32).astype(jnp.bfloat16)


LEFT = (TX - HALO, TX)
RIGHT = (0, HALO)


def sweeps(chains, first_chain, za_ref, zb_ref, coef_ref, own_rows, side_rows, store):
    width = chains * LEV
    buffers = (za_ref, zb_ref)
    for sweep in range(SWEEPS):
        source, target = buffers[sweep % 2], buffers[(sweep + 1) % 2]

        def one_column(at, rows, place, source=source, target=target, sweep=sweep):
            base = at * width
            plane = (at - 1) * LEV
            if not isinstance(at, int):
                base, plane = pl.multiple_of(base, LEV), pl.multiple_of(plane, LEV)
            for half in range(2):
                coef = [coef_ref[pl.ds(kind * PLANE + plane + 8 * half, 8), :] for kind in range(7)]
                for chain in range(chains):
                    row = base + chain * LEV + 8 * half
                    centre = source[pl.ds(row, 8), :]
                    step = first_chain + chain + HALO - sweep
                    ref, start = rows(step, place)
                    west_east = coef[1] * source[pl.ds(row - width, 8), :] + coef[2] * source[pl.ds(row + width, 8), :]
                    along = coef[3] * pltpu.roll(centre, 1, 1) + coef[4] * pltpu.roll(centre, NY - 1, 1)
                    down_up = coef[5] * source[pl.ds(row - 1, 8), :] + coef[6] * source[pl.ds(row + 1, 8), :]
                    total = ref[pl.ds(start + 8 * half, 8), :] + coef[0] * centre
                    total = ((total + west_east) + down_up) + along
                    if sweep < SWEEPS - 1:
                        target[pl.ds(row, 8), :] = total
                    else:
                        store(chain, at, half, total)

        def block(index, carry, one_column=one_column):
            for offset in range(BLOCK):
                place = index * BLOCK + offset
                one_column(SWEEPS + place, own_rows, place)
            return carry

        lax.fori_loop(0, TX // BLOCK, block, 0)
        for offset in range(HALO - sweep):
            one_column(SWEEPS - 1 - offset, side_rows, HALO - 1 - offset)
            one_column(SWEEPS + TX + offset, side_rows, HALO + offset)


def factors(last_ref):
    last = last_ref[0] != 0
    return jnp.where(last, circ_alpha, 1.0), jnp.where(last, 0.0, 1.0), jnp.where(last, circ_alpha, 0.0)


def own_kernel(last_ref, inn_ref, cell_ref, t_ref, f_ref):
    wrap, _, extra = factors(last_ref)
    row_y = level_rows()

    def own_steps(index, carry):
        for offset in range(4):
            step = index * 4 + offset
            value = inn_ref[pl.ds(pl.multiple_of(step * LEV, LEV), LEV), :]
            placed = place_forcing(value, cell_ref[pl.ds(step, 1), :], (0, TX), row_y)
            f_ref[pl.ds(pl.multiple_of(step * STEP, STEP), STEP), :] = placed
        return carry

    lax.fori_loop(0, STEPS_DEV // 4, own_steps, 0)
    for step in range(FNEXT):
        value = t_ref[step * LEV : step * LEV + LEV, :] * wrap
        cell = t_ref[FNEXT * LEV + step : FNEXT * LEV + step + 1, :].astype(jnp.int32)
        start = (STEPS_DEV + step) * STEP
        placed = place_forcing(value, cell, (0, TX), row_y)
        if step == 0:
            for col in range(TX):
                state = t_ref[TAIL + col * T_COL : TAIL + col * T_COL + LEV, :]
                f_ref[start + col * LEV : start + col * LEV + LEV, :] = placed[col * LEV : col * LEV + LEV, :] - state * extra
        else:
            f_ref[start : start + STEP, :] = placed


def early_kernel(
    f_ref, own_ref, diff_ref, wx_ref, wy_ref, vm_ref, left_ref, right_ref,
    out_ref, coef_ref, side_ref,
    za_ref, zb_ref,
):
    lane = lax.broadcasted_iota(jnp.int32, (8, NY), 1)
    sub = lax.broadcasted_iota(jnp.int32, (8, NY), 0)
    for at in range(XW):
        mixings = []

        def put(kind, at_row, value):
            coef_ref[kind * PLANE + at_row : kind * PLANE + at_row + 8, :] = value

        for half in range(2):
            fields = []
            for index, ref in enumerate((diff_ref, wx_ref, wy_ref, vm_ref)):
                if HALO <= at < HALO + TX:
                    fields.append(column(ref, 0, at - HALO, half))
                else:
                    side, place = (left_ref, at) if at < HALO else (right_ref, at - HALO - TX)
                    row = N_LAM + (index * HALO + place) * LEV + 8 * half
                    fields.append(side[row : row + 8, :])
            diff, wind_x, wind_y, mixing = fields
            e_rate, w_rate = toward(diff, wind_x), against(diff, wind_x)
            n_rate, s_rate = toward(diff, wind_y), against(diff, wind_y)
            mixings.append(mixing)
            row = at * LEV + 8 * half
            put(0, row, 1.0 - (e_rate + w_rate + n_rate + s_rate + mixing + mixing))
            if at < XW - 1:
                put(1, row + LEV, e_rate)
            if at > 0:
                put(2, row - LEV, w_rate)
            put(3, row, jnp.where(lane == 0, 0.0, pltpu.roll(n_rate, 1, 1)))
            put(4, row, jnp.where(lane == NY - 1, 0.0, pltpu.roll(s_rate, NY - 1, 1)))
        row = at * LEV
        down_low, down_high = pltpu.roll(mixings[0], 1, 0), pltpu.roll(mixings[1], 1, 0)
        put(5, row, jnp.where(sub == 0, 0.0, down_low))
        put(5, row + 8, jnp.where(sub == 0, down_low, down_high))
        up_low, up_high = pltpu.roll(mixings[0], 7, 0), pltpu.roll(mixings[1], 7, 0)
        put(6, row, jnp.where(sub == 7, up_high, up_low))
        put(6, row + 8, jnp.where(sub == 7, 0.0, up_high))
    coef_ref[PLANE : PLANE + LEV, :] = left_ref[N_RATE:N_EDGE, :]
    coef_ref[3 * PLANE - LEV : 3 * PLANE, :] = right_ref[N_RATE:N_EDGE, :]

    row_y = level_rows()

    def side_step(step, carry):
        for index, (ref, columns) in enumerate(((left_ref, LEFT), (right_ref, RIGHT))):
            value = ref[pl.ds(pl.multiple_of(N_EDGE + (step - 1) * LEV, LEV), LEV), :]
            cell = ref[pl.ds(N_INN + step, 1), :].astype(jnp.int32)
            placed = place_forcing(value, cell, columns, row_y)
            side_ref[pl.ds(pl.multiple_of(step * STEP + index * HALO * LEV, LEV), HALO * LEV), :] = placed
        return carry

    def side_steps(index, carry):
        for offset in range(2):
            side_step(2 + index * 2 + offset, 0)
        return carry

    side_step(1, 0)
    lax.fori_loop(0, 3, side_steps, 0)

    block = SWEEPS * OWN * LEV
    inner = TX * OWN * LEV
    za_ref[0:block, :] = left_ref[0:block, :]
    za_ref[block : block + inner, :] = own_ref[...]
    za_ref[block + inner : 2 * block + inner, :] = right_ref[0:block, :]

    def rows_of_ref(ref):
        return lambda step, place: (ref, step * STEP + place * LEV)

    def store(chain, at, half, total):
        out_ref[pl.ds(chain * STEP + half * 8 * TX + at - SWEEPS, 8, stride=TX), :] = total

    sweeps(OWN, 0, za_ref, zb_ref, coef_ref, rows_of_ref(f_ref), rows_of_ref(side_ref), store)


def late_kernel(
    last_ref, early_ref, coef_ref, f_ref, side_ref, t_ref, left_ref, right_ref,
    out_ref, za_ref, zb_ref, fnext_ref,
):
    wrap, first, extra = factors(last_ref)
    out_ref[0 : OWN * STEP, :] = early_ref[...]
    for at in range(ZW):
        if at < SWEEPS:
            ref, base = left_ref, at * T_COL
        elif at < SWEEPS + TX:
            ref, base = t_ref, TAIL + (at - SWEEPS) * T_COL
        else:
            ref, base = right_ref, TAIL + (at - SWEEPS - TX) * T_COL
        row = at * T_COL
        za_ref[row : row + LEV, :] = ref[base : base + LEV, :] * first
        za_ref[row + LEV : row + T_COL, :] = ref[base + LEV : base + T_COL, :] * wrap

    row_y = level_rows()

    def side_steps(pair, carry):
        for offset in range(2):
            step = pair * 2 + offset
            for index, (ref, base, columns) in enumerate(((left_ref, M_LAM, LEFT), (right_ref, 0, RIGHT))):
                value = ref[pl.ds(pl.multiple_of(base + step * LEV, 8), LEV), :] * wrap
                cell = ref[pl.ds(base + FNEXT * LEV + step, 1), :].astype(jnp.int32)
                placed = place_forcing(value, cell, columns, row_y)
                fnext_ref[pl.ds(pl.multiple_of(step * STEP + index * HALO * LEV, LEV), HALO * LEV), :] = placed
        return carry

    lax.fori_loop(0, FNEXT // 2, side_steps, 0)

    @pl.when(extra != 0.0)
    def _():
        for place in range(2 * HALO):
            ref, base = (left_ref, (place + 1) * T_COL) if place < HALO else (right_ref, TAIL + (place - HALO) * T_COL)
            rows = slice(place * LEV, place * LEV + LEV)
            fnext_ref[rows, :] = fnext_ref[rows, :] - ref[base : base + LEV, :] * extra

    def own_rows(step, place):
        return f_ref, step * STEP + place * LEV

    def side_rows(step, place):
        ref, base = (side_ref, step) if step < STEPS_DEV else (fnext_ref, step - STEPS_DEV)
        return ref, base * STEP + place * LEV

    def store(chain, at, half, total):
        out_ref[pl.ds((OWN + chain) * STEP + half * 8 * TX + at - SWEEPS, 8, stride=TX), :] = total

    sweeps(NEXT, OWN, za_ref, zb_ref, coef_ref, own_rows, side_rows, store)


def vmem(count):
    return [pl.BlockSpec(memory_space=pltpu.VMEM)] * count


def rows_of(count):
    return jax.ShapeDtypeStruct((count, NY), jnp.float32)


def scratch(count):
    return pltpu.VMEM((count, NY), jnp.float32)


SMEM_SPEC = pl.BlockSpec(memory_space=pltpu.SMEM)


def body(adjoint_iterate, innovations, station_cells, diffusivity, wind_x, wind_y, vertical_mixing):
    time_parts = lax.axis_size("tm")
    tiles = lax.axis_size("space")
    lam = adjoint_iterate.reshape(STEPS_DEV * STEP, NY)
    inn = innovations.reshape(STEPS_DEV * LEV, NY)
    fields = [field.reshape(STEP, NY) for field in (diffusivity, wind_x, wind_y, vertical_mixing)]
    last = (lax.axis_index("tm") == time_parts - 1).astype(jnp.int32).reshape(1)

    ahead = [((i + 1) % time_parts, i) for i in range(time_parts)]
    upward = [(i, i + 1) for i in range(tiles - 1)]
    downward = [(i + 1, i) for i in range(tiles - 1)]

    arguments = (lam, inn, station_cells, *fields)
    pay_up, pay_down, pay_t, own = pl.pallas_call(
        pack_kernel,
        out_shape=(rows_of(N_ROWS), rows_of(N_ROWS), rows_of(T_ROWS), rows_of(OWN * STEP)),
        in_specs=[pl.BlockSpec(memory_space=pltpu.HBM)] * 7,
        out_specs=tuple(vmem(4)),
        scratch_shapes=[pltpu.VMEM(value.shape, value.dtype) for value in arguments] + [pltpu.SemaphoreType.DMA((8,))],
        compiler_params=pltpu.CompilerParams(vmem_limit_bytes=8 << 20),
        name="pack",
    )(*[pltpu.with_memory_space_constraint(value, pltpu.HBM) for value in arguments])
    got_t = lax.ppermute(pay_t, "tm", ahead)
    left_one = lax.ppermute(pay_up, "space", upward)
    right_one = lax.ppermute(pay_down, "space", downward)
    left_two = lax.ppermute(got_t[T_ROWS - M_ROWS :], "space", upward)
    right_two = lax.ppermute(got_t[:M_ROWS], "space", downward)

    forcing = pl.pallas_call(
        own_kernel,
        out_shape=rows_of((STEPS_DEV + FNEXT) * STEP),
        in_specs=[SMEM_SPEC] + vmem(3),
        out_specs=vmem(1)[0],
        compiler_params=pltpu.CompilerParams(vmem_limit_bytes=16 << 20),
        cost_estimate=pl.CostEstimate(flops=5_000_000, bytes_accessed=4_000_000, transcendentals=0),
        name="own",
    )(last, inn, station_cells, got_t)
    out_early, coef, side = pl.pallas_call(
        early_kernel,
        out_shape=(rows_of(OWN * STEP), rows_of(7 * PLANE), rows_of(STEPS_DEV * STEP)),
        in_specs=vmem(8),
        out_specs=tuple(vmem(3)),
        scratch_shapes=[scratch(ZW * OWN * LEV), scratch(ZW * OWN * LEV)],
        compiler_params=pltpu.CompilerParams(vmem_limit_bytes=16 << 20),
        cost_estimate=pl.CostEstimate(flops=20_000_000, bytes_accessed=8_000_000, transcendentals=0),
        name="early",
    )(forcing, own, *fields, left_one, right_one)
    out = pl.pallas_call(
        late_kernel,
        out_shape=rows_of(STEPS_DEV * STEP),
        in_specs=[SMEM_SPEC] + vmem(7),
        out_specs=vmem(1)[0],
        scratch_shapes=[scratch(ZW * T_COL), scratch(ZW * T_COL), scratch(FNEXT * STEP)],
        compiler_params=pltpu.CompilerParams(vmem_limit_bytes=16 << 20),
        cost_estimate=pl.CostEstimate(flops=20_000_000, bytes_accessed=8_000_000, transcendentals=0),
        name="late",
    )(last, out_early, coef, forcing, side, got_t, left_two, right_two)
    return out.reshape(STEPS_DEV, LEV, TX, NY)


def solution(mesh):
    in_specs = (
        P("tm", None, "space", None),
        P("tm", None, "space"),
        P("tm", "space"),
        P(None, "space", None),
        P(None, "space", None),
        P(None, "space", None),
        P(None, "space", None),
    )
    out_specs = P("tm", None, "space", None)
    return jax.shard_map(body, mesh=mesh, in_specs=in_specs, out_specs=out_specs, check_vma=False)
```

time: 41.5 us -> 27.6 us (0.67)
  Pallas kernels: 17.8 us -> 9.21 us
  local copies, waits for them, and re-layouts: 6.69 us -> 0.72 us
  waiting for transfers between devices: 2.4 us -> 3.51 us
    pallas_call x1, Pallas kernels: 9.72 us -> 2.97 us  [body(): pl.pallas_call(early_kernel, out_shape=(rows_of(OWN * STEP), rows_of(7 *...]
    unnamed x30 -> x12, local copies, waits for them, and re-layouts: 6.62 us -> 0.69 us
    pallas_call x1, Pallas kernels: 7.97 us -> 3.93 us  [body(): pl.pallas_call(late_kernel, out_shape=rows_of(STEPS_DEV * STEP), in_specs...]
    ppermute x1, waiting for transfers between devices: 0.01 us -> 2.07 us  [body(): right_two = lax.ppermute(got_t[:M_ROWS], 'space', downward)]
    pallas_call x1, Pallas kernels: 0.16 us -> 1.38 us  [body(): pl.pallas_call(pack_kernel, out_shape=(rows_of(N_ROWS), rows_of(N_ROWS),...]
    ppermute x1, waiting for transfers between devices: 2 us -> 0.99 us  [body(): right_one = lax.ppermute(pay_down, 'space', downward)]
    pallas_call x0 -> x1, Pallas kernels: none -> 0.93 us  [body(): pl.pallas_call(own_kernel, out_shape=rows_of((STEPS_DEV + FNEXT) * STEP),...]
  transfers between devices with their start and end apart: 5 -> 5, of which waited for: 2 -> 3; matrix products, arithmetic and copies ran while one was open for 0% -> 0% of each run, Pallas kernels for 24% -> 14%
where the time goes in v3:
time: 27.6 us; the launch traced here: 27.3 us
  starting transfers between devices  13.8 us (50%)
  Pallas kernels  9.21 us (33%)
  waiting for transfers between devices  3.51 us (13%)
  local copies, waits for them, and re-layouts  0.72 us (3%)
    ppermute x1, starting transfers between devices, body(): left_two = lax.ppermute(got_t[T_ROWS - M_ROWS:], 'space', upward)  4.13 us
    pallas_call x1, Pallas kernels, body(): pl.pallas_call(late_kernel, out_shape=rows_of(STEPS_DEV * STEP), in_specs...  3.93 us
    ppermute x1, starting transfers between devices, body(): left_one = lax.ppermute(pay_up, 'space', upward)  3.49 us
    ppermute x1, starting transfers between devices, body(): got_t = lax.ppermute(pay_t, 'tm', ahead)  3.41 us
    pallas_call x1, Pallas kernels, body(): pl.pallas_call(early_kernel, out_shape=(rows_of(OWN * STEP), rows_of(7 *...  2.97 us
    ppermute x1, waiting for transfers between devices, body(): right_two = lax.ppermute(got_t[:M_ROWS], 'space', downward)  2.07 us
    ppermute x1, starting transfers between devices, body(): right_one = lax.ppermute(pay_down, 'space', downward)  1.42 us
    pallas_call x1, Pallas kernels, body(): pl.pallas_call(pack_kernel, out_shape=(rows_of(N_ROWS), rows_of(N_ROWS),...  1.38 us
  transfers between devices with their start and end apart: 5, of which 3 were waited for; matrix products, arithmetic and copies ran while one was open for 0% of the time, Pallas kernels for 14%

profile of v3, /device:TPU:0, one launch (start us, length us, event | category | flops | bytes accessed | tf_op | source)
XLA Modules:
  0.0 27.3 jit_solution(7434186081203757952)
XLA Ops:
  0.0 1.4 %pack.1 = (f32[632,128]{1,0:T(8,128)S(1)}, f32[632,128]{1,0:T(8,128)S(1)}, f32[784,128]{1,0:T(8,128)S(1)}, f32[384,128]{1,0:T(8,128)S(1)}) custom-call(f32[1024,128]{1,0:T(8,128)} %bitcast.18, f32[128,128]{1,0:T(8,128)} %bitcast.8, s32[8,128]{1,0:T(8,128)} %cell_ref.1, f32[128,128]{1,0:T(8,128)} %bitcast.10, f32[128,128]{1,0:T(8,128)} %bitcast.12, ...), custom_call_target="tpu_custom_call" | custom-call | tf_op jit(solution)/shard_map/pack/pallas_call | solution.py:362
  1.4 3.4 %collective-permute-start = (f32[784,128]{1,0:T(8,128)S(1)}, f32[784,128]{1,0:T(8,128)S(1)}, u32[]{:S(2)}, u32[]{:S(2)}) collective-permute-start(f32[784,128]{1,0:T(8,128)S(1)} %get-tuple-element.12), channel_id=1, source_target_pairs={{4,0},{8,4},{12,8},{16,12},{20,16},{24,20},{28,24},{0,28},{5,1},{9... | collective-permute-start | bytes 1204232 | tf_op jit(solution)/shard_map/ppermute | solution.py:371
  4.8 3.5 %collective-permute-start.1 = (f32[632,128]{1,0:T(8,128)S(1)}, f32[632,128]{1,0:T(8,128)S(1)}, u32[]{:S(2)}, u32[]{:S(2)}) collective-permute-start(f32[632,128]{1,0:T(8,128)S(1)} %get-tuple-element.14), channel_id=1, source_target_pairs={{0,1},{1,2},{2,3},{4,5},{5,6},{6,7},{8,9},{9,10},{10,11},{12,13},{... | collective-permute-start | bytes 970760 | tf_op jit(solution)/shard_map/ppermute | solution.py:372
  8.3 0.0 copy-start
  8.3 1.4 %collective-permute-start.2 = (f32[632,128]{1,0:T(8,128)S(1)}, f32[632,128]{1,0:T(8,128)S(1)}, u32[]{:S(2)}, u32[]{:S(2)}) collective-permute-start(f32[632,128]{1,0:T(8,128)S(1)} %get-tuple-element.15), channel_id=1, source_target_pairs={{1,0},{2,1},{3,2},{5,4},{6,5},{7,6},{9,8},{10,9},{11,10},{13,12},{... | collective-permute-start | bytes 970760 | tf_op jit(solution)/shard_map/ppermute | solution.py:373
  9.7 0.4 %collective-permute-done.t_ref = f32[784,128]{1,0:T(8,128)S(1)} collective-permute-done((f32[784,128]{1,0:T(8,128)S(1)}, f32[784,128]{1,0:T(8,128)S(1)}, u32[]{:S(2)}, u32[]{:S(2)}) %collective-permute-start) | collective-permute-done | bytes 401440 | tf_op jit(solution)/shard_map/ppermute | solution.py:371
  10.2 4.1 %collective-permute-start.3 = (f32[472,128]{1,0:T(8,128)S(1)}, f32[472,128]{1,0:T(8,128)S(1)}, u32[]{:S(2)}, u32[]{:S(2)}) collective-permute-start(f32[472,128]{1,0:T(8,128)S(1)} %get-tuple-element.20), channel_id=1, source_target_pairs={{0,1},{1,2},{2,3},{4,5},{5,6},{6,7},{8,9},{9,10},{10,11},{12,13},{... | collective-permute-start | bytes 725000 | tf_op jit(solution)/shard_map/ppermute | solution.py:374
  14.4 1.3 %collective-permute-start.4 = (f32[472,128]{1,0:T(8,128)S(1)}, f32[472,128]{1,0:T(8,128)S(1)}, u32[]{:S(2)}, u32[]{:S(2)}) collective-permute-start(f32[472,128]{1,0:T(8,128)S(1)} %get-tuple-element.19), channel_id=1, source_target_pairs={{1,0},{2,1},{3,2},{5,4},{6,5},{7,6},{9,8},{10,9},{11,10},{13,12},{... | collective-permute-start | bytes 725000 | tf_op jit(solution)/shard_map/ppermute | solution.py:375
  15.7 0.0 copy-start.5
  15.7 0.0 copy-done
  15.7 0.7 %copy-done.5 = s32[8,128]{1,0:T(8,128)S(1)} copy-done((s32[8,128]{1,0:T(8,128)S(1)}, s32[8,128]{1,0:T(8,128)}, u32[]{:S(2)}) %copy-start.5) | copy-done | bytes 4120
  16.4 0.0 copy-start.1
  16.4 0.0 copy-start.2
  16.4 0.0 copy-start.3
  16.4 0.0 copy-start.4
  16.4 0.9 %own.1.f_ref = f32[1536,128]{1,0:T(8,128)S(1)} custom-call(s32[1]{0:T(128)} %bitcast.last_ref, f32[128,128]{1,0:T(8,128)S(1)} %bitcast.9, s32[8,128]{1,0:T(8,128)S(1)} %copy-done.5, f32[784,128]{1,0:T(8,128)S(1)} %collective-permute-done.t_ref), custom_call_target="tpu_custom_call" | custom-call | flops 5000000 | bytes 4000000 | tf_op jit(solution)/shard_map/own/pallas_call | solution.py:377
  17.3 0.0 collective-permute-done.1.left_ref
  17.3 1.0 %collective-permute-done.2.right_ref = f32[632,128]{1,0:T(8,128)S(1)} collective-permute-done((f32[632,128]{1,0:T(8,128)S(1)}, f32[632,128]{1,0:T(8,128)S(1)}, u32[]{:S(2)}, u32[]{:S(2)}) %collective-permute-start.2) | collective-permute-done | bytes 323616 | tf_op jit(solution)/shard_map/ppermute | solution.py:373
  18.3 0.0 copy-done.1
  18.3 0.0 copy-done.2
  18.3 0.0 copy-done.3
  18.3 0.0 copy-done.4
  18.3 3.0 %early.1 = (f32[384,128]{1,0:T(8,128)S(1)}, f32[1792,128]{1,0:T(8,128)S(1)}, f32[1024,128]{1,0:T(8,128)S(1)}) custom-call(f32[1536,128]{1,0:T(8,128)S(1)} %own.1.f_ref, f32[384,128]{1,0:T(8,128)S(1)} %get-tuple-element.13.own_ref, f32[128,128]{1,0:T(8,128)S(1)} %bitcast.11, f32[128,128]{1,0:T(8,128)S(1)} %bitcast.13, f32[128,128]{1,0:T(8,128)S(1)} %bitcast.15, ...), custom_call_target="tpu_custom_call" | custom-call | flops 20000000 | bytes 8000000 | tf_op jit(solution)/shard_map/early/pallas_call | solution.py:386
  21.3 0.0 collective-permute-done.3.left_ref
  21.3 2.1 %collective-permute-done.4.right_ref = f32[472,128]{1,0:T(8,128)S(1)} collective-permute-done((f32[472,128]{1,0:T(8,128)S(1)}, f32[472,128]{1,0:T(8,128)S(1)}, u32[]{:S(2)}, u32[]{:S(2)}) %collective-permute-start.4) | collective-permute-done | bytes 241696 | tf_op jit(solution)/shard_map/ppermute | solution.py:375
  23.4 3.9 %late.1 = f32[1024,128]{1,0:T(8,128)} custom-call(s32[1]{0:T(128)} %bitcast.last_ref, f32[384,128]{1,0:T(8,128)S(1)} %get-tuple-element.16.early_ref, f32[1792,128]{1,0:T(8,128)S(1)} %get-tuple-element.17.coef_ref, f32[1536,128]{1,0:T(8,128)S(1)} %own.1.f_ref, f32[1024,128]{1,0:T(8,128)S(1)} %get-tuple-element.18.side_ref, ...), custom_call_target="tpu_custom_call" | custom-call | flops 20000000 | bytes 8000000 | tf_op jit(solution)/shard_map/late/pallas_call | solution.py:396
  (1 shorter events, 0.0 us)
Async XLA Ops:
  1.4 8.8 %collective-permute-start = (f32[784,128]{1,0:T(8,128)S(1)}, f32[784,128]{1,0:T(8,128)S(1)}, u32[]{:S(2)}, u32[]{:S(2)}) collective-permute-start(f32[784,128]{1,0:T(8,128)S(1)} %get-tuple-element.12), channel_id=1, source_target_pairs={{4,0},{8,4},{12,8},{16,12},{20,16},{24,20},{28,24},{0,28},{5,1},{9... | collective-permute-start | bytes 1204232 | tf_op jit(solution)/shard_map/ppermute | solution.py:371
  4.8 12.5 %collective-permute-start.1 = (f32[632,128]{1,0:T(8,128)S(1)}, f32[632,128]{1,0:T(8,128)S(1)}, u32[]{:S(2)}, u32[]{:S(2)}) collective-permute-start(f32[632,128]{1,0:T(8,128)S(1)} %get-tuple-element.14), channel_id=1, source_target_pairs={{0,1},{1,2},{2,3},{4,5},{5,6},{6,7},{8,9},{9,10},{10,11},{12,13},{... | collective-permute-start | bytes 970760 | tf_op jit(solution)/shard_map/ppermute | solution.py:372
  8.3 7.4 %copy-start = (f32[8,16,128]{2,1,0:T(8,128)S(1)}, f32[8,16,128]{2,1,0:T(8,128)}, u32[]{:S(2)}) copy-start(f32[8,16,128]{2,1,0:T(8,128)} %param.8) | copy-start | bytes 196612
  8.3 10.0 %collective-permute-start.2 = (f32[632,128]{1,0:T(8,128)S(1)}, f32[632,128]{1,0:T(8,128)S(1)}, u32[]{:S(2)}, u32[]{:S(2)}) collective-permute-start(f32[632,128]{1,0:T(8,128)S(1)} %get-tuple-element.15), channel_id=1, source_target_pairs={{1,0},{2,1},{3,2},{5,4},{6,5},{7,6},{9,8},{10,9},{11,10},{13,12},{... | collective-permute-start | bytes 970760 | tf_op jit(solution)/shard_map/ppermute | solution.py:373
  10.2 11.1 %collective-permute-start.3 = (f32[472,128]{1,0:T(8,128)S(1)}, f32[472,128]{1,0:T(8,128)S(1)}, u32[]{:S(2)}, u32[]{:S(2)}) collective-permute-start(f32[472,128]{1,0:T(8,128)S(1)} %get-tuple-element.20), channel_id=1, source_target_pairs={{0,1},{1,2},{2,3},{4,5},{5,6},{6,7},{8,9},{9,10},{10,11},{12,13},{... | collective-permute-start | bytes 725000 | tf_op jit(solution)/shard_map/ppermute | solution.py:374
  14.4 9.0 %collective-permute-start.4 = (f32[472,128]{1,0:T(8,128)S(1)}, f32[472,128]{1,0:T(8,128)S(1)}, u32[]{:S(2)}, u32[]{:S(2)}) collective-permute-start(f32[472,128]{1,0:T(8,128)S(1)} %get-tuple-element.19), channel_id=1, source_target_pairs={{1,0},{2,1},{3,2},{5,4},{6,5},{7,6},{9,8},{10,9},{11,10},{13,12},{... | collective-permute-start | bytes 725000 | tf_op jit(solution)/shard_map/ppermute | solution.py:375
  15.7 0.7 %copy-start.5 = (s32[8,128]{1,0:T(8,128)S(1)}, s32[8,128]{1,0:T(8,128)}, u32[]{:S(2)}) copy-start(s32[8,128]{1,0:T(8,128)} %cell_ref.1) | copy-start | bytes 12292
  16.4 1.9 %copy-start.1 = (f32[16,8,128]{2,1,0:T(8,128)S(1)}, f32[16,8,128]{2,1,0:T(8,128)}, u32[]{:S(2)}) copy-start(f32[16,8,128]{2,1,0:T(8,128)} %param.10) | copy-start | bytes 196612
  16.4 1.9 %copy-start.2 = (f32[16,8,128]{2,1,0:T(8,128)S(1)}, f32[16,8,128]{2,1,0:T(8,128)}, u32[]{:S(2)}) copy-start(f32[16,8,128]{2,1,0:T(8,128)} %param.11) | copy-start | bytes 196612
  16.4 1.9 %copy-start.3 = (f32[16,8,128]{2,1,0:T(8,128)S(1)}, f32[16,8,128]{2,1,0:T(8,128)}, u32[]{:S(2)}) copy-start(f32[16,8,128]{2,1,0:T(8,128)} %param.12) | copy-start | bytes 196612
  16.4 1.9 %copy-start.4 = (f32[16,8,128]{2,1,0:T(8,128)S(1)}, f32[16,8,128]{2,1,0:T(8,128)}, u32[]{:S(2)}) copy-start(f32[16,8,128]{2,1,0:T(8,128)} %param.13) | copy-start | bytes 196612

commit v4 on v3

--- a/solution.py
+++ b/solution.py
@@ -30,6 +30,10 @@
 N_EDGE = N_RATE + LEV
 N_INN = N_EDGE + 7 * LEV
 N_ROWS = N_INN + 8
+K_INN = OWN * STEP
+K_CELL = K_INN + STEPS_DEV * LEV
+K_RATE = K_CELL + 8
+K_ROWS = K_RATE + 4 * STEP
 M_LAM = SWEEPS * T_COL
 M_ROWS = M_LAM + TAIL
 
@@ -46,49 +50,57 @@
     return ref[pl.ds(base + half * 8 * TX + col, 8, stride=TX), :]
 
 
+def flags_of(code_ref):
+    return [lax.shift_right_logical(code_ref[0], bit) & 1 for bit in range(4)]
+
+
 def pack_kernel(
-    lam_hbm, inn_hbm, cell_hbm, diff_hbm, wx_hbm, wy_hbm, vm_hbm,
-    up_ref, down_ref, t_ref, own_ref,
-    lam_ref, inn_ref, cell_ref, diff_ref, wx_ref, wy_ref, vm_ref, sems,
+    code_ref, lam_hbm, inn_hbm, cell_hbm, diff_hbm, wx_hbm, wy_hbm, vm_hbm,
+    here_ref, back_ref, t_ref, keep_ref,
+    lam_ref, cell_ref, sems,
 ):
     late, soon = pl.ds(NEXT * STEP, OWN * STEP), pl.ds(0, NEXT * STEP)
     pairs = [(lam_hbm.at[late], lam_ref.at[late])]
-    pairs += [(diff_hbm, diff_ref), (wx_hbm, wx_ref), (wy_hbm, wy_ref), (vm_hbm, vm_ref)]
-    pairs += [(inn_hbm, inn_ref), (cell_hbm, cell_ref), (lam_hbm.at[soon], lam_ref.at[soon])]
+    pairs += [
+        (rate, keep_ref.at[pl.ds(K_RATE + index * STEP, STEP)])
+        for index, rate in enumerate((diff_hbm, wx_hbm, wy_hbm, vm_hbm))
+    ]
+    pairs += [(inn_hbm, keep_ref.at[pl.ds(K_INN, STEPS_DEV * LEV)]), (cell_hbm, cell_ref)]
+    pairs += [(lam_hbm.at[soon], lam_ref.at[soon])]
     copies = [pltpu.make_async_copy(source, target, sems.at[index]) for index, (source, target) in enumerate(pairs)]
     for copy in copies:
         copy.start()
+    odd = flags_of(code_ref)[1]
     for copy in copies[:-1]:
         copy.wait()
     cells = cell_ref[...].astype(jnp.float32)
-    rates = (diff_ref, wx_ref, wy_ref, vm_ref)
+    keep_ref[K_CELL:K_RATE, :] = cells
+    far = TX - SWEEPS
+    for ref, first in ((here_ref, far * (1 - odd)), (back_ref, far * odd)):
+        rate_first = jnp.where(first == 0, 0, TX - HALO)
+        for half in range(2):
+            for place in range(SWEEPS):
+                for slot in range(OWN):
+                    row = (place * OWN + slot) * LEV + 8 * half
+                    ref[row : row + 8, :] = column(lam_ref, (NEXT + slot) * STEP, first + place, half)
+            for index in range(4):
+                for place in range(HALO):
+                    row = N_LAM + (index * HALO + place) * LEV + 8 * half
+                    ref[row : row + 8, :] = column(keep_ref, K_RATE + index * STEP, rate_first + place, half)
+            row = N_RATE + 8 * half
+            leaving = toward(column(keep_ref, K_RATE, far, half), column(keep_ref, K_RATE + STEP, far, half))
+            place = SWEEPS - 1
+            entering = against(column(keep_ref, K_RATE, place, half), column(keep_ref, K_RATE + STEP, place, half))
+            ref[row : row + 8, :] = jnp.where(first == 0, entering, leaving)
+        ref[N_EDGE:N_INN, :] = keep_ref[K_INN + LEV : K_INN + 8 * LEV, :]
+        ref[N_INN:N_ROWS, :] = cells
     for half in range(2):
         for col in range(TX):
             for slot in range(OWN):
-                value = column(lam_ref, (NEXT + slot) * STEP, col, half)
-                row = slot * LEV + 8 * half
-                own_ref[col * OWN * LEV + row : col * OWN * LEV + row + 8, :] = value
-                if col >= TX - SWEEPS:
-                    start = (col - TX + SWEEPS) * OWN * LEV + row
-                    up_ref[start : start + 8, :] = value
-                if col < SWEEPS:
-                    start = col * OWN * LEV + row
-                    down_ref[start : start + 8, :] = value
-        for index, ref in enumerate(rates):
-            for place in range(HALO):
-                row = N_LAM + (index * HALO + place) * LEV + 8 * half
-                up_ref[row : row + 8, :] = column(ref, 0, TX - HALO + place, half)
-                down_ref[row : row + 8, :] = column(ref, 0, place, half)
-        row = N_RATE + 8 * half
-        col = TX - SWEEPS
-        up_ref[row : row + 8, :] = toward(column(diff_ref, 0, col, half), column(wx_ref, 0, col, half))
-        col = SWEEPS - 1
-        down_ref[row : row + 8, :] = against(column(diff_ref, 0, col, half), column(wx_ref, 0, col, half))
-    for ref in (up_ref, down_ref):
-        ref[N_EDGE:N_INN, :] = inn_ref[LEV : 8 * LEV, :]
-        ref[N_INN:N_ROWS, :] = cells
+                row = (col * OWN + slot) * LEV + 8 * half
+                keep_ref[row : row + 8, :] = column(lam_ref, (NEXT + slot) * STEP, col, half)
     for base in (0, TAIL + TX * T_COL):
-        t_ref[base : base + FNEXT * LEV, :] = inn_ref[0 : FNEXT * LEV, :]
+        t_ref[base : base + FNEXT * LEV, :] = keep_ref[K_INN : K_INN + FNEXT * LEV, :]
         t_ref[base + FNEXT * LEV : base + TAIL, :] = cells
     copies[-1].wait()
     for half in range(2):
@@ -96,6 +108,15 @@
             for slot in range(NEXT):
                 row = TAIL + col * T_COL + slot * LEV + 8 * half
                 t_ref[row : row + 8, :] = column(lam_ref, slot * STEP, col, half)
+
+
+def by_side(odd, here_ref, back_ref, left_ref, right_ref):
+    for parity, sources in enumerate(((here_ref, back_ref), (back_ref, here_ref))):
+
+        @pl.when(odd == parity)
+        def _(sources=sources):
+            for source, target in zip(sources, (left_ref, right_ref)):
+                target[...] = source[...]
 
 
 def place_forcing(value, cell, columns, row_y):
@@ -172,20 +193,21 @@
             one_column(SWEEPS + TX + offset, side_rows, HALO + offset)
 
 
-def factors(last_ref):
-    last = last_ref[0] != 0
+def factors(last):
+    last = last != 0
     return jnp.where(last, circ_alpha, 1.0), jnp.where(last, 0.0, 1.0), jnp.where(last, circ_alpha, 0.0)
 
 
-def own_kernel(last_ref, inn_ref, cell_ref, t_ref, f_ref):
-    wrap, _, extra = factors(last_ref)
+def own_kernel(code_ref, keep_ref, t_ref, f_ref):
+    wrap, _, extra = factors(flags_of(code_ref)[0])
     row_y = level_rows()
 
     def own_steps(index, carry):
         for offset in range(4):
             step = index * 4 + offset
-            value = inn_ref[pl.ds(pl.multiple_of(step * LEV, LEV), LEV), :]
-            placed = place_forcing(value, cell_ref[pl.ds(step, 1), :], (0, TX), row_y)
+            value = keep_ref[pl.ds(pl.multiple_of(K_INN + step * LEV, LEV), LEV), :]
+            cell = keep_ref[pl.ds(K_CELL + step, 1), :].astype(jnp.int32)
+            placed = place_forcing(value, cell, (0, TX), row_y)
             f_ref[pl.ds(pl.multiple_of(step * STEP, STEP), STEP), :] = placed
         return carry
 
@@ -204,10 +226,14 @@
 
 
 def early_kernel(
-    f_ref, own_ref, diff_ref, wx_ref, wy_ref, vm_ref, left_ref, right_ref,
+    code_ref, f_ref, keep_ref, here_ref, back_ref,
     out_ref, coef_ref, side_ref,
-    za_ref, zb_ref,
+    za_ref, zb_ref, left_ref, right_ref,
 ):
+    _, odd, first_tile, last_tile = flags_of(code_ref)
+    by_side(odd, here_ref, back_ref, left_ref, right_ref)
+    open_left = jnp.where(first_tile != 0, 0.0, 1.0)
+    open_right = jnp.where(last_tile != 0, 0.0, 1.0)
     lane = lax.broadcasted_iota(jnp.int32, (8, NY), 1)
     sub = lax.broadcasted_iota(jnp.int32, (8, NY), 0)
     for at in range(XW):
@@ -218,9 +244,9 @@
 
         for half in range(2):
             fields = []
-            for index, ref in enumerate((diff_ref, wx_ref, wy_ref, vm_ref)):
+            for index in range(4):
                 if HALO <= at < HALO + TX:
-                    fields.append(column(ref, 0, at - HALO, half))
+                    fields.append(column(keep_ref, K_RATE + index * STEP, at - HALO, half))
                 else:
                     side, place = (left_ref, at) if at < HALO else (right_ref, at - HALO - TX)
                     row = N_LAM + (index * HALO + place) * LEV + 8 * half
@@ -232,9 +258,9 @@
             row = at * LEV + 8 * half
             put(0, row, 1.0 - (e_rate + w_rate + n_rate + s_rate + mixing + mixing))
             if at < XW - 1:
-                put(1, row + LEV, e_rate)
+                put(1, row + LEV, e_rate * open_left if at == HALO - 1 else e_rate)
             if at > 0:
-                put(2, row - LEV, w_rate)
+                put(2, row - LEV, w_rate * open_right if at == HALO + TX else w_rate)
             put(3, row, jnp.where(lane == 0, 0.0, pltpu.roll(n_rate, 1, 1)))
             put(4, row, jnp.where(lane == NY - 1, 0.0, pltpu.roll(s_rate, NY - 1, 1)))
         row = at * LEV
@@ -268,7 +294,7 @@
     block = SWEEPS * OWN * LEV
     inner = TX * OWN * LEV
     za_ref[0:block, :] = left_ref[0:block, :]
-    za_ref[block : block + inner, :] = own_ref[...]
+    za_ref[block : block + inner, :] = keep_ref[0:inner, :]
     za_ref[block + inner : 2 * block + inner, :] = right_ref[0:block, :]
 
     def rows_of_ref(ref):
@@ -281,10 +307,12 @@
 
 
 def late_kernel(
-    last_ref, early_ref, coef_ref, f_ref, side_ref, t_ref, left_ref, right_ref,
-    out_ref, za_ref, zb_ref, fnext_ref,
+    code_ref, early_ref, coef_ref, f_ref, side_ref, t_ref, here_ref, back_ref,
+    out_ref, za_ref, zb_ref, fnext_ref, left_ref, right_ref,
 ):
-    wrap, first, extra = factors(last_ref)
+    last, odd = flags_of(code_ref)[:2]
+    wrap, first, extra = factors(last)
+    by_side(odd, here_ref, back_ref, left_ref, right_ref)
     out_ref[0 : OWN * STEP, :] = early_ref[...]
     for at in range(ZW):
         if at < SWEEPS:
@@ -352,57 +380,76 @@
     lam = adjoint_iterate.reshape(STEPS_DEV * STEP, NY)
     inn = innovations.reshape(STEPS_DEV * LEV, NY)
     fields = [field.reshape(STEP, NY) for field in (diffusivity, wind_x, wind_y, vertical_mixing)]
-    last = (lax.axis_index("tm") == time_parts - 1).astype(jnp.int32).reshape(1)
+    time_rank, tile = lax.axis_index("tm"), lax.axis_index("space")
+    odd = time_rank & 1
+    code = (time_rank == time_parts - 1) + 2 * odd + 4 * (tile == 0) + 8 * (tile == tiles - 1)
+    code = code.astype(jnp.int32).reshape(1)
 
     ahead = [((i + 1) % time_parts, i) for i in range(time_parts)]
-    upward = [(i, i + 1) for i in range(tiles - 1)]
-    downward = [(i + 1, i) for i in range(tiles - 1)]
+
+    def neighbours(flip):
+        pairs = []
+        for part in range(time_parts):
+            step = 1 if part % 2 == flip else -1
+            for place in range(tiles):
+                inside = 0 <= place + step < tiles
+                target = part * tiles + place + step if inside else (part ^ 1) * tiles + place
+                pairs.append((part * tiles + place, target))
+        return pairs
+
+    there, again = neighbours(0), neighbours(1)
+    both = ("tm", "space")
 
     arguments = (lam, inn, station_cells, *fields)
-    pay_up, pay_down, pay_t, own = pl.pallas_call(
+    pay_here, pay_back, pay_t, keep = pl.pallas_call(
         pack_kernel,
-        out_shape=(rows_of(N_ROWS), rows_of(N_ROWS), rows_of(T_ROWS), rows_of(OWN * STEP)),
-        in_specs=[pl.BlockSpec(memory_space=pltpu.HBM)] * 7,
+        out_shape=(rows_of(N_ROWS), rows_of(N_ROWS), rows_of(T_ROWS), rows_of(K_ROWS)),
+        in_specs=[SMEM_SPEC] + [pl.BlockSpec(memory_space=pltpu.HBM)] * 7,
         out_specs=tuple(vmem(4)),
-        scratch_shapes=[pltpu.VMEM(value.shape, value.dtype) for value in arguments] + [pltpu.SemaphoreType.DMA((8,))],
+        scratch_shapes=[
+            scratch(STEPS_DEV * STEP),
+            pltpu.VMEM(station_cells.shape, station_cells.dtype),
+            pltpu.SemaphoreType.DMA((8,)),
+        ],
         compiler_params=pltpu.CompilerParams(vmem_limit_bytes=8 << 20),
         name="pack",
-    )(*[pltpu.with_memory_space_constraint(value, pltpu.HBM) for value in arguments])
+    )(code, *[pltpu.with_memory_space_constraint(value, pltpu.HBM) for value in arguments])
     got_t = lax.ppermute(pay_t, "tm", ahead)
-    left_one = lax.ppermute(pay_up, "space", upward)
-    right_one = lax.ppermute(pay_down, "space", downward)
-    left_two = lax.ppermute(got_t[T_ROWS - M_ROWS :], "space", upward)
-    right_two = lax.ppermute(got_t[:M_ROWS], "space", downward)
+    here_one = lax.ppermute(pay_here, both, there)
+    back_one = lax.ppermute(pay_back, both, again)
+    start = (T_ROWS - M_ROWS) * (1 - odd)
+    here_two = lax.ppermute(lax.dynamic_slice_in_dim(got_t, start, M_ROWS), both, there)
+    back_two = lax.ppermute(lax.dynamic_slice_in_dim(got_t, T_ROWS - M_ROWS - start, M_ROWS), both, again)
 
     forcing = pl.pallas_call(
         own_kernel,
         out_shape=rows_of((STEPS_DEV + FNEXT) * STEP),
-        in_specs=[SMEM_SPEC] + vmem(3),
+        in_specs=[SMEM_SPEC] + vmem(2),
         out_specs=vmem(1)[0],
         compiler_params=pltpu.CompilerParams(vmem_limit_bytes=16 << 20),
         cost_estimate=pl.CostEstimate(flops=5_000_000, bytes_accessed=4_000_000, transcendentals=0),
         name="own",
-    )(last, inn, station_cells, got_t)
+    )(code, keep, got_t)
     out_early, coef, side = pl.pallas_call(
         early_kernel,
         out_shape=(rows_of(OWN * STEP), rows_of(7 * PLANE), rows_of(STEPS_DEV * STEP)),
-        in_specs=vmem(8),
+        in_specs=[SMEM_SPEC] + vmem(4),
         out_specs=tuple(vmem(3)),
-        scratch_shapes=[scratch(ZW * OWN * LEV), scratch(ZW * OWN * LEV)],
+        scratch_shapes=[scratch(ZW * OWN * LEV), scratch(ZW * OWN * LEV), scratch(N_ROWS), scratch(N_ROWS)],
         compiler_params=pltpu.CompilerParams(vmem_limit_bytes=16 << 20),
         cost_estimate=pl.CostEstimate(flops=20_000_000, bytes_accessed=8_000_000, transcendentals=0),
         name="early",
-    )(forcing, own, *fields, left_one, right_one)
+    )(code, forcing, keep, here_one, back_one)
     out = pl.pallas_call(
         late_kernel,
         out_shape=rows_of(STEPS_DEV * STEP),
         in_specs=[SMEM_SPEC] + vmem(7),
         out_specs=vmem(1)[0],
-        scratch_shapes=[scratch(ZW * T_COL), scratch(ZW * T_COL), scratch(FNEXT * STEP)],
+        scratch_shapes=[scratch(ZW * T_COL), scratch(ZW * T_COL), scratch(FNEXT * STEP), scratch(M_ROWS), scratch(M_ROWS)],
         compiler_params=pltpu.CompilerParams(vmem_limit_bytes=16 << 20),
         cost_estimate=pl.CostEstimate(flops=20_000_000, bytes_accessed=8_000_000, transcendentals=0),
         name="late",
-    )(last, out_early, coef, forcing, side, got_t, left_two, right_two)
+    )(code, out_early, coef, forcing, side, got_t, here_two, back_two)
     return out.reshape(STEPS_DEV, LEV, TX, NY)
 
 

time: 27.6 us -> 22.6 us (0.82)
  starting transfers between devices: 13.8 us -> 6.59 us
  waiting for transfers between devices: 3.51 us -> 6.67 us
  local copies, waits for them, and re-layouts: 0.72 us -> 0.03 us
    ppermute x4, starting transfers between devices: 10.3 us -> 3.17 us  [the longest x1 1.59 us: body(): lax.ppermute(lax.dynamic_slice_in_dim(got_t, start, M_ROWS), both, there)]
    ppermute x1, waiting for transfers between devices: 0.44 us -> 3.8 us  [body(): got_t = lax.ppermute(pay_t, 'tm', ahead)]
    unnamed x12 -> x0, local copies, waits for them, and re-layouts: 0.69 us -> none
  transfers between devices with their start and end apart: 5 -> 5, of which waited for: 3 -> 5; matrix products, arithmetic and copies ran while one was open for 0% -> 0% of each run, Pallas kernels for 14% -> 17%
where the time goes in v4:
time: 22.6 us; the launch traced here: 22.4 us
  Pallas kernels  9.13 us (40%)
  waiting for transfers between devices  6.67 us (30%)
  starting transfers between devices  6.59 us (29%)
    pallas_call x1, Pallas kernels, body(): pl.pallas_call(late_kernel, out_shape=rows_of(STEPS_DEV * STEP), in_specs...  3.86 us
    ppermute x1, waiting for transfers between devices, body(): got_t = lax.ppermute(pay_t, 'tm', ahead)  3.8 us
    ppermute x1, starting transfers between devices, body(): got_t = lax.ppermute(pay_t, 'tm', ahead)  3.41 us
    pallas_call x1, Pallas kernels, body(): pl.pallas_call(early_kernel, out_shape=(rows_of(OWN * STEP), rows_of(7 *...  2.95 us
    ppermute x1, starting transfers between devices, body(): lax.ppermute(lax.dynamic_slice_in_dim(got_t, start, M_ROWS), both, there)  1.59 us
    ppermute x1, starting transfers between devices, body(): here_one = lax.ppermute(pay_here, both, there)  1.58 us
    pallas_call x1, Pallas kernels, body(): pl.pallas_call(pack_kernel, out_shape=(rows_of(N_ROWS), rows_of(N_ROWS),...  1.38 us
    ppermute x1, waiting for transfers between devices, body(): lax.ppermute(lax.dynamic_slice_in_dim(got_t, start, M_ROWS), both, there)  1.08 us
  transfers between devices with their start and end apart: 5, of which 5 were waited for; matrix products, arithmetic and copies ran while one was open for 0% of the time, Pallas kernels for 17%

profile of v4, /device:TPU:0, one launch (start us, length us, event | category | flops | bytes accessed | tf_op | source)
XLA Modules:
  0.0 22.4 jit_solution(11703958850100952290)
XLA Ops:
  0.0 1.4 %pack.1 = (f32[632,128]{1,0:T(8,128)S(1)}, f32[632,128]{1,0:T(8,128)S(1)}, f32[784,128]{1,0:T(8,128)S(1)}, f32[1032,128]{1,0:T(8,128)S(1)}) custom-call(s32[1]{0:T(128)} %bitcast.code_ref, f32[1024,128]{1,0:T(8,128)} %bitcast.8, f32[128,128]{1,0:T(8,128)} %bitcast.9, s32[8,128]{1,0:T(8,128)} %cell_hbm.1, f32[128,128]{1,0:T(8,128)} %bitcast.10, ...), custom_call_target="tpu_custom_call" | custom-call | tf_op jit(solution)/shard_map/pack/pallas_call | solution.py:404
  1.4 3.4 %collective-permute-start = (f32[784,128]{1,0:T(8,128)S(1)}, f32[784,128]{1,0:T(8,128)S(1)}, u32[]{:S(2)}, u32[]{:S(2)}) collective-permute-start(f32[784,128]{1,0:T(8,128)S(1)} %get-tuple-element.13), channel_id=1, source_target_pairs={{4,0},{8,4},{12,8},{16,12},{20,16},{24,20},{28,24},{0,28},{5,1},{9... | collective-permute-start | bytes 1204232 | tf_op jit(solution)/shard_map/ppermute | solution.py:417
  4.8 1.6 %collective-permute-start.1 = (f32[632,128]{1,0:T(8,128)S(1)}, f32[632,128]{1,0:T(8,128)S(1)}, u32[]{:S(2)}, u32[]{:S(2)}) collective-permute-start(f32[632,128]{1,0:T(8,128)S(1)} %get-tuple-element.14), channel_id=1, source_target_pairs={{0,1},{1,2},{2,3},{3,7},{4,0},{5,4},{6,5},{7,6},{8,9},{9,10},{10,1... | collective-permute-start | bytes 970760 | tf_op jit(solution)/shard_map/ppermute | solution.py:418
  6.4 0.0 collective-permute-start.2
  6.4 3.8 %collective-permute-done.t_ref = f32[784,128]{1,0:T(8,128)S(1)} collective-permute-done((f32[784,128]{1,0:T(8,128)S(1)}, f32[784,128]{1,0:T(8,128)S(1)}, u32[]{:S(2)}, u32[]{:S(2)}) %collective-permute-start) | collective-permute-done | bytes 401440 | tf_op jit(solution)/shard_map/ppermute | solution.py:417
  10.2 1.6 %collective-permute-start.3 = (f32[472,128]{1,0:T(8,128)S(1)}, f32[472,128]{1,0:T(8,128)S(1)}, u32[]{:S(2)}, u32[]{:S(2)}) collective-permute-start(f32[472,128]{1,0:T(8,128)S(1)} %get-tuple-element.20), channel_id=1, source_target_pairs={{0,1},{1,2},{2,3},{3,7},{4,0},{5,4},{6,5},{7,6},{8,9},{9,10},{10,1... | collective-permute-start | bytes 725000 | tf_op jit(solution)/shard_map/ppermute | solution.py:421
  11.8 0.0 collective-permute-start.4
  11.8 0.9 %own.1.f_ref = f32[1536,128]{1,0:T(8,128)S(1)} custom-call(s32[1]{0:T(128)} %bitcast.code_ref, f32[1032,128]{1,0:T(8,128)S(1)} %get-tuple-element.12.keep_ref, f32[784,128]{1,0:T(8,128)S(1)} %collective-permute-done.t_ref), custom_call_target="tpu_custom_call" | custom-call | flops 5000000 | bytes 4000000 | tf_op jit(solution)/shard_map/own/pallas_call | solution.py:424
  12.8 0.2 collective-permute-done.1.here_ref
  13.0 0.8 %collective-permute-done.2.back_ref = f32[632,128]{1,0:T(8,128)S(1)} collective-permute-done((f32[632,128]{1,0:T(8,128)S(1)}, f32[632,128]{1,0:T(8,128)S(1)}, u32[]{:S(2)}, u32[]{:S(2)}) %collective-permute-start.2) | collective-permute-done | bytes 323616 | tf_op jit(solution)/shard_map/ppermute | solution.py:419
  13.8 2.9 %early.1 = (f32[384,128]{1,0:T(8,128)S(1)}, f32[1792,128]{1,0:T(8,128)S(1)}, f32[1024,128]{1,0:T(8,128)S(1)}) custom-call(s32[1]{0:T(128)} %bitcast.code_ref, f32[1536,128]{1,0:T(8,128)S(1)} %own.1.f_ref, f32[1032,128]{1,0:T(8,128)S(1)} %get-tuple-element.12.keep_ref, f32[632,128]{1,0:T(8,128)S(1)} %collective-permute-done.1.here_ref, ...), custom_call_target="tpu_custom_call" | custom-call | flops 20000000 | bytes 8000000 | tf_op jit(solution)/shard_map/early/pallas_call | solution.py:433
  16.7 1.1 %collective-permute-done.3.here_ref = f32[472,128]{1,0:T(8,128)S(1)} collective-permute-done((f32[472,128]{1,0:T(8,128)S(1)}, f32[472,128]{1,0:T(8,128)S(1)}, u32[]{:S(2)}, u32[]{:S(2)}) %collective-permute-start.3) | collective-permute-done | bytes 241696 | tf_op jit(solution)/shard_map/ppermute | solution.py:421
  17.8 0.8 %collective-permute-done.4.back_ref = f32[472,128]{1,0:T(8,128)S(1)} collective-permute-done((f32[472,128]{1,0:T(8,128)S(1)}, f32[472,128]{1,0:T(8,128)S(1)}, u32[]{:S(2)}, u32[]{:S(2)}) %collective-permute-start.4) | collective-permute-done | bytes 241696 | tf_op jit(solution)/shard_map/ppermute | solution.py:422
  18.6 3.9 %late.1 = f32[1024,128]{1,0:T(8,128)} custom-call(s32[1]{0:T(128)} %bitcast.code_ref, f32[384,128]{1,0:T(8,128)S(1)} %get-tuple-element.16.early_ref, f32[1792,128]{1,0:T(8,128)S(1)} %get-tuple-element.17.coef_ref, f32[1536,128]{1,0:T(8,128)S(1)} %own.1.f_ref, f32[1024,128]{1,0:T(8,128)S(1)} %get-tuple-element.18.side_ref, ...), custom_call_target="tpu_custom_call" | custom-call | flops 20000000 | bytes 8000000 | tf_op jit(solution)/shard_map/late/pallas_call | solution.py:443
  (1 shorter events, 0.0 us)
Async XLA Ops:
  1.4 8.8 %collective-permute-start = (f32[784,128]{1,0:T(8,128)S(1)}, f32[784,128]{1,0:T(8,128)S(1)}, u32[]{:S(2)}, u32[]{:S(2)}) collective-permute-start(f32[784,128]{1,0:T(8,128)S(1)} %get-tuple-element.13), channel_id=1, source_target_pairs={{4,0},{8,4},{12,8},{16,12},{20,16},{24,20},{28,24},{0,28},{5,1},{9... | collective-permute-start | bytes 1204232 | tf_op jit(solution)/shard_map/ppermute | solution.py:417
  4.8 8.2 %collective-permute-start.1 = (f32[632,128]{1,0:T(8,128)S(1)}, f32[632,128]{1,0:T(8,128)S(1)}, u32[]{:S(2)}, u32[]{:S(2)}) collective-permute-start(f32[632,128]{1,0:T(8,128)S(1)} %get-tuple-element.14), channel_id=1, source_target_pairs={{0,1},{1,2},{2,3},{3,7},{4,0},{5,4},{6,5},{7,6},{8,9},{9,10},{10,1... | collective-permute-start | bytes 970760 | tf_op jit(solution)/shard_map/ppermute | solution.py:418
  6.4 7.4 %collective-permute-start.2 = (f32[632,128]{1,0:T(8,128)S(1)}, f32[632,128]{1,0:T(8,128)S(1)}, u32[]{:S(2)}, u32[]{:S(2)}) collective-permute-start(f32[632,128]{1,0:T(8,128)S(1)} %get-tuple-element.15), channel_id=1, source_target_pairs={{0,4},{1,0},{2,1},{3,2},{4,5},{5,6},{6,7},{7,3},{8,12},{9,8},{10,9... | collective-permute-start | bytes 970760 | tf_op jit(solution)/shard_map/ppermute | solution.py:419
  10.2 7.6 %collective-permute-start.3 = (f32[472,128]{1,0:T(8,128)S(1)}, f32[472,128]{1,0:T(8,128)S(1)}, u32[]{:S(2)}, u32[]{:S(2)}) collective-permute-start(f32[472,128]{1,0:T(8,128)S(1)} %get-tuple-element.20), channel_id=1, source_target_pairs={{0,1},{1,2},{2,3},{3,7},{4,0},{5,4},{6,5},{7,6},{8,9},{9,10},{10,1... | collective-permute-start | bytes 725000 | tf_op jit(solution)/shard_map/ppermute | solution.py:421
  11.8 6.8 %collective-permute-start.4 = (f32[472,128]{1,0:T(8,128)S(1)}, f32[472,128]{1,0:T(8,128)S(1)}, u32[]{:S(2)}, u32[]{:S(2)}) collective-permute-start(f32[472,128]{1,0:T(8,128)S(1)} %get-tuple-element.19), channel_id=1, source_target_pairs={{0,4},{1,0},{2,1},{3,2},{4,5},{5,6},{6,7},{7,3},{8,12},{9,8},{10,9... | collective-permute-start | bytes 725000 | tf_op jit(solution)/shard_map/ppermute | solution.py:422

commit v5 on v4

v5 whole, which is shorter than its diff:
```python
import jax
import jax.numpy as jnp
from jax import lax
from jax.experimental import pallas as pl
from jax.experimental.pallas import tpu as pltpu
from jax.sharding import PartitionSpec as P


LEV = 16
TX = 8
NY = 128
STEPS_DEV = 8
SWEEPS = 5
HALO = SWEEPS - 1
NEXT = SWEEPS
FNEXT = SWEEPS - 1
OWN = STEPS_DEV - NEXT
XW = TX + 2 * HALO
ZW = XW + 2
STEP = LEV * TX
PLANE = XW * LEV

circ_alpha = 0.1

PARTS = ((0, 2, 0, 1), (2, 3, 1, 3))
TAILS = tuple(part[3] * LEV + 8 for part in PARTS)
T_BASE = (0, 2 * TAILS[0] + TX * PARTS[0][1] * LEV)
T_ROWS = T_BASE[1] + 2 * TAILS[1] + TX * PARTS[1][1] * LEV
N_INN = SWEEPS * OWN * LEV
N_CELL = N_INN + 7 * LEV
N_RATE = N_CELL + 8
N_EDGE = N_RATE + 4 * HALO * LEV
N_ROWS = N_EDGE + LEV
K_INN = OWN * STEP
K_CELL = K_INN + STEPS_DEV * LEV
K_RATE = K_CELL + 8
K_ROWS = K_RATE + 4 * STEP


def part_rows(part):
    return SWEEPS * PARTS[part][1] * LEV + TAILS[part]


def toward(diff, wind):
    return diff + jnp.maximum(-wind, 0.0)


def against(diff, wind):
    return diff + jnp.maximum(wind, 0.0)


def column(ref, base, col, half):
    return ref[pl.ds(base + half * 8 * TX + col, 8, stride=TX), :]


def flags_of(code_ref):
    return [lax.shift_right_logical(code_ref[0], bit) & 1 for bit in range(4)]


def pack_kernel(
    code_ref, lam_hbm, inn_hbm, cell_hbm, diff_hbm, wx_hbm, wy_hbm, vm_hbm,
    here_ref, back_ref, t_ref, keep_ref,
    lam_ref, cell_ref, sems,
):
    late, soon = pl.ds(NEXT * STEP, OWN * STEP), pl.ds(0, NEXT * STEP)
    pairs = [(lam_hbm.at[late], lam_ref.at[late])]
    pairs += [
        (rate, keep_ref.at[pl.ds(K_RATE + index * STEP, STEP)])
        for index, rate in enumerate((diff_hbm, wx_hbm, wy_hbm, vm_hbm))
    ]
    pairs += [(inn_hbm, keep_ref.at[pl.ds(K_INN, STEPS_DEV * LEV)]), (cell_hbm, cell_ref)]
    pairs += [(lam_hbm.at[soon], lam_ref.at[soon])]
    copies = [pltpu.make_async_copy(source, target, sems.at[index]) for index, (source, target) in enumerate(pairs)]
    for copy in copies:
        copy.start()
    odd = flags_of(code_ref)[1]
    far = TX - SWEEPS
    sides = ((here_ref, far * (1 - odd)), (back_ref, far * odd))
    copies[0].wait()
    for half in range(2):
        for col in range(TX):
            for slot in range(OWN):
                row = (col * OWN + slot) * LEV + 8 * half
                keep_ref[row : row + 8, :] = column(lam_ref, (NEXT + slot) * STEP, col, half)
    for ref, first in sides:
        start = pl.multiple_of(first * (OWN * LEV), LEV)
        ref[0:N_INN, :] = keep_ref[pl.ds(start, N_INN), :]
    for copy in copies[1:5]:
        copy.wait()
    first = sides[0][1]
    rate_first = (TX - HALO) * (1 - odd)
    for half in range(2):
        for index in range(4):
            for place in range(HALO):
                row = N_RATE + (index * HALO + place) * LEV + 8 * half
                here_ref[row : row + 8, :] = column(keep_ref, K_RATE + index * STEP, rate_first + place, half)
        leaving = toward(column(keep_ref, K_RATE, far, half), column(keep_ref, K_RATE + STEP, far, half))
        place = SWEEPS - 1
        entering = against(column(keep_ref, K_RATE, place, half), column(keep_ref, K_RATE + STEP, place, half))
        here_ref[N_EDGE + 8 * half : N_EDGE + 8 * half + 8, :] = jnp.where(odd == 0, leaving, entering)
    for copy in copies[5:7]:
        copy.wait()
    cells = cell_ref[...].astype(jnp.float32)
    keep_ref[K_CELL:K_RATE, :] = cells
    for ref in (here_ref, back_ref):
        ref[N_INN:N_CELL, :] = keep_ref[K_INN + LEV : K_INN + 8 * LEV, :]
        ref[N_CELL:N_RATE, :] = cells
    for (_, states, first_inn, inns), tail, base in zip(PARTS, TAILS, T_BASE):
        for start in (base, base + tail + TX * states * LEV):
            row = K_INN + first_inn * LEV
            t_ref[start : start + inns * LEV, :] = keep_ref[row : row + inns * LEV, :]
            t_ref[start + inns * LEV : start + tail, :] = cells
    copies[7].wait()
    for (first_state, states, _, _), tail, base in zip(PARTS, TAILS, T_BASE):
        for half in range(2):
            for col in range(TX):
                for slot in range(states):
                    row = base + tail + (col * states + slot) * LEV + 8 * half
                    t_ref[row : row + 8, :] = column(lam_ref, (first_state + slot) * STEP, col, half)


def by_side(odd, work, here, back):
    pl.when(odd == 0)(lambda: work(here, back))
    pl.when(odd != 0)(lambda: work(back, here))


def place_forcing(value, cell, columns, row_y):
    cell_x = lax.shift_right_logical(cell, 7).astype(jnp.float32)
    cell_y = (cell & (NY - 1)).astype(jnp.float32)
    high = value.astype(jnp.bfloat16)
    rest = value - high.astype(jnp.float32)
    mid = rest.astype(jnp.bfloat16)
    low = (rest - mid.astype(jnp.float32)).astype(jnp.bfloat16)
    spread_x = jnp.broadcast_to(cell_x, (LEV, NY)).astype(jnp.bfloat16)
    spread_y = jnp.broadcast_to(cell_y, (LEV, NY)).astype(jnp.bfloat16)
    zero = jnp.zeros((LEV, NY), jnp.bfloat16)
    one = jnp.ones((LEV, NY), jnp.bfloat16)
    hot_y = jnp.concatenate(
        [jnp.where(row_y[LEV * part : LEV * part + LEV] == spread_y, one, zero) for part in range(NY // LEV)], axis=0
    )
    blocks = []
    for x in range(*columns):
        hot = spread_x == jnp.full((LEV, NY), x, jnp.bfloat16)
        blocks.append(jnp.concatenate([jnp.where(hot, part, zero) for part in (high, mid, low)], axis=1))
    return lax.dot_general(
        jnp.concatenate(blocks, axis=0),
        jnp.concatenate([hot_y, hot_y, hot_y], axis=1),
        (((1,), (1,)), ((), ())),
        preferred_element_type=jnp.float32,
    )


def level_rows():
    return lax.broadcasted_iota(jnp.int32, (NY, NY), 0).astype(jnp.float32).astype(jnp.bfloat16)


LEFT = (TX - HALO, TX)
RIGHT = (0, HALO)


def sweeps(chains, first_chain, za_ref, zb_ref, coef_ref, own_rows, side_rows, store):
    width = chains * LEV
    buffers = (za_ref, zb_ref)
    for sweep in range(SWEEPS):
        source, target = buffers[sweep % 2], buffers[(sweep + 1) % 2]

        def one_column(at, rows, place, source=source, target=target, sweep=sweep):
            base = at * width
            plane = (at - 1) * LEV
            for half in range(2):
                coef = [coef_ref[pl.ds(kind * PLANE + plane + 8 * half, 8), :] for kind in range(7)]
                for chain in range(chains):
                    row = base + chain * LEV + 8 * half
                    centre = source[pl.ds(row, 8), :]
                    step = first_chain + chain + HALO - sweep
                    ref, start = rows(step, place)
                    west_east = coef[1] * source[pl.ds(row - width, 8), :] + coef[2] * source[pl.ds(row + width, 8), :]
                    along = coef[3] * pltpu.roll(centre, 1, 1) + coef[4] * pltpu.roll(centre, NY - 1, 1)
                    down_up = coef[5] * source[pl.ds(row - 1, 8), :] + coef[6] * source[pl.ds(row + 1, 8), :]
                    total = ref[pl.ds(start + 8 * half, 8), :] + coef[0] * centre
                    total = ((total + west_east) + down_up) + along
                    if sweep < SWEEPS - 1:
                        target[pl.ds(row, 8), :] = total
                    else:
                        store(chain, at, half, total)

        for place in range(TX):
            one_column(SWEEPS + place, own_rows, place)
        for offset in range(HALO - sweep):
            one_column(SWEEPS - 1 - offset, side_rows, HALO - 1 - offset)
            one_column(SWEEPS + TX + offset, side_rows, HALO + offset)


def factors(last):
    last = last != 0
    return jnp.where(last, circ_alpha, 1.0), jnp.where(last, 0.0, 1.0), jnp.where(last, circ_alpha, 0.0)


def own_kernel(keep_ref, f_ref):
    row_y = level_rows()

    def own_steps(index, carry):
        for offset in range(4):
            step = index * 4 + offset
            value = keep_ref[pl.ds(pl.multiple_of(K_INN + step * LEV, LEV), LEV), :]
            cell = keep_ref[pl.ds(K_CELL + step, 1), :].astype(jnp.int32)
            placed = place_forcing(value, cell, (0, TX), row_y)
            f_ref[pl.ds(pl.multiple_of(step * STEP, STEP), STEP), :] = placed
        return carry

    lax.fori_loop(0, STEPS_DEV // 4, own_steps, 0)


def next_kernel(code_ref, t_ref, f_ref):
    wrap, _, extra = factors(flags_of(code_ref)[0])
    row_y = level_rows()
    for (_, _, first_inn, inns), base in zip(PARTS, T_BASE):
        for slot in range(inns):
            step = first_inn + slot
            value = t_ref[base + slot * LEV : base + slot * LEV + LEV, :] * wrap
            row = base + inns * LEV + step
            cell = t_ref[row : row + 1, :].astype(jnp.int32)
            placed = place_forcing(value, cell, (0, TX), row_y)
            if step == 0:
                width = PARTS[0][1] * LEV
                states = [t_ref[TAILS[0] + col * width : TAILS[0] + col * width + LEV, :] for col in range(TX)]
                placed = placed - jnp.concatenate(states, axis=0) * extra
            f_ref[step * STEP : step * STEP + STEP, :] = placed


def early_kernel(
    code_ref, f_ref, keep_ref, here_ref, back_ref, swap_ref,
    out_ref, coef_ref, side_ref,
    za_ref, zb_ref, left_ref, right_ref, inn_left_ref, inn_right_ref,
):
    _, odd, first_tile, last_tile = flags_of(code_ref)
    block = SWEEPS * OWN * LEV
    inner = TX * OWN * LEV

    def states(left, right):
        za_ref[0:block, :] = left[0:block, :]
        za_ref[block + inner : 2 * block + inner, :] = right[0:block, :]
        inn_left_ref[...] = left[N_INN:N_RATE, :]
        inn_right_ref[...] = right[N_INN:N_RATE, :]

    def rates(left, right):
        left_ref[...] = left[...]
        right_ref[...] = right[...]

    by_side(odd, states, here_ref, back_ref)
    by_side(odd, rates, here_ref.at[pl.ds(N_RATE, N_ROWS - N_RATE)], swap_ref)
    za_ref[block : block + inner, :] = keep_ref[0:inner, :]
    open_left = jnp.where(first_tile != 0, 0.0, 1.0)
    open_right = jnp.where(last_tile != 0, 0.0, 1.0)
    lane = lax.broadcasted_iota(jnp.int32, (8, NY), 1)
    sub = lax.broadcasted_iota(jnp.int32, (8, NY), 0)
    for at in range(XW):
        mixings = []

        def put(kind, at_row, value):
            coef_ref[kind * PLANE + at_row : kind * PLANE + at_row + 8, :] = value

        for half in range(2):
            fields = []
            for index in range(4):
                if HALO <= at < HALO + TX:
                    fields.append(column(keep_ref, K_RATE + index * STEP, at - HALO, half))
                else:
                    side, place = (left_ref, at) if at < HALO else (right_ref, at - HALO - TX)
                    row = (index * HALO + place) * LEV + 8 * half
                    fields.append(side[row : row + 8, :])
            diff, wind_x, wind_y, mixing = fields
            e_rate, w_rate = toward(diff, wind_x), against(diff, wind_x)
            n_rate, s_rate = toward(diff, wind_y), against(diff, wind_y)
            mixings.append(mixing)
            row = at * LEV + 8 * half
            put(0, row, 1.0 - (e_rate + w_rate + n_rate + s_rate + mixing + mixing))
            if at < XW - 1:
                put(1, row + LEV, e_rate * open_left if at == HALO - 1 else e_rate)
            if at > 0:
                put(2, row - LEV, w_rate * open_right if at == HALO + TX else w_rate)
            put(3, row, jnp.where(lane == 0, 0.0, pltpu.roll(n_rate, 1, 1)))
            put(4, row, jnp.where(lane == NY - 1, 0.0, pltpu.roll(s_rate, NY - 1, 1)))
        row = at * LEV
        down_low, down_high = pltpu.roll(mixings[0], 1, 0), pltpu.roll(mixings[1], 1, 0)
        put(5, row, jnp.where(sub == 0, 0.0, down_low))
        put(5, row + 8, jnp.where(sub == 0, down_low, down_high))
        up_low, up_high = pltpu.roll(mixings[0], 7, 0), pltpu.roll(mixings[1], 7, 0)
        put(6, row, jnp.where(sub == 7, up_high, up_low))
        put(6, row + 8, jnp.where(sub == 7, 0.0, up_high))
    edge = slice(N_EDGE - N_RATE, N_ROWS - N_RATE)
    coef_ref[PLANE : PLANE + LEV, :] = left_ref[edge, :]
    coef_ref[3 * PLANE - LEV : 3 * PLANE, :] = right_ref[edge, :]

    row_y = level_rows()

    def side_step(step):
        for index, (ref, columns) in enumerate(((inn_left_ref, LEFT), (inn_right_ref, RIGHT))):
            value = ref[pl.ds(pl.multiple_of((step - 1) * LEV, LEV), LEV), :]
            cell = ref[pl.ds(7 * LEV + step, 1), :].astype(jnp.int32)
            placed = place_forcing(value, cell, columns, row_y)
            side_ref[pl.ds(pl.multiple_of(step * STEP + index * HALO * LEV, LEV), HALO * LEV), :] = placed

    def side_steps(index, carry):
        for offset in range(2):
            side_step(2 + index * 2 + offset)
        return carry

    side_step(1)
    lax.fori_loop(0, 3, side_steps, 0)

    def rows_of_ref(ref):
        return lambda step, place: (ref, step * STEP + place * LEV)

    def store(chain, at, half, total):
        out_ref[pl.ds(chain * STEP + half * 8 * TX + at - SWEEPS, 8, stride=TX), :] = total

    sweeps(OWN, 0, za_ref, zb_ref, coef_ref, rows_of_ref(f_ref), rows_of_ref(side_ref), store)


def next_chains(part, code_ref, coef_ref, t_ref, here_ref, back_ref, za_ref, zb_ref, tails, sides, forcing, store):
    first_state, states, first_inn, inns = PARTS[part]
    last, odd = flags_of(code_ref)[:2]
    wrap, first, extra = factors(last)
    width = states * LEV
    tail = TAILS[part]

    def scaled(value):
        amounts = [first if first_state + slot == 0 else wrap for slot in range(states)]
        return [value[slot * LEV : slot * LEV + LEV, :] * amount for slot, amount in enumerate(amounts)]

    def fill(at, ref, base):
        for slot, value in enumerate(scaled(ref[base : base + width, :])):
            row = at * width + slot * LEV
            za_ref[row : row + LEV, :] = value

    def edges(left, right):
        for place in range(SWEEPS):
            fill(place, left, place * width)
            fill(SWEEPS + TX + place, right, tail + place * width)
        tails[0][...] = left[SWEEPS * width : SWEEPS * width + tail, :]
        tails[1][...] = right[0:tail, :]

    by_side(odd, edges, here_ref, back_ref)
    for col in range(TX):
        fill(SWEEPS + col, t_ref, T_BASE[part] + tail + col * width)

    row_y = level_rows()
    for slot in range(inns):
        for index, (ref, columns) in enumerate(zip(tails, (LEFT, RIGHT))):
            value = ref[slot * LEV : slot * LEV + LEV, :] * wrap
            row = inns * LEV + first_inn + slot
            cell = ref[row : row + 1, :].astype(jnp.int32)
            placed = place_forcing(value, cell, columns, row_y)
            start = slot * STEP + index * HALO * LEV
            sides[part][start : start + HALO * LEV, :] = placed

    if first_state == 0:

        @pl.when(last != 0)
        def _():
            def leave(left, right):
                for place in range(2 * HALO):
                    inside = place < HALO
                    ref, base = (left, (place + 1) * width) if inside else (right, tail + (place - HALO) * width)
                    rows = slice(place * LEV, place * LEV + LEV)
                    sides[part][rows, :] = sides[part][rows, :] - ref[base : base + LEV, :] * extra

            by_side(odd, leave, here_ref, back_ref)

    def own_rows(step, place):
        ref, base = (forcing[0], step) if step < STEPS_DEV else (forcing[1], step - STEPS_DEV)
        return ref, base * STEP + place * LEV

    def side_rows(step, place):
        if step < STEPS_DEV:
            return forcing[2], step * STEP + place * LEV
        part_of = 0 if step - STEPS_DEV < PARTS[1][2] else 1
        return sides[part_of], (step - STEPS_DEV - PARTS[part_of][2]) * STEP + place * LEV

    sweeps(states, OWN + first_state, za_ref, zb_ref, coef_ref, own_rows, side_rows, store)


def mid_kernel(
    code_ref, coef_ref, f_ref, fnext_ref, side_ref, t_ref, here_ref, back_ref,
    out_ref, side_out_ref,
    za_ref, zb_ref, tail_left_ref, tail_right_ref,
):
    def store(chain, at, half, total):
        out_ref[pl.ds(chain * STEP + half * 8 * TX + at - SWEEPS, 8, stride=TX), :] = total

    next_chains(
        0, code_ref, coef_ref, t_ref, here_ref, back_ref, za_ref, zb_ref, (tail_left_ref, tail_right_ref),
        (side_out_ref, None), (f_ref, fnext_ref, side_ref), store,
    )


def late_kernel(
    code_ref, early_ref, mid_ref, coef_ref, f_ref, fnext_ref, side_ref, side_mid_ref, t_ref, here_ref, back_ref,
    out_ref,
    za_ref, zb_ref, tail_left_ref, tail_right_ref, side_late_ref,
):
    begun = OWN + PARTS[0][1]
    out_ref[0 : OWN * STEP, :] = early_ref[...]
    out_ref[OWN * STEP : begun * STEP, :] = mid_ref[...]

    def store(chain, at, half, total):
        out_ref[pl.ds((begun + chain) * STEP + half * 8 * TX + at - SWEEPS, 8, stride=TX), :] = total

    next_chains(
        1, code_ref, coef_ref, t_ref, here_ref, back_ref, za_ref, zb_ref, (tail_left_ref, tail_right_ref),
        (side_mid_ref, side_late_ref), (f_ref, fnext_ref, side_ref), store,
    )


def vmem(count):
    return [pl.BlockSpec(memory_space=pltpu.VMEM)] * count


def rows_of(count):
    return jax.ShapeDtypeStruct((count, NY), jnp.float32)


def scratch(count):
    return pltpu.VMEM((count, NY), jnp.float32)


SMEM_SPEC = pl.BlockSpec(memory_space=pltpu.SMEM)


def update(adjoint_iterate, innovations, station_cells, diffusivity, wind_x, wind_y, vertical_mixing):
    time_parts = lax.axis_size("tm")
    tiles = lax.axis_size("space")
    lam = adjoint_iterate.reshape(STEPS_DEV * STEP, NY)
    inn = innovations.reshape(STEPS_DEV * LEV, NY)
    fields = [field.reshape(STEP, NY) for field in (diffusivity, wind_x, wind_y, vertical_mixing)]
    time_rank, tile = lax.axis_index("tm"), lax.axis_index("space")
    odd = time_rank & 1
    code = (time_rank == time_parts - 1) + 2 * odd + 4 * (tile == 0) + 8 * (tile == tiles - 1)
    code = code.astype(jnp.int32).reshape(1)

    ahead = [((i + 1) % time_parts, i) for i in range(time_parts)]

    def neighbours(flip):
        pairs = []
        for part in range(time_parts):
            step = 1 if part % 2 == flip else -1
            for place in range(tiles):
                inside = 0 <= place + step < tiles
                target = part * tiles + place + step if inside else (part ^ 1) * tiles + place
                pairs.append((part * tiles + place, target))
        return pairs

    there, again = neighbours(0), neighbours(1)
    both = ("tm", "space")
    partners = [(part, part ^ 1) for part in range(time_parts)]

    def kernel(function, inputs, outputs, scratches, flops):
        return pl.pallas_call(
            function,
            out_shape=tuple(rows_of(rows) for rows in outputs),
            in_specs=inputs,
            out_specs=tuple(vmem(len(outputs))),
            scratch_shapes=scratches,
            compiler_params=pltpu.CompilerParams(vmem_limit_bytes=12 << 20),
            cost_estimate=pl.CostEstimate(flops=flops, bytes_accessed=4_000_000, transcendentals=0),
        )

    arguments = (lam, inn, station_cells, *fields)
    pay_here, pay_back, pay_t, keep = kernel(
        pack_kernel,
        [SMEM_SPEC] + [pl.BlockSpec(memory_space=pltpu.HBM)] * 7,
        (N_ROWS, N_RATE, T_ROWS, K_ROWS),
        [
            scratch(STEPS_DEV * STEP),
            pltpu.VMEM(station_cells.shape, station_cells.dtype),
            pltpu.SemaphoreType.DMA((8,)),
        ],
        1_000_000,
    )(code, *[pltpu.with_memory_space_constraint(value, pltpu.HBM) for value in arguments])

    got_t = lax.ppermute(pay_t, "tm", ahead)
    here_one = lax.ppermute(pay_here, both, there)
    back_one = lax.ppermute(pay_back, both, again)
    parts = []
    for part in range(2):
        rows = part_rows(part)
        span = 2 * TAILS[part] + TX * PARTS[part][1] * LEV - rows
        up = span * (1 - odd)
        here = lax.dynamic_slice_in_dim(got_t, T_BASE[part] + up, rows)
        back = lax.dynamic_slice_in_dim(got_t, T_BASE[part] + span - up, rows)
        parts.append((lax.ppermute(here, both, there), lax.ppermute(back, both, again)))
    swapped = lax.ppermute(here_one[N_RATE:], "tm", partners)

    (forcing,) = kernel(own_kernel, vmem(1), (STEPS_DEV * STEP,), [], 5_000_000)(keep)
    (forcing_next,) = kernel(next_kernel, [SMEM_SPEC] + vmem(1), (FNEXT * STEP,), [], 3_000_000)(code, got_t)

    def states(count):
        return [scratch(ZW * count * LEV)] * 2

    out_early, coef, side = kernel(
        early_kernel,
        [SMEM_SPEC] + vmem(5),
        (OWN * STEP, 7 * PLANE, STEPS_DEV * STEP),
        states(OWN) + [scratch(N_ROWS - N_RATE)] * 2 + [scratch(N_RATE - N_INN)] * 2,
        10_000_000,
    )(code, forcing, keep, here_one, back_one, swapped)
    out_mid, side_mid = kernel(
        mid_kernel,
        [SMEM_SPEC] + vmem(7),
        (PARTS[0][1] * STEP, PARTS[0][3] * STEP),
        states(PARTS[0][1]) + [scratch(TAILS[0])] * 2,
        7_000_000,
    )(code, coef, forcing, forcing_next, side, got_t, *parts[0])
    (out,) = kernel(
        late_kernel,
        [SMEM_SPEC] + vmem(10),
        (STEPS_DEV * STEP,),
        states(PARTS[1][1]) + [scratch(TAILS[1])] * 2 + [scratch(PARTS[1][3] * STEP)],
        10_000_000,
    )(code, out_early, out_mid, coef, forcing, forcing_next, side, side_mid, got_t, *parts[1])
    return out.reshape(STEPS_DEV, LEV, TX, NY)


def solution(mesh):
    in_specs = (
        P("tm", None, "space", None),
        P("tm", None, "space"),
        P("tm", "space"),
        P(None, "space", None),
        P(None, "space", None),
        P(None, "space", None),
        P(None, "space", None),
    )
    out_specs = P("tm", None, "space", None)
    return jax.shard_map(update, mesh=mesh, in_specs=in_specs, out_specs=out_specs, check_vma=False)
```

time: 22.6 us -> 23.3 us (1.031)
  starting transfers between devices: 6.59 us -> 9.6 us
  Pallas kernels: 9.13 us -> 6.99 us
  waiting for transfers between devices: 6.67 us -> 6.37 us
    ppermute x5 -> x8, starting transfers between devices: 6.59 us -> 9.6 us  [the longest x2 4.53 us: update(): lax.ppermute(here, both, there)]
    pallas_call x4 -> x6, Pallas kernels: 9.13 us -> 6.99 us  [the longest x1 2.01 us: update(): kernel(early_kernel, [SMEM_SPEC] + vmem(5), (OWN * STEP, 7 * PLANE, STEPS...]
    ppermute x5 -> x8, waiting for transfers between devices: 6.67 us -> 6.37 us  [the longest x1 4.77 us: update(): here_one = lax.ppermute(pay_here, both, there)]
  transfers between devices with their start and end apart: 5 -> 8, of which waited for: 5 -> 3; matrix products, arithmetic and copies ran while one was open for 0% -> 0% of each run, Pallas kernels for 17% -> 16%
where the time goes in v5:
time: 23.3 us; the launch traced here: 23.1 us
  starting transfers between devices  9.6 us (41%)
  Pallas kernels  6.99 us (30%)
  waiting for transfers between devices  6.37 us (27%)
    ppermute x1, waiting for transfers between devices, update(): here_one = lax.ppermute(pay_here, both, there)  4.77 us
    ppermute x2, starting transfers between devices, update(): lax.ppermute(here, both, there)  4.53 us
    ppermute x1, starting transfers between devices, update(): got_t = lax.ppermute(pay_t, 'tm', ahead)  3.41 us
    pallas_call x1, Pallas kernels, update(): kernel(early_kernel, [SMEM_SPEC] + vmem(5), (OWN * STEP, 7 * PLANE, STEPS...  2.01 us
    pallas_call x1, Pallas kernels, update(): kernel(late_kernel, [SMEM_SPEC] + vmem(10), (STEPS_DEV * STEP,), states(P...  1.82 us
    ppermute x1, starting transfers between devices, update(): here_one = lax.ppermute(pay_here, both, there)  1.58 us
    pallas_call x1, Pallas kernels, update(): kernel(pack_kernel, [SMEM_SPEC] + [pl.BlockSpec(memory_space=pltpu.HBM)]...  1.38 us
    pallas_call x1, Pallas kernels, update(): kernel(mid_kernel, [SMEM_SPEC] + vmem(7), (PARTS[0][1] * STEP, PARTS[0][3...  0.84 us
  transfers between devices with their start and end apart: 8, of which 3 were waited for; matrix products, arithmetic and copies ran while one was open for 0% of the time, Pallas kernels for 16%

profile of v5, /device:TPU:0, one launch (start us, length us, event | category | flops | bytes accessed | tf_op | source)
XLA Modules:
  0.0 23.1 jit_solution(5182637949117746441)
XLA Ops:
  0.0 1.4 %shard_map.73 = (f32[632,128]{1,0:T(8,128)S(1)}, f32[360,128]{1,0:T(8,128)S(1)}, f32[800,128]{1,0:T(8,128)S(1)}, f32[1032,128]{1,0:T(8,128)S(1)}) custom-call(s32[1]{0:T(128)} %bitcast.code_ref, f32[1024,128]{1,0:T(8,128)} %bitcast.8, f32[128,128]{1,0:T(8,128)} %bitcast.9, s32[8,128]{1,0:T(8,128)} %cell_hbm.1, f32[128,128]{1,0:T(8,128)} %bitcast.10, ...), custom_call_target="tpu_custom_call" | custom-call | flops 1000000 | bytes 4000000 | tf_op jit(solution)/shard_map/pallas_call | solution.py:470
  1.4 3.4 %collective-permute-start.3 = (f32[800,128]{1,0:T(8,128)S(1)}, f32[800,128]{1,0:T(8,128)S(1)}, u32[]{:S(2)}, u32[]{:S(2)}) collective-permute-start(f32[800,128]{1,0:T(8,128)S(1)} %get-tuple-element.19), channel_id=1, source_target_pairs={{4,0},{8,4},{12,8},{16,12},{20,16},{24,20},{28,24},{0,28},{5,1},{9... | collective-permute-start | bytes 1228808 | tf_op jit(solution)/shard_map/ppermute | solution.py:482
  4.8 1.6 %collective-permute-start = (f32[632,128]{1,0:T(8,128)S(1)}, f32[632,128]{1,0:T(8,128)S(1)}, u32[]{:S(2)}, u32[]{:S(2)}) collective-permute-start(f32[632,128]{1,0:T(8,128)S(1)} %get-tuple-element.15), channel_id=1, source_target_pairs={{0,1},{1,2},{2,3},{3,7},{4,0},{5,4},{6,5},{7,6},{8,9},{9,10},{10,1... | collective-permute-start | bytes 970760 | tf_op jit(solution)/shard_map/ppermute | solution.py:483
  6.4 0.0 collective-permute-start.1
  6.4 4.8 %collective-permute-done.here_ref = f32[632,128]{1,0:T(8,128)S(1)} collective-permute-done((f32[632,128]{1,0:T(8,128)S(1)}, f32[632,128]{1,0:T(8,128)S(1)}, u32[]{:S(2)}, u32[]{:S(2)}) %collective-permute-start) | collective-permute-done | bytes 323616 | tf_op jit(solution)/shard_map/ppermute | solution.py:483
  11.2 0.1 collective-permute-start.2
  11.2 0.0 collective-permute-done.3.t_ref
  11.3 2.5 %collective-permute-start.6 = (f32[296,128]{1,0:T(8,128)S(1)}, f32[296,128]{1,0:T(8,128)S(1)}, u32[]{:S(2)}, u32[]{:S(2)}) collective-permute-start(f32[296,128]{1,0:T(8,128)S(1)} %get-tuple-element.24), channel_id=1, source_target_pairs={{0,1},{1,2},{2,3},{3,7},{4,0},{5,4},{6,5},{7,6},{8,9},{9,10},{10,1... | collective-permute-start | bytes 454664 | tf_op jit(solution)/shard_map/ppermute | solution.py:492
  13.8 0.0 collective-permute-start.7
  13.8 2.0 %collective-permute-start.4 = (f32[184,128]{1,0:T(8,128)S(1)}, f32[184,128]{1,0:T(8,128)S(1)}, u32[]{:S(2)}, u32[]{:S(2)}) collective-permute-start(f32[184,128]{1,0:T(8,128)S(1)} %get-tuple-element.26), channel_id=1, source_target_pairs={{0,1},{1,2},{2,3},{3,7},{4,0},{5,4},{6,5},{7,6},{8,9},{9,10},{10,1... | collective-permute-start | bytes 282632 | tf_op jit(solution)/shard_map/ppermute | solution.py:492
  15.9 0.0 collective-permute-done.1.back_ref
  15.9 0.0 collective-permute-start.5
  15.9 0.6 %shard_map.74.f_ref = f32[1024,128]{1,0:T(8,128)S(1)} custom-call(f32[1032,128]{1,0:T(8,128)S(1)} %get-tuple-element.14.keep_ref), custom_call_target="tpu_custom_call" | custom-call | flops 5000000 | bytes 4000000 | tf_op jit(solution)/shard_map/pallas_call | solution.py:495
  16.5 0.3 %shard_map.76.fnext_ref = f32[512,128]{1,0:T(8,128)S(1)} custom-call(s32[1]{0:T(128)} %bitcast.code_ref, f32[800,128]{1,0:T(8,128)S(1)} %collective-permute-done.3.t_ref), custom_call_target="tpu_custom_call" | custom-call | flops 3000000 | bytes 4000000 | tf_op jit(solution)/shard_map/pallas_call | solution.py:496
  16.8 0.0 collective-permute-done.2.swap_ref
  16.8 2.0 %shard_map.75 = (f32[384,128]{1,0:T(8,128)S(1)}, f32[1792,128]{1,0:T(8,128)S(1)}, f32[1024,128]{1,0:T(8,128)S(1)}) custom-call(s32[1]{0:T(128)} %bitcast.code_ref, f32[1024,128]{1,0:T(8,128)S(1)} %shard_map.74.f_ref, f32[1032,128]{1,0:T(8,128)S(1)} %get-tuple-element.14.keep_ref, f32[632,128]{1,0:T(8,128)S(1)} %collective-permute-done.here_ref, ...), custom_call_target="tpu_custom_call" | custom-call | flops 10000000 | bytes 4000000 | tf_op jit(solution)/shard_map/pallas_call | solution.py:501
  18.8 0.8 %collective-permute-done.4.here_ref = f32[184,128]{1,0:T(8,128)S(1)} collective-permute-done((f32[184,128]{1,0:T(8,128)S(1)}, f32[184,128]{1,0:T(8,128)S(1)}, u32[]{:S(2)}, u32[]{:S(2)}) %collective-permute-start.4) | collective-permute-done | bytes 94240 | tf_op jit(solution)/shard_map/ppermute | solution.py:492
  19.7 0.8 %collective-permute-done.5.back_ref = f32[184,128]{1,0:T(8,128)S(1)} collective-permute-done((f32[184,128]{1,0:T(8,128)S(1)}, f32[184,128]{1,0:T(8,128)S(1)}, u32[]{:S(2)}, u32[]{:S(2)}) %collective-permute-start.5) | collective-permute-done | bytes 94240 | tf_op jit(solution)/shard_map/ppermute | solution.py:492
  20.4 0.8 %shard_map.77 = (f32[256,128]{1,0:T(8,128)S(1)}, f32[128,128]{1,0:T(8,128)S(1)}) custom-call(s32[1]{0:T(128)} %bitcast.code_ref, f32[1792,128]{1,0:T(8,128)S(1)} %get-tuple-element.18.coef_ref, f32[1024,128]{1,0:T(8,128)S(1)} %shard_map.74.f_ref, f32[512,128]{1,0:T(8,128)S(1)} %shard_map.76.fnext_ref, f32[1024,128]{1,0:T(8,128)S(1)} %get-tuple-element.20.side_ref, ...), custom_call_target="tpu_custom_call" | custom-call | flops 7000000 | bytes 4000000 | tf_op jit(solution)/shard_map/pallas_call | solution.py:508
  21.3 0.0 collective-permute-done.6.here_ref
  21.3 0.0 collective-permute-done.7.back_ref
  21.3 1.8 %shard_map.78 = f32[1024,128]{1,0:T(8,128)} custom-call(s32[1]{0:T(128)} %bitcast.code_ref, f32[384,128]{1,0:T(8,128)S(1)} %get-tuple-element.17.early_ref, f32[256,128]{1,0:T(8,128)S(1)} %get-tuple-element.21.mid_ref, f32[1792,128]{1,0:T(8,128)S(1)} %get-tuple-element.18.coef_ref, f32[1024,128]{1,0:T(8,128)S(1)} %shard_map.74.f_ref, ...), custom_call_target="tpu_custom_call" | custom-call | flops 10000000 | bytes 4000000 | tf_op jit(solution)/shard_map/pallas_call | solution.py:515
  (3 shorter events, 0.1 us)
Async XLA Ops:
  1.4 9.9 %collective-permute-start.3 = (f32[800,128]{1,0:T(8,128)S(1)}, f32[800,128]{1,0:T(8,128)S(1)}, u32[]{:S(2)}, u32[]{:S(2)}) collective-permute-start(f32[800,128]{1,0:T(8,128)S(1)} %get-tuple-element.19), channel_id=1, source_target_pairs={{4,0},{8,4},{12,8},{16,12},{20,16},{24,20},{28,24},{0,28},{5,1},{9... | collective-permute-start | bytes 1228808 | tf_op jit(solution)/shard_map/ppermute | solution.py:482
  4.8 6.3 %collective-permute-start = (f32[632,128]{1,0:T(8,128)S(1)}, f32[632,128]{1,0:T(8,128)S(1)}, u32[]{:S(2)}, u32[]{:S(2)}) collective-permute-start(f32[632,128]{1,0:T(8,128)S(1)} %get-tuple-element.15), channel_id=1, source_target_pairs={{0,1},{1,2},{2,3},{3,7},{4,0},{5,4},{6,5},{7,6},{8,9},{9,10},{10,1... | collective-permute-start | bytes 970760 | tf_op jit(solution)/shard_map/ppermute | solution.py:483
  6.4 9.5 %collective-permute-start.1 = (f32[360,128]{1,0:T(8,128)S(1)}, f32[360,128]{1,0:T(8,128)S(1)}, u32[]{:S(2)}, u32[]{:S(2)}) collective-permute-start(f32[360,128]{1,0:T(8,128)S(1)} %get-tuple-element.16), channel_id=1, source_target_pairs={{0,4},{1,0},{2,1},{3,2},{4,5},{5,6},{6,7},{7,3},{8,12},{9,8},{10,9... | collective-permute-start | bytes 552968 | tf_op jit(solution)/shard_map/ppermute | solution.py:484
  11.2 5.7 %collective-permute-start.2 = (f32[272,128]{1,0:T(8,128)S(1)}, f32[272,128]{1,0:T(8,128)S(1)}, u32[]{:S(2)}, u32[]{:S(2)}) collective-permute-start(f32[272,128]{1,0:T(8,128)S(1)} %slice.4), channel_id=1, source_target_pairs={{0,4},{4,0},{8,12},{12,8},{16,20},{20,16},{24,28},{28,24},{1,5},{5... | collective-permute-start | bytes 417800 | tf_op jit(solution)/shard_map/ppermute | solution.py:493
  11.3 10.0 %collective-permute-start.6 = (f32[296,128]{1,0:T(8,128)S(1)}, f32[296,128]{1,0:T(8,128)S(1)}, u32[]{:S(2)}, u32[]{:S(2)}) collective-permute-start(f32[296,128]{1,0:T(8,128)S(1)} %get-tuple-element.24), channel_id=1, source_target_pairs={{0,1},{1,2},{2,3},{3,7},{4,0},{5,4},{6,5},{7,6},{8,9},{9,10},{10,1... | collective-permute-start | bytes 454664 | tf_op jit(solution)/shard_map/ppermute | solution.py:492
  13.8 7.5 %collective-permute-start.7 = (f32[296,128]{1,0:T(8,128)S(1)}, f32[296,128]{1,0:T(8,128)S(1)}, u32[]{:S(2)}, u32[]{:S(2)}) collective-permute-start(f32[296,128]{1,0:T(8,128)S(1)} %get-tuple-element.23), channel_id=1, source_target_pairs={{0,4},{1,0},{2,1},{3,2},{4,5},{5,6},{6,7},{7,3},{8,12},{9,8},{10,9... | collective-permute-start | bytes 454664 | tf_op jit(solution)/shard_map/ppermute | solution.py:492
  13.8 5.9 %collective-permute-start.4 = (f32[184,128]{1,0:T(8,128)S(1)}, f32[184,128]{1,0:T(8,128)S(1)}, u32[]{:S(2)}, u32[]{:S(2)}) collective-permute-start(f32[184,128]{1,0:T(8,128)S(1)} %get-tuple-element.26), channel_id=1, source_target_pairs={{0,1},{1,2},{2,3},{3,7},{4,0},{5,4},{6,5},{7,6},{8,9},{9,10},{10,1... | collective-permute-start | bytes 282632 | tf_op jit(solution)/shard_map/ppermute | solution.py:492
  15.9 4.6 %collective-permute-start.5 = (f32[184,128]{1,0:T(8,128)S(1)}, f32[184,128]{1,0:T(8,128)S(1)}, u32[]{:S(2)}, u32[]{:S(2)}) collective-permute-start(f32[184,128]{1,0:T(8,128)S(1)} %get-tuple-element.25), channel_id=1, source_target_pairs={{0,4},{1,0},{2,1},{3,2},{4,5},{5,6},{6,7},{7,3},{8,12},{9,8},{10,9... | collective-permute-start | bytes 282632 | tf_op jit(solution)/shard_map/ppermute | solution.py:492

commit v6 on v5

--- a/solution.py
+++ b/solution.py
@@ -24,8 +24,7 @@
 
 PARTS = ((0, 2, 0, 1), (2, 3, 1, 3))
 TAILS = tuple(part[3] * LEV + 8 for part in PARTS)
-T_BASE = (0, 2 * TAILS[0] + TX * PARTS[0][1] * LEV)
-T_ROWS = T_BASE[1] + 2 * TAILS[1] + TX * PARTS[1][1] * LEV
+T_ROWS = tuple(2 * tail + TX * part[1] * LEV for part, tail in zip(PARTS, TAILS))
 N_INN = SWEEPS * OWN * LEV
 N_CELL = N_INN + 7 * LEV
 N_RATE = N_CELL + 8
@@ -59,7 +58,7 @@
 
 def pack_kernel(
     code_ref, lam_hbm, inn_hbm, cell_hbm, diff_hbm, wx_hbm, wy_hbm, vm_hbm,
-    here_ref, back_ref, t_ref, keep_ref,
+    here_ref, back_ref, ta_ref, tb_ref, keep_ref,
     lam_ref, cell_ref, sems,
 ):
     late, soon = pl.ds(NEXT * STEP, OWN * STEP), pl.ds(0, NEXT * STEP)
@@ -105,17 +104,18 @@
     for ref in (here_ref, back_ref):
         ref[N_INN:N_CELL, :] = keep_ref[K_INN + LEV : K_INN + 8 * LEV, :]
         ref[N_CELL:N_RATE, :] = cells
-    for (_, states, first_inn, inns), tail, base in zip(PARTS, TAILS, T_BASE):
-        for start in (base, base + tail + TX * states * LEV):
+    payloads = (ta_ref, tb_ref)
+    for (_, states, first_inn, inns), tail, t_ref in zip(PARTS, TAILS, payloads):
+        for start in (0, tail + TX * states * LEV):
             row = K_INN + first_inn * LEV
             t_ref[start : start + inns * LEV, :] = keep_ref[row : row + inns * LEV, :]
             t_ref[start + inns * LEV : start + tail, :] = cells
     copies[7].wait()
-    for (first_state, states, _, _), tail, base in zip(PARTS, TAILS, T_BASE):
+    for (first_state, states, _, _), tail, t_ref in zip(PARTS, TAILS, payloads):
         for half in range(2):
             for col in range(TX):
                 for slot in range(states):
-                    row = base + tail + (col * states + slot) * LEV + 8 * half
+                    row = tail + (col * states + slot) * LEV + 8 * half
                     t_ref[row : row + 8, :] = column(lam_ref, (first_state + slot) * STEP, col, half)
 
 
@@ -211,14 +211,14 @@
     lax.fori_loop(0, STEPS_DEV // 4, own_steps, 0)
 
 
-def next_kernel(code_ref, t_ref, f_ref):
+def next_kernel(code_ref, ta_ref, tb_ref, f_ref):
     wrap, _, extra = factors(flags_of(code_ref)[0])
     row_y = level_rows()
-    for (_, _, first_inn, inns), base in zip(PARTS, T_BASE):
+    for (_, _, first_inn, inns), t_ref in zip(PARTS, (ta_ref, tb_ref)):
         for slot in range(inns):
             step = first_inn + slot
-            value = t_ref[base + slot * LEV : base + slot * LEV + LEV, :] * wrap
-            row = base + inns * LEV + step
+            value = t_ref[slot * LEV : slot * LEV + LEV, :] * wrap
+            row = inns * LEV + step
             cell = t_ref[row : row + 1, :].astype(jnp.int32)
             placed = place_forcing(value, cell, (0, TX), row_y)
             if step == 0:
@@ -343,7 +343,7 @@
 
     by_side(odd, edges, here_ref, back_ref)
     for col in range(TX):
-        fill(SWEEPS + col, t_ref, T_BASE[part] + tail + col * width)
+        fill(SWEEPS + col, t_ref, tail + col * width)
 
     row_y = level_rows()
     for slot in range(inns):
@@ -467,10 +467,10 @@
         )
 
     arguments = (lam, inn, station_cells, *fields)
-    pay_here, pay_back, pay_t, keep = kernel(
+    pay_here, pay_back, pay_ta, pay_tb, keep = kernel(
         pack_kernel,
         [SMEM_SPEC] + [pl.BlockSpec(memory_space=pltpu.HBM)] * 7,
-        (N_ROWS, N_RATE, T_ROWS, K_ROWS),
+        (N_ROWS, N_RATE, *T_ROWS, K_ROWS),
         [
             scratch(STEPS_DEV * STEP),
             pltpu.VMEM(station_cells.shape, station_cells.dtype),
@@ -479,21 +479,22 @@
         1_000_000,
     )(code, *[pltpu.with_memory_space_constraint(value, pltpu.HBM) for value in arguments])
 
-    got_t = lax.ppermute(pay_t, "tm", ahead)
+    got_ta = lax.ppermute(pay_ta, "tm", ahead)
     here_one = lax.ppermute(pay_here, both, there)
     back_one = lax.ppermute(pay_back, both, again)
+    got_tb = lax.ppermute(pay_tb, "tm", ahead)
     parts = []
-    for part in range(2):
+    for part, got_t in enumerate((got_ta, got_tb)):
         rows = part_rows(part)
-        span = 2 * TAILS[part] + TX * PARTS[part][1] * LEV - rows
+        span = T_ROWS[part] - rows
         up = span * (1 - odd)
-        here = lax.dynamic_slice_in_dim(got_t, T_BASE[part] + up, rows)
-        back = lax.dynamic_slice_in_dim(got_t, T_BASE[part] + span - up, rows)
+        here = lax.dynamic_slice_in_dim(got_t, up, rows)
+        back = lax.dynamic_slice_in_dim(got_t, span - up, rows)
         parts.append((lax.ppermute(here, both, there), lax.ppermute(back, both, again)))
     swapped = lax.ppermute(here_one[N_RATE:], "tm", partners)
 
     (forcing,) = kernel(own_kernel, vmem(1), (STEPS_DEV * STEP,), [], 5_000_000)(keep)
-    (forcing_next,) = kernel(next_kernel, [SMEM_SPEC] + vmem(1), (FNEXT * STEP,), [], 3_000_000)(code, got_t)
+    (forcing_next,) = kernel(next_kernel, [SMEM_SPEC] + vmem(2), (FNEXT * STEP,), [], 3_000_000)(code, got_ta, got_tb)
 
     def states(count):
         return [scratch(ZW * count * LEV)] * 2
@@ -511,14 +512,14 @@
         (PARTS[0][1] * STEP, PARTS[0][3] * STEP),
         states(PARTS[0][1]) + [scratch(TAILS[0])] * 2,
         7_000_000,
-    )(code, coef, forcing, forcing_next, side, got_t, *parts[0])
+    )(code, coef, forcing, forcing_next, side, got_ta, *parts[0])
     (out,) = kernel(
         late_kernel,
         [SMEM_SPEC] + vmem(10),
         (STEPS_DEV * STEP,),
         states(PARTS[1][1]) + [scratch(TAILS[1])] * 2 + [scratch(PARTS[1][3] * STEP)],
         10_000_000,
-    )(code, out_early, out_mid, coef, forcing, forcing_next, side, side_mid, got_t, *parts[1])
+    )(code, out_early, out_mid, coef, forcing, forcing_next, side, side_mid, got_tb, *parts[1])
     return out.reshape(STEPS_DEV, LEV, TX, NY)
 
 

time: 23.3 us -> 23.3 us (level)
    ppermute x1, waiting for transfers between devices: 4.77 us -> 3.04 us  [update(): here_one = lax.ppermute(pay_here, both, there)]
    ppermute x1 -> x2, waiting for transfers between devices: 0.01 us -> 1.72 us  [the longest x1 1.72 us: update(): got_tb = lax.ppermute(pay_tb, 'tm', ahead)]
    ppermute x2, waiting for transfers between devices: 0.83 us -> 0.01 us  [update(): lax.ppermute(here, both, there)]
    ppermute x2, waiting for transfers between devices: 0.76 us -> 1.56 us  [update(): lax.ppermute(back, both, again)]
    ppermute x1, starting transfers between devices: 0.01 us -> 0.51 us  [update(): back_one = lax.ppermute(pay_back, both, again)]
    ppermute x2, starting transfers between devices: 4.53 us -> 4.08 us  [update(): lax.ppermute(here, both, there)]
    ppermute x1 -> x2, starting transfers between devices: 3.41 us -> 3.42 us  [the longest x1 3.41 us: update(): got_tb = lax.ppermute(pay_tb, 'tm', ahead)]
  transfers between devices with their start and end apart: 8 -> 9, of which waited for: 3 -> 3; matrix products, arithmetic and copies ran while one was open for 0% -> 0% of each run, Pallas kernels for 16% -> 16%
where the time goes in v6:
time: 23.3 us; the launch traced here: 23.2 us
  starting transfers between devices  9.66 us (41%)
  Pallas kernels  7.02 us (30%)
  waiting for transfers between devices  6.33 us (27%)
    ppermute x2, starting transfers between devices, update(): lax.ppermute(here, both, there)  4.08 us
    ppermute x1, starting transfers between devices, update(): got_tb = lax.ppermute(pay_tb, 'tm', ahead)  3.41 us
    ppermute x1, waiting for transfers between devices, update(): here_one = lax.ppermute(pay_here, both, there)  3.04 us
    pallas_call x1, Pallas kernels, update(): kernel(early_kernel, [SMEM_SPEC] + vmem(5), (OWN * STEP, 7 * PLANE, STEPS...  2.03 us
    pallas_call x1, Pallas kernels, update(): kernel(late_kernel, [SMEM_SPEC] + vmem(10), (STEPS_DEV * STEP,), states(P...  1.82 us
    ppermute x1, waiting for transfers between devices, update(): got_tb = lax.ppermute(pay_tb, 'tm', ahead)  1.72 us
    ppermute x1, starting transfers between devices, update(): here_one = lax.ppermute(pay_here, both, there)  1.58 us
    ppermute x2, waiting for transfers between devices, update(): lax.ppermute(back, both, again)  1.56 us
  transfers between devices with their start and end apart: 9, of which 3 were waited for; matrix products, arithmetic and copies ran while one was open for 0% of the time, Pallas kernels for 16%

profile of v6, /device:TPU:0, one launch (start us, length us, event | category | flops | bytes accessed | tf_op | source)
XLA Modules:
  0.0 23.2 jit_solution(4728503988985900707)
XLA Ops:
  0.0 1.4 %shard_map.73 = (f32[632,128]{1,0:T(8,128)S(1)}, f32[360,128]{1,0:T(8,128)S(1)}, f32[304,128]{1,0:T(8,128)S(1)}, f32[496,128]{1,0:T(8,128)S(1)}, f32[1032,128]{1,0:T(8,128)S(1)}) custom-call(s32[1]{0:T(128)} %bitcast.code_ref, f32[1024,128]{1,0:T(8,128)} %bitcast.8, f32[128,128]{1,0:T(8,128)} %bitcast.9, s32[8,128]{1,0:T(8,128)} %cell_hbm.1, ...), custom_call_target="tpu_custom_call" | custom-call | flops 1000000 | bytes 4000000 | tf_op jit(solution)/shard_map/pallas_call | solution.py:470
  1.4 3.4 %collective-permute-start.4 = (f32[496,128]{1,0:T(8,128)S(1)}, f32[496,128]{1,0:T(8,128)S(1)}, u32[]{:S(2)}, u32[]{:S(2)}) collective-permute-start(f32[496,128]{1,0:T(8,128)S(1)} %get-tuple-element.21), channel_id=1, source_target_pairs={{4,0},{8,4},{12,8},{16,12},{20,16},{24,20},{28,24},{0,28},{5,1},{9... | collective-permute-start | bytes 761864 | tf_op jit(solution)/shard_map/ppermute | solution.py:485
  4.8 1.6 %collective-permute-start = (f32[632,128]{1,0:T(8,128)S(1)}, f32[632,128]{1,0:T(8,128)S(1)}, u32[]{:S(2)}, u32[]{:S(2)}) collective-permute-start(f32[632,128]{1,0:T(8,128)S(1)} %get-tuple-element.16), channel_id=1, source_target_pairs={{0,1},{1,2},{2,3},{3,7},{4,0},{5,4},{6,5},{7,6},{8,9},{9,10},{10,1... | collective-permute-start | bytes 970760 | tf_op jit(solution)/shard_map/ppermute | solution.py:483
  6.4 0.0 collective-permute-start.3
  6.4 0.5 %collective-permute-start.1 = (f32[360,128]{1,0:T(8,128)S(1)}, f32[360,128]{1,0:T(8,128)S(1)}, u32[]{:S(2)}, u32[]{:S(2)}) collective-permute-start(f32[360,128]{1,0:T(8,128)S(1)} %get-tuple-element.17), channel_id=1, source_target_pairs={{0,4},{1,0},{2,1},{3,2},{4,5},{5,6},{6,7},{7,3},{8,12},{9,8},{10,9... | collective-permute-start | bytes 552968 | tf_op jit(solution)/shard_map/ppermute | solution.py:484
  6.9 1.7 %collective-permute-done.4.tb_ref.t_ref = f32[496,128]{1,0:T(8,128)S(1)} collective-permute-done((f32[496,128]{1,0:T(8,128)S(1)}, f32[496,128]{1,0:T(8,128)S(1)}, u32[]{:S(2)}, u32[]{:S(2)}) %collective-permute-start.4) | collective-permute-done | bytes 253984 | tf_op jit(solution)/shard_map/ppermute | solution.py:485
  8.6 1.6 %collective-permute-start.7 = (f32[296,128]{1,0:T(8,128)S(1)}, f32[296,128]{1,0:T(8,128)S(1)}, u32[]{:S(2)}, u32[]{:S(2)}) collective-permute-start(f32[296,128]{1,0:T(8,128)S(1)} %get-tuple-element.26), channel_id=1, source_target_pairs={{0,1},{1,2},{2,3},{3,7},{4,0},{5,4},{6,5},{7,6},{8,9},{9,10},{10,1... | collective-permute-start | bytes 454664 | tf_op jit(solution)/shard_map/ppermute | solution.py:493
  10.2 0.0 collective-permute-start.8
  10.2 3.0 %collective-permute-done.here_ref = f32[632,128]{1,0:T(8,128)S(1)} collective-permute-done((f32[632,128]{1,0:T(8,128)S(1)}, f32[632,128]{1,0:T(8,128)S(1)}, u32[]{:S(2)}, u32[]{:S(2)}) %collective-permute-start) | collective-permute-done | bytes 323616 | tf_op jit(solution)/shard_map/ppermute | solution.py:483
  13.3 0.1 collective-permute-start.2
  13.4 0.0 collective-permute-done.3.ta_ref.t_ref
  13.4 2.5 %collective-permute-start.5 = (f32[184,128]{1,0:T(8,128)S(1)}, f32[184,128]{1,0:T(8,128)S(1)}, u32[]{:S(2)}, u32[]{:S(2)}) collective-permute-start(f32[184,128]{1,0:T(8,128)S(1)} %get-tuple-element.28), channel_id=1, source_target_pairs={{0,1},{1,2},{2,3},{3,7},{4,0},{5,4},{6,5},{7,6},{8,9},{9,10},{10,1... | collective-permute-start | bytes 282632 | tf_op jit(solution)/shard_map/ppermute | solution.py:493
  15.9 0.0 collective-permute-done.1.back_ref
  15.9 0.0 collective-permute-start.6
  15.9 0.6 %shard_map.74.f_ref = f32[1024,128]{1,0:T(8,128)S(1)} custom-call(f32[1032,128]{1,0:T(8,128)S(1)} %get-tuple-element.15.keep_ref), custom_call_target="tpu_custom_call" | custom-call | flops 5000000 | bytes 4000000 | tf_op jit(solution)/shard_map/pallas_call | solution.py:496
  16.5 0.3 %shard_map.76.fnext_ref = f32[512,128]{1,0:T(8,128)S(1)} custom-call(s32[1]{0:T(128)} %bitcast.code_ref, f32[304,128]{1,0:T(8,128)S(1)} %collective-permute-done.3.ta_ref.t_ref, f32[496,128]{1,0:T(8,128)S(1)} %collective-permute-done.4.tb_ref.t_ref), custom_call_target="tpu_custom_call" | custom-call | flops 3000000 | bytes 4000000 | tf_op jit(solution)/shard_map/pallas_call | solution.py:497
  16.9 0.0 collective-permute-done.2.swap_ref
  16.9 2.0 %shard_map.75 = (f32[384,128]{1,0:T(8,128)S(1)}, f32[1792,128]{1,0:T(8,128)S(1)}, f32[1024,128]{1,0:T(8,128)S(1)}) custom-call(s32[1]{0:T(128)} %bitcast.code_ref, f32[1024,128]{1,0:T(8,128)S(1)} %shard_map.74.f_ref, f32[1032,128]{1,0:T(8,128)S(1)} %get-tuple-element.15.keep_ref, f32[632,128]{1,0:T(8,128)S(1)} %collective-permute-done.here_ref, ...), custom_call_target="tpu_custom_call" | custom-call | flops 10000000 | bytes 4000000 | tf_op jit(solution)/shard_map/pallas_call | solution.py:502
  18.9 0.0 collective-permute-done.5.here_ref
  18.9 1.6 %collective-permute-done.6.back_ref = f32[184,128]{1,0:T(8,128)S(1)} collective-permute-done((f32[184,128]{1,0:T(8,128)S(1)}, f32[184,128]{1,0:T(8,128)S(1)}, u32[]{:S(2)}, u32[]{:S(2)}) %collective-permute-start.6) | collective-permute-done | bytes 94240 | tf_op jit(solution)/shard_map/ppermute | solution.py:493
  20.5 0.8 %shard_map.77 = (f32[256,128]{1,0:T(8,128)S(1)}, f32[128,128]{1,0:T(8,128)S(1)}) custom-call(s32[1]{0:T(128)} %bitcast.code_ref, f32[1792,128]{1,0:T(8,128)S(1)} %get-tuple-element.19.coef_ref, f32[1024,128]{1,0:T(8,128)S(1)} %shard_map.74.f_ref, f32[512,128]{1,0:T(8,128)S(1)} %shard_map.76.fnext_ref, f32[1024,128]{1,0:T(8,128)S(1)} %get-tuple-element.22.side_ref, ...), custom_call_target="tpu_custom_call" | custom-call | flops 7000000 | bytes 4000000 | tf_op jit(solution)/shard_map/pallas_call | solution.py:509
  21.3 0.0 collective-permute-done.7.here_ref
  21.3 0.0 collective-permute-done.8.back_ref
  21.4 1.8 %shard_map.78 = f32[1024,128]{1,0:T(8,128)} custom-call(s32[1]{0:T(128)} %bitcast.code_ref, f32[384,128]{1,0:T(8,128)S(1)} %get-tuple-element.18.early_ref, f32[256,128]{1,0:T(8,128)S(1)} %get-tuple-element.23.mid_ref, f32[1792,128]{1,0:T(8,128)S(1)} %get-tuple-element.19.coef_ref, f32[1024,128]{1,0:T(8,128)S(1)} %shard_map.74.f_ref, ...), custom_call_target="tpu_custom_call" | custom-call | flops 10000000 | bytes 4000000 | tf_op jit(solution)/shard_map/pallas_call | solution.py:516
  (3 shorter events, 0.1 us)
Async XLA Ops:
  1.4 7.2 %collective-permute-start.4 = (f32[496,128]{1,0:T(8,128)S(1)}, f32[496,128]{1,0:T(8,128)S(1)}, u32[]{:S(2)}, u32[]{:S(2)}) collective-permute-start(f32[496,128]{1,0:T(8,128)S(1)} %get-tuple-element.21), channel_id=1, source_target_pairs={{4,0},{8,4},{12,8},{16,12},{20,16},{24,20},{28,24},{0,28},{5,1},{9... | collective-permute-start | bytes 761864 | tf_op jit(solution)/shard_map/ppermute | solution.py:485
  4.8 8.5 %collective-permute-start = (f32[632,128]{1,0:T(8,128)S(1)}, f32[632,128]{1,0:T(8,128)S(1)}, u32[]{:S(2)}, u32[]{:S(2)}) collective-permute-start(f32[632,128]{1,0:T(8,128)S(1)} %get-tuple-element.16), channel_id=1, source_target_pairs={{0,1},{1,2},{2,3},{3,7},{4,0},{5,4},{6,5},{7,6},{8,9},{9,10},{10,1... | collective-permute-start | bytes 970760 | tf_op jit(solution)/shard_map/ppermute | solution.py:483
  6.4 7.0 %collective-permute-start.3 = (f32[304,128]{1,0:T(8,128)S(1)}, f32[304,128]{1,0:T(8,128)S(1)}, u32[]{:S(2)}, u32[]{:S(2)}) collective-permute-start(f32[304,128]{1,0:T(8,128)S(1)} %get-tuple-element.20), channel_id=1, source_target_pairs={{4,0},{8,4},{12,8},{16,12},{20,16},{24,20},{28,24},{0,28},{5,1},{9... | collective-permute-start | bytes 466952 | tf_op jit(solution)/shard_map/ppermute | solution.py:482
  6.4 9.5 %collective-permute-start.1 = (f32[360,128]{1,0:T(8,128)S(1)}, f32[360,128]{1,0:T(8,128)S(1)}, u32[]{:S(2)}, u32[]{:S(2)}) collective-permute-start(f32[360,128]{1,0:T(8,128)S(1)} %get-tuple-element.17), channel_id=1, source_target_pairs={{0,4},{1,0},{2,1},{3,2},{4,5},{5,6},{6,7},{7,3},{8,12},{9,8},{10,9... | collective-permute-start | bytes 552968 | tf_op jit(solution)/shard_map/ppermute | solution.py:484
  8.6 12.7 %collective-permute-start.7 = (f32[296,128]{1,0:T(8,128)S(1)}, f32[296,128]{1,0:T(8,128)S(1)}, u32[]{:S(2)}, u32[]{:S(2)}) collective-permute-start(f32[296,128]{1,0:T(8,128)S(1)} %get-tuple-element.26), channel_id=1, source_target_pairs={{0,1},{1,2},{2,3},{3,7},{4,0},{5,4},{6,5},{7,6},{8,9},{9,10},{10,1... | collective-permute-start | bytes 454664 | tf_op jit(solution)/shard_map/ppermute | solution.py:493
  10.2 11.1 %collective-permute-start.8 = (f32[296,128]{1,0:T(8,128)S(1)}, f32[296,128]{1,0:T(8,128)S(1)}, u32[]{:S(2)}, u32[]{:S(2)}) collective-permute-start(f32[296,128]{1,0:T(8,128)S(1)} %get-tuple-element.25), channel_id=1, source_target_pairs={{0,4},{1,0},{2,1},{3,2},{4,5},{5,6},{6,7},{7,3},{8,12},{9,8},{10,9... | collective-permute-start | bytes 454664 | tf_op jit(solution)/shard_map/ppermute | solution.py:493
  13.3 3.6 %collective-permute-start.2 = (f32[272,128]{1,0:T(8,128)S(1)}, f32[272,128]{1,0:T(8,128)S(1)}, u32[]{:S(2)}, u32[]{:S(2)}) collective-permute-start(f32[272,128]{1,0:T(8,128)S(1)} %slice.4), channel_id=1, source_target_pairs={{0,4},{4,0},{8,12},{12,8},{16,20},{20,16},{24,28},{28,24},{1,5},{5... | collective-permute-start | bytes 417800 | tf_op jit(solution)/shard_map/ppermute | solution.py:494
  13.4 5.5 %collective-permute-start.5 = (f32[184,128]{1,0:T(8,128)S(1)}, f32[184,128]{1,0:T(8,128)S(1)}, u32[]{:S(2)}, u32[]{:S(2)}) collective-permute-start(f32[184,128]{1,0:T(8,128)S(1)} %get-tuple-element.28), channel_id=1, source_target_pairs={{0,1},{1,2},{2,3},{3,7},{4,0},{5,4},{6,5},{7,6},{8,9},{9,10},{10,1... | collective-permute-start | bytes 282632 | tf_op jit(solution)/shard_map/ppermute | solution.py:493
  15.9 4.6 %collective-permute-start.6 = (f32[184,128]{1,0:T(8,128)S(1)}, f32[184,128]{1,0:T(8,128)S(1)}, u32[]{:S(2)}, u32[]{:S(2)}) collective-permute-start(f32[184,128]{1,0:T(8,128)S(1)} %get-tuple-element.27), channel_id=1, source_target_pairs={{0,4},{1,0},{2,1},{3,2},{4,5},{5,6},{6,7},{7,3},{8,12},{9,8},{10,9... | collective-permute-start | bytes 282632 | tf_op jit(solution)/shard_map/ppermute | solution.py:493
